TPU v7x, 512 devices: a whole 4x4x16 slice. The times are simulated.
512 devices in a mesh: expert: 64 (over x, z), dp: 4 (over y), pair: 2 (over core).
Axes of the slice: x: 4, y: 4, z: 16, core: 2. Of those that a mesh axis runs over, the one named last changes fastest.
Arguments:
- byte_states: bfloat16 [65536, 2048], P(('expert', 'dp')), may hold values from -6 to 6
- positions: int32 [32768], P(('expert', 'dp')), may hold values from 0 to 65535, as said below
- picks: int32 [32768, 2], P(('expert', 'dp')), may hold values from 0 to 63, all different within a row; in each aligned block of 128 rows (0 to 127, 128 to 255, ...) at most 5 rows name the same one
- cotangent: bfloat16 [32768, 2048], P(('expert', 'dp')), may hold values from -6 to 6
- router_weight: bfloat16 [2048, 64], replicated, may hold values from -0.125 to 0.125
- gate_weight: bfloat16 [64, 2048, 768], P('expert', 'dp', 'pair'), may hold values from -0.125 to 0.125
- up_weight: bfloat16 [64, 2048, 768], P('expert', 'dp', 'pair'), may hold values from -0.125 to 0.125
- down_weight: bfloat16 [64, 2048, 768], P('expert', 'dp', 'pair'), may hold values from -0.21875 to 0.21875
Outputs:
- row_grad: bfloat16 [32768, 2048], P(('expert', 'dp'))
- gate_grad: bfloat16 [64, 2048, 768], P('expert', 'dp', 'pair')
- up_grad: bfloat16 [64, 2048, 768], P('expert', 'dp', 'pair')
Inputs may be any that keep to these rules, and one draw needn't show every extreme that they name: `positions`: Increasing; the j-th block of 128 rows points into the bytes j * 256 to (j + 1) * 256 - 1 and names the first and the last of them. The 2 picks of a row differ; in each aligned block of 128 rows (the rows of one index of expert and dp) no expert is named by more than 5 rows, a bound that some block reaches.
All inputs are finite; a program needn't handle non-finite values.
Results may differ from a plain program's by a relative error of at most 0.011.
Values may be sent and summed in bfloat16 or wider, within the bound.
No kernel may reach another device: no remote copies, remote signals or barrier semaphores. Data moves between devices by JAX's collectives and lax.ppermute only.
A program may use at most 64 MiB of HBM per device.

v0:
```python
import jax
import jax.numpy as jnp
from jax import lax
from jax.sharding import PartitionSpec as P


def local(
    byte_states, positions, picks, cotangent, router_weight, gate_weight, up_weight, down_weight
):
    byte_count = byte_states.shape[0]
    row_total = positions.shape[0]
    width = byte_states.shape[1]
    experts = router_weight.shape[1]
    top_count = picks.shape[1]
    capacity = max(2, 5 * row_total * top_count // (4 * experts))
    pick_total = row_total * top_count
    boundary = jnp.take(byte_states, positions % byte_count, axis=0)
    logits = jnp.dot(boundary, router_weight, preferred_element_type=jnp.float32)
    picked = jnp.take_along_axis(logits, picks, axis=1)
    leading = jax.nn.sigmoid(picked[:, 0] - picked[:, 1])
    mixing = jnp.stack([leading, 1.0 - leading], axis=1)
    mix_low = mixing.astype(jnp.bfloat16).reshape(-1)
    flat_picks = picks.reshape(-1)
    expert_ids = jnp.arange(experts, dtype=jnp.int32)
    one_hot = (flat_picks[:, None] == expert_ids[None, :]).astype(jnp.int32)
    slot_rank = jnp.sum(jnp.cumsum(one_hot, axis=0) * one_hot, axis=1) - 1
    target = flat_picks * capacity + slot_rank
    slot_source = jnp.full((experts * capacity,), pick_total, jnp.int32)
    slot_source = slot_source.at[target].set(jnp.arange(pick_total, dtype=jnp.int32))
    is_live = slot_source < pick_total
    clamped = jnp.minimum(slot_source, pick_total - 1)
    source_row = clamped // top_count
    send_rows = jnp.where(is_live[:, None], boundary[source_row], 0).reshape(
        experts, capacity, width
    )
    send_cot = jnp.where(is_live[:, None], cotangent[source_row], 0).reshape(
        experts, capacity, width
    )
    send_mix = jnp.where(is_live, mix_low[clamped], 0).reshape(experts, capacity)
    gate_full, up_full, down_full = (
        lax.all_gather(gate_weight, "dp", axis=1, tiled=True),
        lax.all_gather(up_weight, "dp", axis=1, tiled=True),
        lax.all_gather(down_weight, "dp", axis=1, tiled=True),
    )
    hidden_half = gate_full.shape[2]
    gate_up = jnp.concatenate([gate_full[0], up_full[0]], axis=1)
    down_mat = down_full[0]
    recv_rows, recv_cot, recv_mix = (
        lax.all_to_all(send_rows, "expert", split_axis=0, concat_axis=0, tiled=True),
        lax.all_to_all(send_cot, "expert", split_axis=0, concat_axis=0, tiled=True),
        lax.all_to_all(send_mix, "expert", split_axis=0, concat_axis=0, tiled=True),
    )
    sources = recv_rows.shape[0]
    slot_total = sources * capacity
    expert_rows = recv_rows.reshape(slot_total, width)
    expert_cot = recv_cot.reshape(slot_total, width)
    expert_mix = recv_mix.reshape(slot_total)
    both_pre = jnp.dot(expert_rows, gate_up, preferred_element_type=jnp.float32)
    gate_pre = both_pre[:, :hidden_half]
    up_pre = both_pre[:, hidden_half:]
    sigma = jax.nn.sigmoid(gate_pre)
    activ = gate_pre * sigma
    slope = sigma * (1.0 + gate_pre * (1.0 - sigma))
    hidden = (activ * up_pre).astype(jnp.bfloat16)
    cot_down = jnp.dot(expert_cot, down_mat, preferred_element_type=jnp.float32)
    mix_part = jnp.sum(hidden.astype(jnp.float32) * cot_down, axis=1)
    scaled = (expert_mix.astype(jnp.float32)[:, None] * expert_cot.astype(jnp.float32)).astype(
        jnp.bfloat16
    )
    hidden_grad = jnp.dot(scaled, down_mat, preferred_element_type=jnp.float32)
    gate_pre_grad = (hidden_grad * up_pre * slope).astype(jnp.bfloat16)
    up_pre_grad = (hidden_grad * activ).astype(jnp.bfloat16)
    joined = jnp.concatenate([gate_pre_grad, up_pre_grad], axis=1)
    grad_part = lax.dot_general(
        joined, gate_up, (((1,), (1,)), ((), ())), preferred_element_type=jnp.float32
    )
    weight_sum = lax.psum_scatter(
        lax.dot_general(
            expert_rows, joined, (((0,), (0,)), ((), ())), preferred_element_type=jnp.float32
        ).astype(jnp.bfloat16),
        "dp",
        scatter_dimension=0,
        tiled=True,
    ).astype(jnp.float32)
    gate_grad = weight_sum[:, :hidden_half].astype(jnp.bfloat16)[None]
    up_grad = weight_sum[:, hidden_half:].astype(jnp.bfloat16)[None]
    grad_sum, mix_sum = (
        lax.psum(grad_part.astype(jnp.bfloat16), "pair").astype(jnp.float32),
        lax.psum(mix_part.astype(jnp.bfloat16), "pair").astype(jnp.float32),
    )
    grad_low = grad_sum.astype(jnp.bfloat16).reshape(sources, capacity, width)
    mix_grad_low = mix_sum.astype(jnp.bfloat16).reshape(sources, capacity)
    back_grad, back_mix = (
        lax.all_to_all(grad_low, "expert", split_axis=0, concat_axis=0, tiled=True),
        lax.all_to_all(mix_grad_low, "expert", split_axis=0, concat_axis=0, tiled=True),
    )
    pick_grad = back_grad.reshape(experts * capacity, width)[target]
    row_sum = jnp.sum(pick_grad.reshape(row_total, top_count, width).astype(jnp.float32), axis=1)
    mix_grad = (
        back_mix.reshape(experts * capacity)[target]
        .reshape(row_total, top_count)
        .astype(jnp.float32)
    )
    blended = jnp.sum(mixing * mix_grad, axis=1, keepdims=True)
    logit_grad = mixing * (mix_grad - blended)
    pick_hot = one_hot.reshape(row_total, top_count, experts).astype(jnp.float32)
    coeffs = jnp.sum(logit_grad[:, :, None] * pick_hot, axis=1)
    router_term = jnp.dot(
        coeffs, router_weight.astype(jnp.float32).T, precision=lax.Precision.HIGHEST
    )
    row_grad = (row_sum + router_term).astype(jnp.bfloat16)
    return (row_grad, gate_grad, up_grad)


def solution(mesh):
    in_specs = (
        P(("expert", "dp"), None),
        P(("expert", "dp")),
        P(("expert", "dp"), None),
        P(("expert", "dp"), None),
        P(),
        P("expert", "dp", "pair"),
        P("expert", "dp", "pair"),
        P("expert", "dp", "pair"),
    )
    out_specs = (P(("expert", "dp"), None), P("expert", "dp", "pair"), P("expert", "dp", "pair"))
    return jax.shard_map(local, mesh=mesh, in_specs=in_specs, out_specs=out_specs, check_vma=False)
```

profile of v0, /device:TPU:33, one launch (start us, length us, event | category | flops | bytes accessed | tf_op | source)
XLA Modules:
  0.0 460.3 jit_solution(11875232396426715836)
XLA Ops:
  7.2 0.8 broadcast_multiply_fusion
  7.9 0.8 copy.53
  9.0 0.7 bitcast_or_fusion
  9.7 0.7 compare_and_fusion
  10.7 0.6 reduce-window.6
  11.6 1.4 scatter_custom_fusion
  13.3 0.9 gather_fusion
  14.4 0.3 fusion.25
  14.7 2.0 gather_fusion.6
  17.3 2.4 gather_fusion.1
  19.7 0.8 all_to_all.28
  20.4 17.7 %all-to-all-start = ((bf16[64,1,5]{2,1,0:T(2,128)(2,1)}), bf16[64,1,5]{2,1,0:T(2,128)(2,1)S(1)}, u32[]{:S(2)}, u32[]{:S(2)}) async-start(bf16[64,1,5]{2,1,0:T(2,128)(2,1)} %all_to_all.28), calls=%async_computation | async-start | bytes 65536 | tf_op jit(solution)/shard_map/all_to_all | solution.py:51
  38.1 2.4 gather_fusion.3
  40.6 1.6 gather.33
  42.3 3.0 gather_fusion.2
  45.4 3.6 gather.31
  48.9 4.0 broadcast_select_fusion
  52.9 14.6 %all-to-all-start.1 = ((bf16[64,5,2048]{2,1,0:T(8,128)(2,1)}), bf16[64,5,2048]{2,1,0:T(8,128)(2,1)S(1)}, u32[]{:S(2)}, u32[]{:S(2)}) async-start(bf16[64,5,2048]{2,1,0:T(8,128)(2,1)} %get-tuple-element.14), calls=%async_computation.1 | async-start | bytes 4194304 | tf_op jit(solution)/shard_map/all_to_all | solution.py:50
  67.6 0.7 all-gather.8.cloned.1.call-update
  68.2 94.0 %all-to-all-done.1 = bf16[64,5,2048]{2,1,0:T(8,128)(2,1)S(1)} async-done(((bf16[64,5,2048]{2,1,0:T(8,128)(2,1)}), bf16[64,5,2048]{2,1,0:T(8,128)(2,1)S(1)}, u32[]{:S(2)}, u32[]{:S(2)}) %all-to-all-start.1) | async-done | bytes 1310752 | tf_op jit(solution)/shard_map/all_to_all | solution.py:50
  162.2 10.9 %all-to-all-start.2 = ((bf16[64,5,2048]{2,1,0:T(8,128)(2,1)}), bf16[64,5,2048]{2,1,0:T(8,128)(2,1)}, u32[]{:S(2)}, u32[]{:S(2)}) async-start(bf16[64,5,2048]{2,1,0:T(8,128)(2,1)} %get-tuple-element.13), calls=%async_computation.2 | async-start | bytes 4194304 | tf_op jit(solution)/shard_map/all_to_all | solution.py:49
  173.2 0.7 all-gather.6.cloned.1.call-update
  174.0 0.7 all-gather.4.cloned.1.call-update
  174.9 1.8 multiply_convert_fusion
  176.7 3.6 convert_element_type.98
  180.4 89.3 %all-to-all-done.2 = bf16[64,5,2048]{2,1,0:T(8,128)(2,1)} async-done(((bf16[64,5,2048]{2,1,0:T(8,128)(2,1)}), bf16[64,5,2048]{2,1,0:T(8,128)(2,1)}, u32[]{:S(2)}, u32[]{:S(2)}) %all-to-all-start.2) | async-done | bytes 1310752 | tf_op jit(solution)/shard_map/all_to_all | solution.py:49
  269.7 3.6 reshape.180
  273.4 4.4 fusion.1
  277.8 3.1 multiply_convert_fusion.3
  280.9 0.7 copy-done.7
  281.7 2.3 convolution_convert_fusion.1
  284.0 3.4 reshape.181
  287.5 4.9 %convolution_convert_fusion = bf16[2048,768]{1,0:T(8,128)(2,1)} fusion(bf16[320,2048]{1,0:T(8,128)(2,1)} %reshape.180, bf16[320,384]{1,0:T(8,128)(2,1)} %copy-done.8, bf16[320,384]{1,0:T(8,128)(2,1)} %copy-done.7), kind=kOutput, calls=%fused_computation.9 | convolution fusion | flops 1009188864 | bytes 4947968 | tf_op jit(solution)/shard_map/dot_general | solution.py:78
  292.4 1.4 reshape.183
  293.8 3.0 fusion.9
  297.0 6.0 %psum.15 = bf16[64,1,5]{2,0,1:T(8,128)(2,1)S(1)} all-reduce(bf16[64,1,5]{2,0,1:T(8,128)(2,1)S(1)} %all_to_all.26), channel_id=1, replica_groups=mesh['expert'=64,'dp'=4,'pair'=2] {'pair'}, use_global_device_ids=true, to_apply=%region_7.8 | all-reduce | flops 320 | bytes 1280 | tf_op jit(solution)/shard_map/psum | solution.py:89
  303.0 19.1 %all_to_all.34 = bf16[64,1,5]{2,1,0:T(2,128)(2,1)S(1)} all-to-all(bf16[64,1,5]{2,1,0:T(2,128)(2,1)S(1)} %copy.60), channel_id=1, replica_groups=mesh['expert'=64,'dp'=4,'pair'=2] {'expert'}, dimensions={0} | all-to-all | bytes 1280 | tf_op jit(solution)/shard_map/all_to_all | solution.py:95
  322.1 3.7 all-reduce.2.cloned.1.call-done
  325.8 15.3 %all-to-all-start.3 = ((bf16[64,5,2048]{2,1,0:T(8,128)(2,1)}), bf16[64,5,2048]{2,1,0:T(8,128)(2,1)}, u32[]{:S(2)}, u32[]{:S(2)}) async-start(bf16[64,5,2048]{2,1,0:T(8,128)(2,1)} %all-reduce.2.cloned.1.call-done), calls=%async_computation.3 | async-start | bytes 4194304 | tf_op jit(solution)/shard_map/all_to_all | solution.py:94
  341.4 1.9 gather_fusion.5
  343.6 31.8 %reduce-scatter.2.cloned.1.call-done = bf16[512,768]{1,0:T(8,128)(2,1)} async-done(((bf16[2048,768]{1,0:T(8,128)(2,1)}), bf16[512,768]{1,0:T(8,128)(2,1)}) %reduce-scatter.2.cloned.1.call-update) | async-done | bytes 786448 | tf_op jit(solution)/shard_map/reduce_scatter | solution.py:77
  375.4 2.1 slice_bitcast_fusion
  377.4 62.6 %all-to-all-done.3 = bf16[64,5,2048]{2,1,0:T(8,128)(2,1)} async-done(((bf16[64,5,2048]{2,1,0:T(8,128)(2,1)}), bf16[64,5,2048]{2,1,0:T(8,128)(2,1)}, u32[]{:S(2)}, u32[]{:S(2)}) %all-to-all-start.3) | async-done | bytes 1310752 | tf_op jit(solution)/shard_map/all_to_all | solution.py:94
  440.0 2.6 reshape.182
  442.6 2.3 gather_fusion.4
  444.9 2.4 reshape.186
  447.3 3.9 reduce_sum.46
  451.2 2.6 fusion
  (66 shorter events, 3.2 us)
Async XLA Ops:
  7.2 6.2 %copy-start = (bf16[256,2048]{1,0:T(8,128)(2,1)S(1)}, bf16[256,2048]{1,0:T(8,128)(2,1)}, u32[]{:S(2)}) copy-start(bf16[256,2048]{1,0:T(8,128)(2,1)} %param.8) | copy-start | bytes 3145732
  13.3 1.1 copy-start.3
  14.7 2.2 copy-start.4
  20.4 32.5 %all-to-all-start = ((bf16[64,1,5]{2,1,0:T(2,128)(2,1)}), bf16[64,1,5]{2,1,0:T(2,128)(2,1)S(1)}, u32[]{:S(2)}, u32[]{:S(2)}) async-start(bf16[64,1,5]{2,1,0:T(2,128)(2,1)} %all_to_all.28), calls=%async_computation | async-start | bytes 65536 | tf_op jit(solution)/shard_map/all_to_all | solution.py:51
  40.5 1.8 copy-start.1
  45.4 3.6 copy-start.2
  52.9 109.3 %all-to-all-start.1 = ((bf16[64,5,2048]{2,1,0:T(8,128)(2,1)}), bf16[64,5,2048]{2,1,0:T(8,128)(2,1)S(1)}, u32[]{:S(2)}, u32[]{:S(2)}) async-start(bf16[64,5,2048]{2,1,0:T(8,128)(2,1)} %get-tuple-element.14), calls=%async_computation.1 | async-start | bytes 4194304 | tf_op jit(solution)/shard_map/all_to_all | solution.py:50
  67.5 205.9 %all-gather.8.cloned.1.call-start = ((), (), s32[]{:S(2)}) async-start(), calls=%async_computation.8 | async-start | bytes 1966080 | tf_op jit(solution)/shard_map/all_gather | solution.py:42
  162.2 107.5 %all-to-all-start.2 = ((bf16[64,5,2048]{2,1,0:T(8,128)(2,1)}), bf16[64,5,2048]{2,1,0:T(8,128)(2,1)}, u32[]{:S(2)}, u32[]{:S(2)}) async-start(bf16[64,5,2048]{2,1,0:T(8,128)(2,1)} %get-tuple-element.13), calls=%async_computation.2 | async-start | bytes 4194304 | tf_op jit(solution)/shard_map/all_to_all | solution.py:49
  173.2 100.2 %all-gather.6.cloned.1.call-start = ((), (), s32[]{:S(2)}) async-start(), calls=%async_computation.7 | async-start | bytes 1966080 | tf_op jit(solution)/shard_map/all_gather | solution.py:41
  173.9 103.9 %all-gather.4.cloned.1.call-start = ((), (), s32[]{:S(2)}) async-start(), calls=%async_computation.6 | async-start | bytes 1966080 | tf_op jit(solution)/shard_map/all_gather | solution.py:43
  174.6 151.2 %all-reduce.2.cloned.1.call-start = ((), (), s32[]{:S(2)}) async-start(), calls=%async_computation.9 | async-start | bytes 4194304 | tf_op jit(solution)/shard_map/psum | solution.py:88
  277.8 3.9 copy-start.5
  277.8 3.9 copy-start.6
  280.9 0.7 copy-start.7
  280.9 0.8 copy-start.8
  287.4 87.9 %reduce-scatter.2.cloned.1.call-start = ((), (), s32[]{:S(2)}) async-start(), calls=%async_computation.10 | async-start | bytes 3932160 | tf_op jit(solution)/shard_map/reduce_scatter | solution.py:77
  325.8 114.2 %all-to-all-start.3 = ((bf16[64,5,2048]{2,1,0:T(8,128)(2,1)}), bf16[64,5,2048]{2,1,0:T(8,128)(2,1)}, u32[]{:S(2)}, u32[]{:S(2)}) async-start(bf16[64,5,2048]{2,1,0:T(8,128)(2,1)} %all-reduce.2.cloned.1.call-done), calls=%async_computation.3 | async-start | bytes 4194304 | tf_op jit(solution)/shard_map/all_to_all | solution.py:94
Sparse Core Ops, SparseCore 0:
  70.4 36.1 all-gather.7
  176.1 35.7 all-gather.5
  213.9 34.1 all-gather.3
  287.5 38.2 all-reduce.1
  328.5 46.8 reduce-scatter.1
where the time goes:
time: 461 us; the launch traced here: 460 us
  waiting for transfers between devices  283 us (61%)
  starting transfers between devices  58.8 us (13%)
  local copies, waits for them, and re-layouts  45.2 us (10%)
  blocking collectives  25.1 us (5%)
  matrix products  20.6 us (4%)
  between operations  14.1 us (3%)
  other arithmetic  13 us (3%)
    all_to_all x1, waiting for transfers between devices, local(): lax.all_to_all(send_cot, 'expert', split_axis=0, concat_axis=0, tiled=True)  94 us
    all_to_all x1, waiting for transfers between devices, local(): lax.all_to_all(send_rows, 'expert', split_axis=0, concat_axis=0, tiled=True)  89.3 us
    all_to_all x1, waiting for transfers between devices, local(): lax.all_to_all(grad_low, 'expert', split_axis=0, concat_axis=0, tiled=True)  62.6 us
    reduce_scatter x1, waiting for transfers between devices, local(): lax.psum_scatter(lax.dot_general(expert_rows, joined, (((0,), (0,)), ((),...  31.8 us
    all_to_all x1, blocking collectives, local(): lax.all_to_all(mix_grad_low, 'expert', split_axis=0, concat_axis=0, tiled...  19.1 us
    all_to_all x1, starting transfers between devices, local(): lax.all_to_all(send_mix, 'expert', split_axis=0, concat_axis=0, tiled=True)  17.7 us
    all_to_all x1, starting transfers between devices, local(): lax.all_to_all(grad_low, 'expert', split_axis=0, concat_axis=0, tiled=True)  15.3 us
    all_to_all x1, starting transfers between devices, local(): lax.all_to_all(send_cot, 'expert', split_axis=0, concat_axis=0, tiled=True)  14.6 us
  transfers between devices with their start and end apart: 9, of which 5 were waited for; matrix products, arithmetic and copies ran while one was open for 9% of the time, Pallas kernels for 0%

commit v1 on v0

v1 whole, which is shorter than its diff:
```python
import jax
import jax.numpy as jnp
from jax import lax
from jax.experimental import pallas as pl
from jax.experimental.pallas import tpu as pltpu
from jax.sharding import PartitionSpec as P


F32 = jnp.float32
BF16 = jnp.bfloat16
LANE = 128
VMEM_LIMIT = 24 * 1024 * 1024


def vm(x):
    return pltpu.with_memory_space_constraint(x, pltpu.VMEM)


def vspec():
    return pl.BlockSpec(memory_space=pltpu.VMEM)


def aspec():
    return pl.BlockSpec(memory_space=pl.ANY)


def sspec():
    return pl.BlockSpec(memory_space=pltpu.SMEM)


def params():
    return pltpu.CompilerParams(vmem_limit_bytes=VMEM_LIMIT)


def iota(shape, dim):
    return lax.broadcasted_iota(jnp.int32, shape, dim)


def dot(a, b):
    return jnp.dot(a, b, preferred_element_type=F32)


def dot_nt(a, b):
    return lax.dot_general(a, b, (((1,), (1,)), ((), ())), preferred_element_type=F32)


def dot_tn(a, b):
    return lax.dot_general(a, b, (((0,), (0,)), ((), ())), preferred_element_type=F32)


def local(
    byte_states, positions, picks, cotangent, router_weight, gate_weight, up_weight, down_weight
):
    byte_count, width = byte_states.shape
    rows = positions.shape[0]
    experts = router_weight.shape[1]
    cap = 5
    slots = cap * experts
    half = width // 2
    hc = half // LANE
    shard, fh = gate_weight.shape[1], gate_weight.shape[2]
    dps = width // shard
    disp = cap * 2 * hc
    back = cap * hc + 8

    pair = lax.axis_index("pair").astype(jnp.int32)
    dp = lax.axis_index("dp").astype(jnp.int32)
    idx = jnp.stack([pair, dp])

    def dispatch_kernel(
        idx_ref, bytes_ref, pos_ref, picks_ref, cot_ref, router_ref, out_ref, meta_ref, bnd, scr
    ):
        off = pl.multiple_of(idx_ref[0] * half, half)
        pos = jnp.bitwise_and(pos_ref[...], byte_count - 1)
        pos_hot = jnp.where(iota((byte_count, rows), 0) == pos, 1.0, 0.0).astype(BF16)
        bnd[...] = dot_tn(pos_hot, bytes_ref[...]).astype(BF16)
        p0 = picks_ref[0:1, :]
        p1 = picks_ref[1:2, :]
        ids = iota((experts, rows), 0)
        hot0 = jnp.where(ids == p0, 1.0, 0.0)
        hot1 = jnp.where(ids == p1, 1.0, 0.0)
        before = jnp.where(iota((rows, rows), 0) < iota((rows, rows), 1), 1.0, 0.0).astype(BF16)
        counts = dot((hot0 + hot1).astype(BF16), before)
        rank0 = jnp.sum(hot0 * counts, axis=0, keepdims=True)
        rank1 = jnp.sum(hot1 * counts, axis=0, keepdims=True)
        target0 = rank0 * experts + p0.astype(F32)
        target1 = rank1 * experts + p1.astype(F32)
        logits = dot_nt(router_ref[...], bnd[...])
        l0 = jnp.sum(hot0 * logits, axis=0, keepdims=True)
        l1 = jnp.sum(hot1 * logits, axis=0, keepdims=True)
        mix0 = jax.nn.sigmoid(l0 - l1)
        mix1 = 1.0 - mix0
        low0 = mix0.astype(BF16).astype(F32)
        low1 = mix1.astype(BF16).astype(F32)
        slot_ids = iota((slots, rows), 0).astype(F32)
        sel0 = slot_ids == target0
        sel1 = slot_ids == target1
        take = (jnp.where(sel0, 1.0, 0.0) + jnp.where(sel1, 1.0, 0.0)).astype(BF16)
        take_mix = (jnp.where(sel0, low0, 0.0) + jnp.where(sel1, low1, 0.0)).astype(BF16)
        send = (dot(take, bnd[:, pl.ds(off, half)]), dot(take_mix, cot_ref[:, pl.ds(off, half)]))
        for s in range(cap):
            for t in range(2):
                for c in range(hc):
                    scr[pl.ds((s * 2 + t) * hc + c, experts, stride=disp), :] = send[t][
                        s * experts : (s + 1) * experts, c * LANE : (c + 1) * LANE
                    ]
        out_ref[...] = scr[...].astype(BF16)
        meta_ref[...] = jnp.concatenate(
            [target0, target1, mix0, mix1, p0.astype(F32), p1.astype(F32), mix0, mix1], axis=0
        )

    payload, meta = pl.pallas_call(
        dispatch_kernel,
        out_shape=(
            jax.ShapeDtypeStruct((experts * disp, LANE), BF16),
            pltpu.VMEM((8, rows), F32),
        ),
        in_specs=[sspec()] + [vspec()] * 5,
        out_specs=(vspec(), vspec()),
        scratch_shapes=[pltpu.VMEM((rows, width), BF16), pltpu.VMEM((experts * disp, LANE), F32)],
        compiler_params=params(),
        name="dispatch",
    )(
        idx,
        byte_states,
        positions.reshape(1, rows),
        picks.T,
        cotangent,
        router_weight.T,
    )

    def exchange(x, count):
        return lax.all_to_all(
            x.reshape(experts, count, LANE), "expert", split_axis=0, concat_axis=0, tiled=True
        ).reshape(experts * count, LANE)

    recv = exchange(payload, disp)

    def aux_kernel(idx_ref, meta_ref, router_ref, hot_ref, delta_ref, mix_ref):
        off = pl.multiple_of(idx_ref[0] * half, half)
        slot_ids = iota((3 * LANE, rows), 0).astype(F32)
        for k in range(2):
            hot = jnp.where(slot_ids == meta_ref[k : k + 1, :], 1.0, 0.0)
            hot_ref[k * rows : (k + 1) * rows, :] = hot.T.astype(BF16)
        ids = iota((LANE, rows), 0).astype(F32)
        diff = jnp.where(ids == meta_ref[4:5, :], 1.0, 0.0) - jnp.where(
            ids == meta_ref[5:6, :], 1.0, 0.0
        )
        diff = diff.T.astype(BF16)[:, :experts]
        delta_ref[...] = dot(diff, router_ref[:, pl.ds(off, half)])
        cols = jnp.concatenate([meta_ref[...], jnp.zeros((LANE - 8, rows), F32)], axis=0)
        mix_ref[...] = cols.T

    hots, delta, mix_cols = pl.pallas_call(
        aux_kernel,
        out_shape=(
            jax.ShapeDtypeStruct((2 * rows, 3 * LANE), BF16),
            jax.ShapeDtypeStruct((rows, half), F32),
            jax.ShapeDtypeStruct((rows, LANE), F32),
        ),
        in_specs=[sspec()] + [vspec()] * 2,
        out_specs=(vspec(),) * 3,
        compiler_params=params(),
        name="aux",
    )(idx, vm(meta), router_weight.T)

    weights = jnp.stack([gate_weight[0], up_weight[0], down_weight[0]])
    pieces = [weights]
    for k in range(1, dps):
        pieces.append(lax.ppermute(weights, "dp", [(i, (i - k) % dps) for i in range(dps)]))

    def assemble_kernel(idx_ref, *refs):
        out_ref = refs[dps]
        y = idx_ref[1]
        for k in range(dps):
            row = pl.multiple_of(((y + k) % dps) * shard, shard)
            out_ref[:, pl.ds(row, shard), :] = refs[k][...]

    full = pl.pallas_call(
        assemble_kernel,
        out_shape=jax.ShapeDtypeStruct((3, width, fh), BF16),
        in_specs=[sspec()] + [vspec()] * dps,
        out_specs=vspec(),
        compiler_params=params(),
        name="assemble",
    )(idx, *[vm(x) for x in pieces])

    swap = [(0, 1), (1, 0)]
    recv_other = lax.ppermute(recv, "pair", swap)

    def unpack(ref, wide, x_dst, s_dst):
        wide[...] = ref[...].astype(F32)
        for s in range(cap):
            for t, dst in ((0, x_dst), (1, s_dst)):
                for c in range(hc):
                    val = wide[pl.ds((s * 2 + t) * hc + c, experts, stride=disp), :]
                    dst[s * experts : (s + 1) * experts, c * LANE : (c + 1) * LANE] = val.astype(
                        BF16
                    )

    def fetch(w_hbm, w_buf, sem, h, count):
        row = pl.multiple_of(h * half, half)
        return pltpu.make_async_copy(w_hbm.at[pl.ds(0, count), pl.ds(row, half), :], w_buf, sem)

    def own_kernel(idx_ref, recv_ref, w_hbm, x_ref, pre_ref, wide, s_buf, w_buf, sem):
        load = fetch(w_hbm, w_buf, sem, idx_ref[0], 3)
        load.start()
        unpack(recv_ref, wide, x_ref, s_buf)
        load.wait()
        pre_ref[0] = dot(x_ref[...], w_buf[0])
        pre_ref[1] = dot(x_ref[...], w_buf[1])
        pre_ref[2] = dot(s_buf[...], w_buf[2])

    x_own, pre = pl.pallas_call(
        own_kernel,
        out_shape=(
            pltpu.VMEM((slots, half), BF16),
            pltpu.VMEM((3, slots, fh), F32),
        ),
        in_specs=[sspec(), vspec(), aspec()],
        out_specs=(vspec(),) * 2,
        scratch_shapes=[
            pltpu.VMEM((experts * disp, LANE), F32),
            pltpu.VMEM((slots, half), BF16),
            pltpu.VMEM((3, half, fh), BF16),
            pltpu.SemaphoreType.DMA(()),
        ],
        compiler_params=params(),
        name="own",
    )(idx, vm(recv), full)

    def grads_kernel(
        idx_ref, recv_ref, w_hbm, pre_ref, x_ref, joined_ref, send_ref, mixed_ref, wide, s_buf, w_buf, sem
    ):
        load = fetch(w_hbm, w_buf, sem, 1 - idx_ref[0], 3)
        load.start()
        unpack(recv_ref, wide, x_ref, s_buf)
        load.wait()
        gate = pre_ref[0] + dot(x_ref[...], w_buf[0])
        up = pre_ref[1] + dot(x_ref[...], w_buf[1])
        grad = pre_ref[2] + dot(s_buf[...], w_buf[2])
        sigma = jax.nn.sigmoid(gate)
        activ = gate * sigma
        slope = sigma * (1.0 + gate * (1.0 - sigma))
        hidden = (activ * up).astype(BF16).astype(F32)
        mixed = jnp.sum(hidden * grad, axis=1, keepdims=True)
        gate_grad = (grad * up * slope).astype(BF16)
        up_grad = (grad * activ).astype(BF16)
        joined_ref[:, :fh] = gate_grad
        joined_ref[:, fh:] = up_grad
        send_ref[:, :half] = (
            dot_nt(gate_grad, w_buf[0]) + dot_nt(up_grad, w_buf[1])
        ).astype(BF16)
        wide_mixed = jnp.broadcast_to(mixed, (slots, LANE))
        high = wide_mixed.astype(BF16).astype(F32)
        mixed_ref[...] = wide_mixed
        send_ref[:, half:] = jnp.where(
            iota((slots, LANE), 1) < LANE // 2, high, wide_mixed - high
        ).astype(BF16)

    x_other, joined, send, mixed = pl.pallas_call(
        grads_kernel,
        out_shape=(
            pltpu.VMEM((slots, half), BF16),
            pltpu.VMEM((slots, 2 * fh), BF16),
            pltpu.VMEM((slots, half + LANE), BF16),
            pltpu.VMEM((slots, LANE), F32),
        ),
        in_specs=[sspec(), vspec(), aspec(), vspec()],
        out_specs=(vspec(),) * 4,
        scratch_shapes=[
            pltpu.VMEM((experts * disp, LANE), F32),
            pltpu.VMEM((slots, half), BF16),
            pltpu.VMEM((3, half, fh), BF16),
            pltpu.SemaphoreType.DMA(()),
        ],
        compiler_params=params(),
        name="grads",
    )(idx, vm(recv_other), full, vm(pre))

    sent = lax.ppermute(send, "pair", swap)

    def keep_kernel(idx_ref, joined_ref, w_hbm, keep_ref, w_buf, sem):
        load = fetch(w_hbm, w_buf, sem, idx_ref[0], 2)
        load.start()
        load.wait()
        keep_ref[...] = dot_nt(joined_ref[:, :fh], w_buf[0]) + dot_nt(joined_ref[:, fh:], w_buf[1])

    keep = pl.pallas_call(
        keep_kernel,
        out_shape=pltpu.VMEM((slots, half), F32),
        in_specs=[sspec(), vspec(), aspec()],
        out_specs=vspec(),
        scratch_shapes=[pltpu.VMEM((2, half, fh), BF16), pltpu.SemaphoreType.DMA(())],
        compiler_params=params(),
        name="keep",
    )(idx, vm(joined), full)

    def weight_kernel(idx_ref, own_ref, oth_ref, joined_ref, *refs):
        outs = refs[:dps]
        x_all = refs[dps]
        p = idx_ref[0]
        y = idx_ref[1]
        x_all[:, pl.ds(pl.multiple_of(p * half, half), half)] = own_ref[...]
        x_all[:, pl.ds(pl.multiple_of((1 - p) * half, half), half)] = oth_ref[...]
        for k in range(dps):
            col = pl.multiple_of(((y + k) % dps) * shard, shard)
            outs[k][...] = dot_tn(x_all[:, pl.ds(col, shard)], joined_ref[...]).astype(BF16)

    sums = pl.pallas_call(
        weight_kernel,
        out_shape=(pltpu.VMEM((shard, 2 * fh), BF16),) * dps,
        in_specs=[sspec()] + [vspec()] * 3,
        out_specs=(vspec(),) * dps,
        scratch_shapes=[pltpu.VMEM((slots, width), BF16)],
        compiler_params=params(),
        name="weight",
    )(idx, vm(x_own), vm(x_other), vm(joined))

    def pack_kernel(keep_ref, mixed_ref, sent_ref, out_ref, scr):
        for c in range(hc):
            lanes = slice(c * LANE, (c + 1) * LANE)
            total = keep_ref[:, lanes] + sent_ref[:, lanes].astype(F32)
            for s in range(cap):
                scr[pl.ds(s * hc + c, experts, stride=back), :] = total[
                    s * experts : (s + 1) * experts
                ]
        tail = sent_ref[:, half:].astype(F32)
        full = mixed_ref[...] + tail + pltpu.roll(tail, LANE // 2, 1)
        high = full.astype(BF16).astype(F32)
        both = jnp.where(iota((slots, LANE), 1) < LANE // 2, high, full - high)
        for s in range(8):
            part = both[s * experts : (s + 1) * experts] if s < cap else jnp.zeros((experts, LANE), F32)
            scr[pl.ds(cap * hc + s, experts, stride=back), :] = part
        out_ref[...] = scr[...].astype(BF16)

    packed = pl.pallas_call(
        pack_kernel,
        out_shape=jax.ShapeDtypeStruct((experts * back, LANE), BF16),
        in_specs=[vspec()] * 3,
        out_specs=vspec(),
        scratch_shapes=[pltpu.VMEM((experts * back, LANE), F32)],
        compiler_params=params(),
        name="pack",
    )(vm(keep), vm(mixed), vm(sent))

    returned = exchange(packed, back)

    moved = [sums[0]]
    for k in range(1, dps):
        moved.append(lax.ppermute(sums[k], "dp", [(i, (i + k) % dps) for i in range(dps)]))
    weight_sum = moved[0].astype(F32)
    for piece in moved[1:]:
        weight_sum = weight_sum + piece.astype(F32)
    weight_sum = weight_sum.astype(BF16)
    gate_out = weight_sum[:, :fh][None]
    up_out = weight_sum[:, fh:][None]

    def combine_kernel(back_ref, hot_ref, delta_ref, mix_ref, out_ref, wide, grads, small):
        wide[...] = back_ref[...].astype(F32)
        for s in range(cap):
            span = slice(s * experts, (s + 1) * experts)
            for c in range(hc):
                val = wide[pl.ds(s * hc + c, experts, stride=back), :]
                grads[span, c * LANE : (c + 1) * LANE] = val.astype(BF16)
            small[span, :] = wide[pl.ds(cap * hc + s, experts, stride=back), :].astype(BF16)
        grads[slots:, :] = jnp.zeros((3 * LANE - slots, half), BF16)
        small[slots:, :] = jnp.zeros((3 * LANE - slots, LANE), BF16)
        hot0 = hot_ref[:rows, :]
        hot1 = hot_ref[rows:, :]
        u0 = dot(hot0, small[...])
        u1 = dot(hot1, small[...])
        u0 = u0[:, 0:1] + u0[:, LANE // 2 : LANE // 2 + 1]
        u1 = u1[:, 0:1] + u1[:, LANE // 2 : LANE // 2 + 1]
        logit = mix_ref[:, 3:4] * u0 - mix_ref[:, 2:3] * u1
        out_ref[...] = (dot(hot0 + hot1, grads[...]) + logit * delta_ref[...]).astype(BF16)

    row_half = pl.pallas_call(
        combine_kernel,
        out_shape=jax.ShapeDtypeStruct((rows, half), BF16),
        in_specs=[vspec()] * 4,
        out_specs=vspec(),
        scratch_shapes=[
            pltpu.VMEM((experts * back, LANE), F32),
            pltpu.VMEM((3 * LANE, half), BF16),
            pltpu.VMEM((3 * LANE, LANE), BF16),
        ],
        compiler_params=params(),
        name="combine",
    )(vm(returned), hots, delta, mix_cols)

    row_half_other = lax.ppermute(row_half, "pair", swap)
    row_grad = jnp.where(
        pair == 0,
        jnp.concatenate([row_half, row_half_other], axis=1),
        jnp.concatenate([row_half_other, row_half], axis=1),
    )
    return (row_grad, gate_out, up_out)


def solution(mesh):
    in_specs = (
        P(("expert", "dp"), None),
        P(("expert", "dp")),
        P(("expert", "dp"), None),
        P(("expert", "dp"), None),
        P(),
        P("expert", "dp", "pair"),
        P("expert", "dp", "pair"),
        P("expert", "dp", "pair"),
    )
    out_specs = (P(("expert", "dp"), None), P("expert", "dp", "pair"), P("expert", "dp", "pair"))

    return jax.shard_map(local, mesh=mesh, in_specs=in_specs, out_specs=out_specs, check_vma=False)
```

time: 461 us -> 230 us (0.50)
  the two profiles are of different devices: /device:TPU:33 before, /device:TPU:1 now
where the time goes in v1:
time: 230 us; the launch traced here: 229 us
  waiting for transfers between devices  139 us (60%)
  starting transfers between devices  59.2 us (26%)
  Pallas kernels  19.3 us (8%)
  local copies, waits for them, and re-layouts  7.77 us (3%)
  other arithmetic  3.05 us (1%)
    all_to_all x2, waiting for transfers between devices, exchange(): lax.all_to_all(x.reshape(experts, count, LANE), 'expert', split_axis=0, c...  86.9 us
    ppermute x3, waiting for transfers between devices, local(): lax.ppermute(weights, 'dp', [(i, (i - k) % dps) for i in range(dps)])  51.7 us
    all_to_all x2, starting transfers between devices, exchange(): lax.all_to_all(x.reshape(experts, count, LANE), 'expert', split_axis=0, c...  25.9 us
    ppermute x3, starting transfers between devices, local(): lax.ppermute(weights, 'dp', [(i, (i - k) % dps) for i in range(dps)])  9.51 us
    ppermute x3, starting transfers between devices, local(): lax.ppermute(sums[k], 'dp', [(i, (i + k) % dps) for i in range(dps)])  8.4 us
    ppermute x1, starting transfers between devices, local(): recv_other = lax.ppermute(recv, 'pair', swap)  7.53 us
    unnamed x22, local copies, waits for them, and re-layouts  5.75 us
    ppermute x1, starting transfers between devices, local(): row_half_other = lax.ppermute(row_half, 'pair', swap)  5.44 us
  transfers between devices with their start and end apart: 11, of which 5 were waited for; matrix products, arithmetic and copies ran while one was open for 2% of the time, Pallas kernels for 5%

profile of v1, /device:TPU:1, one launch (start us, length us, event | category | flops | bytes accessed | tf_op | source)
XLA Modules:
  0.0 229.1 jit_solution(1786628402195492626)
XLA Ops:
  0.6 0.1 pad_add_fusion.idx_ref
  0.7 1.2 copy-done
  1.9 0.9 copy-done.1
  2.9 1.0 copy-done.5
  3.9 0.7 copy-done.6
  4.6 0.7 copy-done.7
  5.3 3.1 %dispatch.1 = (bf16[5120,128]{1,0:T(8,128)(2,1)}, f32[8,128]{1,0:T(8,128)S(1)}) custom-call(s32[2]{0:T(128)S(1)} %pad_add_fusion.idx_ref, bf16[256,2048]{1,0:T(8,128)(2,1)S(1)} %copy-done, s32[1,128]{1,0:T(1,128)S(1)} %bitcast.19, s32[2,128]{1,0:T(2,128)S(1)} %bitcast.18, bf16[128,2048]{1,0:T(8,128)(2,1)S(1)} %copy-done.5, bf16[64,2048]{1,0:T(8,128)(2,1)S(1)} %bitcast.16), custom_call_target="tpu_custom_call" | custom-call | tf_op jit(solution)/shard_map/dispatch/pallas_call | solution.py:112
  8.4 19.2 %all-to-all-start = ((bf16[64,80,128]{2,1,0:T(8,128)(2,1)}), bf16[64,80,128]{2,1,0:T(8,128)(2,1)S(1)}, u32[]{:S(2)}, u32[]{:S(2)}) async-start(bf16[64,80,128]{2,1,0:T(8,128)(2,1)} %bitcast.5), calls=%async_computation | async-start | bytes 2621440 | tf_op jit(solution)/shard_map/all_to_all | solution.py:133
  27.6 0.0 copy-done.8
  27.7 60.4 %all-to-all-done = bf16[64,80,128]{2,1,0:T(8,128)(2,1)S(1)} async-done(((bf16[64,80,128]{2,1,0:T(8,128)(2,1)}), bf16[64,80,128]{2,1,0:T(8,128)(2,1)S(1)}, u32[]{:S(2)}, u32[]{:S(2)}) %all-to-all-start) | async-done | bytes 1310752 | tf_op jit(solution)/shard_map/all_to_all | solution.py:133
  88.1 7.5 %collective-permute-start = (bf16[5120,128]{1,0:T(8,128)(2,1)S(1)}, bf16[5120,128]{1,0:T(8,128)(2,1)S(1)}, u32[]{:S(2)}, u32[]{:S(2)}) collective-permute-start(bf16[5120,128]{1,0:T(8,128)(2,1)S(1)} %bitcast.13), channel_id=1, source_target_pairs={{0,1},{1,0},{2,3},{3,2},{4,5},{5,4},{6,7},{7,6},{8,9},{9,8},{10,11... | collective-permute-start | bytes 3932168 | tf_op jit(solution)/shard_map/ppermute | solution.py:189
  95.7 0.0 copy-done.9
  95.7 0.1 constant_dynamic-update-slice_fusion.1
  95.7 1.1 constant_dynamic-update-slice_fusion.refs_0_
  96.8 4.6 %collective-permute-start.1 = (bf16[3,512,384]{2,1,0:T(8,128)(2,1)S(1)}, bf16[3,512,384]{2,1,0:T(8,128)(2,1)S(1)}, u32[]{:S(2)}, u32[]{:S(2)}) collective-permute-start(bf16[3,512,384]{2,1,0:T(8,128)(2,1)S(1)} %constant_dynamic-update-slice_fusion.refs_0_), channel_id=1, source_target_pairs={{0,6},{2,0},{4,2},{6,4},{1,7},{3,1},{5,3},{7,5},{8,14},{10,8},{12,... | collective-permute-start | bytes 3538952 | tf_op jit(solution)/shard_map/ppermute | solution.py:170
  101.5 2.3 collective-permute-start.2
  103.7 2.6 %collective-permute-start.3 = (bf16[3,512,384]{2,1,0:T(8,128)(2,1)S(1)}, bf16[3,512,384]{2,1,0:T(8,128)(2,1)S(1)}, u32[]{:S(2)}, u32[]{:S(2)}) collective-permute-start(bf16[3,512,384]{2,1,0:T(8,128)(2,1)S(1)} %constant_dynamic-update-slice_fusion.refs_0_), channel_id=1, source_target_pairs={{0,2},{2,4},{4,6},{6,0},{1,3},{3,5},{5,7},{7,1},{8,10},{10,12},{12... | collective-permute-start | bytes 3538952 | tf_op jit(solution)/shard_map/ppermute | solution.py:170
  106.3 45.6 %collective-permute-done.1.refs_1_ = bf16[3,512,384]{2,1,0:T(8,128)(2,1)S(1)} collective-permute-done((bf16[3,512,384]{2,1,0:T(8,128)(2,1)S(1)}, bf16[3,512,384]{2,1,0:T(8,128)(2,1)S(1)}, u32[]{:S(2)}, u32[]{:S(2)}) %collective-permute-start.1) | collective-permute-done | bytes 1179680 | tf_op jit(solution)/shard_map/ppermute | solution.py:170
  151.9 0.0 collective-permute-done.2.refs_2_
  151.9 6.1 %collective-permute-done.3.refs_3_ = bf16[3,512,384]{2,1,0:T(8,128)(2,1)S(1)} collective-permute-done((bf16[3,512,384]{2,1,0:T(8,128)(2,1)S(1)}, bf16[3,512,384]{2,1,0:T(8,128)(2,1)S(1)}, u32[]{:S(2)}, u32[]{:S(2)}) %collective-permute-start.3) | collective-permute-done | bytes 1179680 | tf_op jit(solution)/shard_map/ppermute | solution.py:170
  158.0 1.0 assemble.1.w_hbm
  159.0 2.9 %own.1 = (bf16[320,1024]{1,0:T(8,128)(2,1)S(1)}, f32[3,320,384]{2,1,0:T(8,128)S(1)}) custom-call(s32[2]{0:T(128)S(1)} %pad_add_fusion.idx_ref, bf16[5120,128]{1,0:T(8,128)(2,1)S(1)} %bitcast.14, bf16[3,2048,384]{2,1,0:T(8,128)(2,1)S(1)} %assemble.1.w_hbm), custom_call_target="tpu_custom_call" | custom-call | tf_op jit(solution)/shard_map/own/pallas_call | solution.py:214
  161.9 0.0 collective-permute-done.recv_ref
  161.9 3.8 %grads.1 = (bf16[320,1024]{1,0:T(8,128)(2,1)S(1)}, bf16[320,768]{1,0:T(8,128)(2,1)S(1)}, bf16[320,1152]{1,0:T(8,128)(2,1)S(1)}, f32[320,128]{1,0:T(8,128)S(1)}) custom-call(s32[2]{0:T(128)S(1)} %pad_add_fusion.idx_ref, bf16[5120,128]{1,0:T(8,128)(2,1)S(1)} %collective-permute-done.recv_ref, bf16[3,2048,384]{2,1,0:T(8,128)(2,1)S(1)} %assemble.1.w_hbm, ...), custom_call_target="tpu_custom_call" | custom-call | tf_op jit(solution)/shard_map/grads/pallas_call | solution.py:261
  165.8 0.0 copy-start.3
  165.8 2.4 %collective-permute-start.4 = (bf16[320,1152]{1,0:T(8,128)(2,1)S(1)}, bf16[320,1152]{1,0:T(8,128)(2,1)S(1)}, u32[]{:S(2)}, u32[]{:S(2)}) collective-permute-start(bf16[320,1152]{1,0:T(8,128)(2,1)S(1)} %get-tuple-element.22), channel_id=1, source_target_pairs={{0,1},{1,0},{2,3},{3,2},{4,5},{5,4},{6,7},{7,6},{8,9},{9,8},{10,11... | collective-permute-start | bytes 2211848 | tf_op jit(solution)/shard_map/ppermute | solution.py:281
  168.2 1.5 keep.1.keep_ref
  169.8 0.0 copy-done.3
  169.8 0.3 collective-permute-done.4.sent_ref
  170.0 1.8 pack.1
  171.8 6.7 %all-to-all-start.1 = ((bf16[64,48,128]{2,1,0:T(8,128)(2,1)}), bf16[64,48,128]{2,1,0:T(8,128)(2,1)S(1)}, u32[]{:S(2)}, u32[]{:S(2)}) async-start(bf16[64,48,128]{2,1,0:T(8,128)(2,1)} %bitcast.7), calls=%async_computation.1 | async-start | bytes 1572864 | tf_op jit(solution)/shard_map/all_to_all | solution.py:133
  178.5 0.0 copy-start.4
  178.5 1.1 copy-done.4
  179.6 3.4 %weight.1 = (bf16[512,768]{1,0:T(8,128)(2,1)S(1)}, bf16[512,768]{1,0:T(8,128)(2,1)}, bf16[512,768]{1,0:T(8,128)(2,1)}, bf16[512,768]{1,0:T(8,128)(2,1)}) custom-call(s32[2]{0:T(128)S(1)} %pad_add_fusion.idx_ref, bf16[320,1024]{1,0:T(8,128)(2,1)S(1)} %get-tuple-element.27.own_ref, bf16[320,1024]{1,0:T(8,128)(2,1)S(1)} %copy-done.4, ...), custom_call_target="tpu_custom_call" | custom-call | tf_op jit(solution)/shard_map/weight/pallas_call | solution.py:310
  183.0 1.9 collective-permute-start.6
  184.9 3.4 %collective-permute-start.7 = (bf16[512,768]{1,0:T(8,128)(2,1)}, bf16[512,768]{1,0:T(8,128)(2,1)}, u32[]{:S(2)}, u32[]{:S(2)}) collective-permute-start(bf16[512,768]{1,0:T(8,128)(2,1)} %get-tuple-element.31), channel_id=1, source_target_pairs={{0,4},{2,6},{4,0},{6,2},{1,5},{3,7},{5,1},{7,3},{8,12},{10,14},{12... | collective-permute-start | bytes 2359304 | tf_op jit(solution)/shard_map/ppermute | solution.py:351
  188.3 3.1 %collective-permute-start.8 = (bf16[512,768]{1,0:T(8,128)(2,1)}, bf16[512,768]{1,0:T(8,128)(2,1)}, u32[]{:S(2)}, u32[]{:S(2)}) collective-permute-start(bf16[512,768]{1,0:T(8,128)(2,1)} %get-tuple-element.32), channel_id=1, source_target_pairs={{0,6},{2,0},{4,2},{6,4},{1,7},{3,1},{5,3},{7,5},{8,14},{10,8},{12,... | collective-permute-start | bytes 2359304 | tf_op jit(solution)/shard_map/ppermute | solution.py:351
  191.4 0.8 aux.1
  192.3 26.5 %all-to-all-done.1 = bf16[64,48,128]{2,1,0:T(8,128)(2,1)S(1)} async-done(((bf16[64,48,128]{2,1,0:T(8,128)(2,1)}), bf16[64,48,128]{2,1,0:T(8,128)(2,1)S(1)}, u32[]{:S(2)}, u32[]{:S(2)}) %all-to-all-start.1) | async-done | bytes 786464 | tf_op jit(solution)/shard_map/all_to_all | solution.py:133
  218.7 0.9 combine.1
  219.7 5.4 %collective-permute-start.5 = (bf16[128,1024]{1,0:T(8,128)(2,1)S(1)}, bf16[128,1024]{1,0:T(8,128)(2,1)S(1)}, u32[]{:S(2)}, u32[]{:S(2)}) collective-permute-start(bf16[128,1024]{1,0:T(8,128)(2,1)S(1)} %combine.1), channel_id=1, source_target_pairs={{0,1},{1,0},{2,3},{3,2},{4,5},{5,4},{6,7},{7,6},{8,9},{9,8},{10,11... | collective-permute-start | bytes 786440 | tf_op jit(solution)/shard_map/ppermute | solution.py:392
  225.1 0.0 collective-permute-done.6
  225.1 0.0 collective-permute-done.7
  225.1 0.0 collective-permute-done.8
  225.1 2.0 add_convert_fusion
  227.2 1.0 slice_bitcast_fusion
  228.1 0.0 collective-permute-done.5
  228.1 0.9 maximum_select_fusion
  (10 shorter events, 0.1 us)
Async XLA Ops:
  0.7 1.2 copy-start
  1.9 0.9 copy-start.1
  2.9 1.0 copy-start.5
  3.9 0.7 copy-start.6
  4.6 0.7 copy-start.7
  8.4 19.2 %copy-start.8 = (bf16[1,512,384]{2,1,0:T(8,128)(2,1)S(1)}, bf16[1,512,384]{2,1,0:T(8,128)(2,1)}, u32[]{:S(2)}) copy-start(bf16[1,512,384]{2,1,0:T(8,128)(2,1)} %param.13) | copy-start | bytes 1179652
  8.4 87.3 %copy-start.9 = (bf16[1,512,384]{2,1,0:T(8,128)(2,1)S(1)}, bf16[1,512,384]{2,1,0:T(8,128)(2,1)}, u32[]{:S(2)}) copy-start(bf16[1,512,384]{2,1,0:T(8,128)(2,1)} %param.14) | copy-start | bytes 1179652
  8.4 79.7 %all-to-all-start = ((bf16[64,80,128]{2,1,0:T(8,128)(2,1)}), bf16[64,80,128]{2,1,0:T(8,128)(2,1)S(1)}, u32[]{:S(2)}, u32[]{:S(2)}) async-start(bf16[64,80,128]{2,1,0:T(8,128)(2,1)} %bitcast.5), calls=%async_computation | async-start | bytes 2621440 | tf_op jit(solution)/shard_map/all_to_all | solution.py:133
  88.1 73.8 %collective-permute-start = (bf16[5120,128]{1,0:T(8,128)(2,1)S(1)}, bf16[5120,128]{1,0:T(8,128)(2,1)S(1)}, u32[]{:S(2)}, u32[]{:S(2)}) collective-permute-start(bf16[5120,128]{1,0:T(8,128)(2,1)S(1)} %bitcast.13), channel_id=1, source_target_pairs={{0,1},{1,0},{2,3},{3,2},{4,5},{5,4},{6,7},{7,6},{8,9},{9,8},{10,11... | collective-permute-start | bytes 3932168 | tf_op jit(solution)/shard_map/ppermute | solution.py:189
  96.8 55.1 %collective-permute-start.1 = (bf16[3,512,384]{2,1,0:T(8,128)(2,1)S(1)}, bf16[3,512,384]{2,1,0:T(8,128)(2,1)S(1)}, u32[]{:S(2)}, u32[]{:S(2)}) collective-permute-start(bf16[3,512,384]{2,1,0:T(8,128)(2,1)S(1)} %constant_dynamic-update-slice_fusion.refs_0_), channel_id=1, source_target_pairs={{0,6},{2,0},{4,2},{6,4},{1,7},{3,1},{5,3},{7,5},{8,14},{10,8},{12,... | collective-permute-start | bytes 3538952 | tf_op jit(solution)/shard_map/ppermute | solution.py:170
  101.5 50.4 %collective-permute-start.2 = (bf16[3,512,384]{2,1,0:T(8,128)(2,1)S(1)}, bf16[3,512,384]{2,1,0:T(8,128)(2,1)S(1)}, u32[]{:S(2)}, u32[]{:S(2)}) collective-permute-start(bf16[3,512,384]{2,1,0:T(8,128)(2,1)S(1)} %constant_dynamic-update-slice_fusion.refs_0_), channel_id=1, source_target_pairs={{0,4},{2,6},{4,0},{6,2},{1,5},{3,7},{5,1},{7,3},{8,12},{10,14},{12... | collective-permute-start | bytes 3538952 | tf_op jit(solution)/shard_map/ppermute | solution.py:170
  103.7 54.3 %collective-permute-start.3 = (bf16[3,512,384]{2,1,0:T(8,128)(2,1)S(1)}, bf16[3,512,384]{2,1,0:T(8,128)(2,1)S(1)}, u32[]{:S(2)}, u32[]{:S(2)}) collective-permute-start(bf16[3,512,384]{2,1,0:T(8,128)(2,1)S(1)} %constant_dynamic-update-slice_fusion.refs_0_), channel_id=1, source_target_pairs={{0,2},{2,4},{4,6},{6,0},{1,3},{3,5},{5,7},{7,1},{8,10},{10,12},{12... | collective-permute-start | bytes 3538952 | tf_op jit(solution)/shard_map/ppermute | solution.py:170
  165.8 4.0 %copy-start.3 = (bf16[320,1024]{1,0:T(8,128)(2,1)}, bf16[320,1024]{1,0:T(8,128)(2,1)S(1)}, u32[]{:S(2)}) copy-start(bf16[320,1024]{1,0:T(8,128)(2,1)S(1)} %get-tuple-element.28.oth_ref) | copy-start | bytes 1966084
  165.8 4.2 %collective-permute-start.4 = (bf16[320,1152]{1,0:T(8,128)(2,1)S(1)}, bf16[320,1152]{1,0:T(8,128)(2,1)S(1)}, u32[]{:S(2)}, u32[]{:S(2)}) collective-permute-start(bf16[320,1152]{1,0:T(8,128)(2,1)S(1)} %get-tuple-element.22), channel_id=1, source_target_pairs={{0,1},{1,0},{2,3},{3,2},{4,5},{5,4},{6,7},{7,6},{8,9},{9,8},{10,11... | collective-permute-start | bytes 2211848 | tf_op jit(solution)/shard_map/ppermute | solution.py:281
  171.8 19.6 %copy-start.2 = (bf16[2048,64]{0,1:T(8,128)(2,1)S(1)}, bf16[2048,64]{0,1:T(8,128)(2,1)}, u32[]{:S(2)}) copy-start(bf16[2048,64]{0,1:T(8,128)(2,1)} %param.12) | copy-start | bytes 786436
  171.8 46.9 %all-to-all-start.1 = ((bf16[64,48,128]{2,1,0:T(8,128)(2,1)}), bf16[64,48,128]{2,1,0:T(8,128)(2,1)S(1)}, u32[]{:S(2)}, u32[]{:S(2)}) async-start(bf16[64,48,128]{2,1,0:T(8,128)(2,1)} %bitcast.7), calls=%async_computation.1 | async-start | bytes 1572864 | tf_op jit(solution)/shard_map/all_to_all | solution.py:133
  178.5 1.1 copy-start.4
  183.0 42.1 %collective-permute-start.6 = (bf16[512,768]{1,0:T(8,128)(2,1)}, bf16[512,768]{1,0:T(8,128)(2,1)}, u32[]{:S(2)}, u32[]{:S(2)}) collective-permute-start(bf16[512,768]{1,0:T(8,128)(2,1)} %get-tuple-element.30), channel_id=1, source_target_pairs={{0,2},{2,4},{4,6},{6,0},{1,3},{3,5},{5,7},{7,1},{8,10},{10,12},{12... | collective-permute-start | bytes 2359304 | tf_op jit(solution)/shard_map/ppermute | solution.py:351
  184.9 40.2 %collective-permute-start.7 = (bf16[512,768]{1,0:T(8,128)(2,1)}, bf16[512,768]{1,0:T(8,128)(2,1)}, u32[]{:S(2)}, u32[]{:S(2)}) collective-permute-start(bf16[512,768]{1,0:T(8,128)(2,1)} %get-tuple-element.31), channel_id=1, source_target_pairs={{0,4},{2,6},{4,0},{6,2},{1,5},{3,7},{5,1},{7,3},{8,12},{10,14},{12... | collective-permute-start | bytes 2359304 | tf_op jit(solution)/shard_map/ppermute | solution.py:351
  188.3 36.8 %collective-permute-start.8 = (bf16[512,768]{1,0:T(8,128)(2,1)}, bf16[512,768]{1,0:T(8,128)(2,1)}, u32[]{:S(2)}, u32[]{:S(2)}) collective-permute-start(bf16[512,768]{1,0:T(8,128)(2,1)} %get-tuple-element.32), channel_id=1, source_target_pairs={{0,6},{2,0},{4,2},{6,4},{1,7},{3,1},{5,3},{7,5},{8,14},{10,8},{12,... | collective-permute-start | bytes 2359304 | tf_op jit(solution)/shard_map/ppermute | solution.py:351
  219.7 8.5 %collective-permute-start.5 = (bf16[128,1024]{1,0:T(8,128)(2,1)S(1)}, bf16[128,1024]{1,0:T(8,128)(2,1)S(1)}, u32[]{:S(2)}, u32[]{:S(2)}) collective-permute-start(bf16[128,1024]{1,0:T(8,128)(2,1)S(1)} %combine.1), channel_id=1, source_target_pairs={{0,1},{1,0},{2,3},{3,2},{4,5},{5,4},{6,7},{7,6},{8,9},{9,8},{10,11... | collective-permute-start | bytes 786440 | tf_op jit(solution)/shard_map/ppermute | solution.py:392

commit v2 on v1

--- a/solution.py
+++ b/solution.py
@@ -16,6 +16,10 @@
     return pltpu.with_memory_space_constraint(x, pltpu.VMEM)
 
 
+def hb(x):
+    return pltpu.with_memory_space_constraint(x, pltpu.HBM)
+
+
 def vspec():
     return pl.BlockSpec(memory_space=pltpu.VMEM)
 
@@ -24,8 +28,12 @@
     return pl.BlockSpec(memory_space=pl.ANY)
 
 
-def sspec():
-    return pl.BlockSpec(memory_space=pltpu.SMEM)
+def pair_id():
+    return lax.axis_index("pair").astype(jnp.int32)
+
+
+def dp_id():
+    return lax.axis_index("dp").astype(jnp.int32)
 
 
 def params():
@@ -61,19 +69,27 @@
     shard, fh = gate_weight.shape[1], gate_weight.shape[2]
     dps = width // shard
     disp = cap * 2 * hc
-    back = cap * hc + 8
-
-    pair = lax.axis_index("pair").astype(jnp.int32)
-    dp = lax.axis_index("dp").astype(jnp.int32)
-    idx = jnp.stack([pair, dp])
+    back = cap * hc + 2
+    part = shard // 2
 
     def dispatch_kernel(
-        idx_ref, bytes_ref, pos_ref, picks_ref, cot_ref, router_ref, out_ref, meta_ref, bnd, scr
+        bytes_hbm, pos_hbm, picks_hbm, cot_hbm, router_hbm, out_ref, meta_ref,
+        bytes_ref, pos_ref, picks_ref, cot_ref, router_ref, bnd, scr, sems,
     ):
-        off = pl.multiple_of(idx_ref[0] * half, half)
+        off = pl.multiple_of(pair_id() * half, half)
+        loads = [
+            pltpu.make_async_copy(pos_hbm, pos_ref, sems.at[0]),
+            pltpu.make_async_copy(picks_hbm, picks_ref, sems.at[1]),
+            pltpu.make_async_copy(bytes_hbm, bytes_ref, sems.at[2]),
+            pltpu.make_async_copy(router_hbm, router_ref, sems.at[3]),
+            pltpu.make_async_copy(cot_hbm.at[:, pl.ds(off, half)], cot_ref, sems.at[4]),
+        ]
+        for load in loads:
+            load.start()
+        loads[0].wait()
+        loads[1].wait()
         pos = jnp.bitwise_and(pos_ref[...], byte_count - 1)
         pos_hot = jnp.where(iota((byte_count, rows), 0) == pos, 1.0, 0.0).astype(BF16)
-        bnd[...] = dot_tn(pos_hot, bytes_ref[...]).astype(BF16)
         p0 = picks_ref[0:1, :]
         p1 = picks_ref[1:2, :]
         ids = iota((experts, rows), 0)
@@ -85,6 +101,9 @@
         rank1 = jnp.sum(hot1 * counts, axis=0, keepdims=True)
         target0 = rank0 * experts + p0.astype(F32)
         target1 = rank1 * experts + p1.astype(F32)
+        loads[2].wait()
+        bnd[...] = dot_tn(pos_hot, bytes_ref[...]).astype(BF16)
+        loads[3].wait()
         logits = dot_nt(router_ref[...], bnd[...])
         l0 = jnp.sum(hot0 * logits, axis=0, keepdims=True)
         l1 = jnp.sum(hot1 * logits, axis=0, keepdims=True)
@@ -97,7 +116,8 @@
         sel1 = slot_ids == target1
         take = (jnp.where(sel0, 1.0, 0.0) + jnp.where(sel1, 1.0, 0.0)).astype(BF16)
         take_mix = (jnp.where(sel0, low0, 0.0) + jnp.where(sel1, low1, 0.0)).astype(BF16)
-        send = (dot(take, bnd[:, pl.ds(off, half)]), dot(take_mix, cot_ref[:, pl.ds(off, half)]))
+        loads[4].wait()
+        send = (dot(take, bnd[:, pl.ds(off, half)]), dot(take_mix, cot_ref[...]))
         for s in range(cap):
             for t in range(2):
                 for c in range(hc):
@@ -115,29 +135,39 @@
             jax.ShapeDtypeStruct((experts * disp, LANE), BF16),
             pltpu.VMEM((8, rows), F32),
         ),
-        in_specs=[sspec()] + [vspec()] * 5,
+        in_specs=[aspec()] * 5,
         out_specs=(vspec(), vspec()),
-        scratch_shapes=[pltpu.VMEM((rows, width), BF16), pltpu.VMEM((experts * disp, LANE), F32)],
+        scratch_shapes=[
+            pltpu.VMEM((byte_count, width), BF16),
+            pltpu.VMEM((1, rows), jnp.int32),
+            pltpu.VMEM((2, rows), jnp.int32),
+            pltpu.VMEM((rows, half), BF16),
+            pltpu.VMEM((experts, width), BF16),
+            pltpu.VMEM((rows, width), BF16),
+            pltpu.VMEM((experts * disp, LANE), F32),
+            pltpu.SemaphoreType.DMA((5,)),
+        ],
         compiler_params=params(),
         name="dispatch",
     )(
-        idx,
-        byte_states,
-        positions.reshape(1, rows),
-        picks.T,
-        cotangent,
-        router_weight.T,
+        hb(byte_states),
+        hb(positions.reshape(1, rows)),
+        hb(picks.T),
+        hb(cotangent),
+        hb(router_weight.T),
     )
 
-    def exchange(x, count):
-        return lax.all_to_all(
-            x.reshape(experts, count, LANE), "expert", split_axis=0, concat_axis=0, tiled=True
-        ).reshape(experts * count, LANE)
-
-    recv = exchange(payload, disp)
-
-    def aux_kernel(idx_ref, meta_ref, router_ref, hot_ref, delta_ref, mix_ref):
-        off = pl.multiple_of(idx_ref[0] * half, half)
+    def exchange(x, count, sub):
+        shape = x.shape
+        x = x.reshape((experts, count // sub) + shape[1:])
+        return lax.all_to_all(x, "expert", split_axis=0, concat_axis=0, tiled=True).reshape(shape)
+
+    recv = exchange(payload, disp, 1)
+
+    def aux_kernel(
+        meta_ref, router_ref, hot_hbm, delta_hbm, mix_hbm, hot_ref, delta_ref, mix_ref, sems
+    ):
+        off = pl.multiple_of(pair_id() * half, half)
         slot_ids = iota((3 * LANE, rows), 0).astype(F32)
         for k in range(2):
             hot = jnp.where(slot_ids == meta_ref[k : k + 1, :], 1.0, 0.0)
@@ -150,40 +180,95 @@
         delta_ref[...] = dot(diff, router_ref[:, pl.ds(off, half)])
         cols = jnp.concatenate([meta_ref[...], jnp.zeros((LANE - 8, rows), F32)], axis=0)
         mix_ref[...] = cols.T
+        copies = [
+            pltpu.make_async_copy(hot_ref, hot_hbm, sems.at[0]),
+            pltpu.make_async_copy(delta_ref, delta_hbm, sems.at[1]),
+            pltpu.make_async_copy(mix_ref, mix_hbm, sems.at[2]),
+        ]
+        for copy in copies:
+            copy.start()
+        for copy in copies:
+            copy.wait()
 
     hots, delta, mix_cols = pl.pallas_call(
         aux_kernel,
         out_shape=(
-            jax.ShapeDtypeStruct((2 * rows, 3 * LANE), BF16),
-            jax.ShapeDtypeStruct((rows, half), F32),
-            jax.ShapeDtypeStruct((rows, LANE), F32),
+            pltpu.HBM((2 * rows, 3 * LANE), BF16),
+            pltpu.HBM((rows, half), F32),
+            pltpu.HBM((rows, LANE), F32),
         ),
-        in_specs=[sspec()] + [vspec()] * 2,
-        out_specs=(vspec(),) * 3,
+        in_specs=[vspec()] * 2,
+        out_specs=(aspec(),) * 3,
+        scratch_shapes=[
+            pltpu.VMEM((2 * rows, 3 * LANE), BF16),
+            pltpu.VMEM((rows, half), F32),
+            pltpu.VMEM((rows, LANE), F32),
+            pltpu.SemaphoreType.DMA((3,)),
+        ],
         compiler_params=params(),
         name="aux",
-    )(idx, vm(meta), router_weight.T)
-
-    weights = jnp.stack([gate_weight[0], up_weight[0], down_weight[0]])
-    pieces = [weights]
-    for k in range(1, dps):
-        pieces.append(lax.ppermute(weights, "dp", [(i, (i - k) % dps) for i in range(dps)]))
-
-    def assemble_kernel(idx_ref, *refs):
-        out_ref = refs[dps]
-        y = idx_ref[1]
+    )(vm(meta), router_weight.T)
+
+    def stack_kernel(gate_hbm, up_hbm, down_hbm, low_ref, high_ref, sems):
+        copies = []
+        for i, src in enumerate((gate_hbm, up_hbm, down_hbm)):
+            for j, dst in enumerate((low_ref, high_ref)):
+                copies.append(
+                    pltpu.make_async_copy(
+                        src.at[0, pl.ds(j * part, part), :], dst.at[i], sems.at[2 * i + j]
+                    )
+                )
+        for copy in copies:
+            copy.start()
+        for copy in copies:
+            copy.wait()
+
+    low, high = pl.pallas_call(
+        stack_kernel,
+        out_shape=(pltpu.VMEM((3, part, fh), BF16),) * 2,
+        in_specs=[aspec()] * 3,
+        out_specs=(vspec(),) * 2,
+        scratch_shapes=[pltpu.SemaphoreType.DMA((6,))],
+        compiler_params=params(),
+        name="stack",
+    )(hb(gate_weight), hb(up_weight), hb(down_weight))
+
+    ahead = [(i, (i + 1) % dps) for i in range(dps)]
+    behind = [(i, (i - 1) % dps) for i in range(dps)]
+    low_prev = lax.ppermute(low, "dp", ahead)
+    high_next = lax.ppermute(high, "dp", behind)
+    high_prev = lax.ppermute(high, "dp", ahead)
+    low_next = lax.ppermute(low, "dp", behind)
+    low_far = lax.ppermute(low_prev, "dp", ahead)
+    high_far = lax.ppermute(high_next, "dp", behind)
+    pieces = (low, high, low_next, high_next, low_far, high_far, low_prev, high_prev)
+
+    def assemble_kernel(*refs):
+        out_hbm, sems = refs[2 * dps :]
+        y = dp_id()
+        copies = []
         for k in range(dps):
-            row = pl.multiple_of(((y + k) % dps) * shard, shard)
-            out_ref[:, pl.ds(row, shard), :] = refs[k][...]
+            for j in range(2):
+                row = pl.multiple_of(((y + k) % dps) * shard + j * part, part)
+                copies.append(
+                    pltpu.make_async_copy(
+                        refs[2 * k + j], out_hbm.at[:, pl.ds(row, part), :], sems.at[2 * k + j]
+                    )
+                )
+        for copy in copies:
+            copy.start()
+        for copy in copies:
+            copy.wait()
 
     full = pl.pallas_call(
         assemble_kernel,
-        out_shape=jax.ShapeDtypeStruct((3, width, fh), BF16),
-        in_specs=[sspec()] + [vspec()] * dps,
-        out_specs=vspec(),
+        out_shape=pltpu.HBM((3, width, fh), BF16),
+        in_specs=[vspec()] * (2 * dps),
+        out_specs=aspec(),
+        scratch_shapes=[pltpu.SemaphoreType.DMA((2 * dps,))],
         compiler_params=params(),
         name="assemble",
-    )(idx, *[vm(x) for x in pieces])
+    )(*[vm(x) for x in pieces])
 
     swap = [(0, 1), (1, 0)]
     recv_other = lax.ppermute(recv, "pair", swap)
@@ -202,8 +287,8 @@
         row = pl.multiple_of(h * half, half)
         return pltpu.make_async_copy(w_hbm.at[pl.ds(0, count), pl.ds(row, half), :], w_buf, sem)
 
-    def own_kernel(idx_ref, recv_ref, w_hbm, x_ref, pre_ref, wide, s_buf, w_buf, sem):
-        load = fetch(w_hbm, w_buf, sem, idx_ref[0], 3)
+    def own_kernel(recv_ref, w_hbm, x_ref, pre_ref, wide, s_buf, w_buf, sem):
+        load = fetch(w_hbm, w_buf, sem, pair_id(), 3)
         load.start()
         unpack(recv_ref, wide, x_ref, s_buf)
         load.wait()
@@ -217,7 +302,7 @@
             pltpu.VMEM((slots, half), BF16),
             pltpu.VMEM((3, slots, fh), F32),
         ),
-        in_specs=[sspec(), vspec(), aspec()],
+        in_specs=[vspec(), aspec()],
         out_specs=(vspec(),) * 2,
         scratch_shapes=[
             pltpu.VMEM((experts * disp, LANE), F32),
@@ -227,12 +312,12 @@
         ],
         compiler_params=params(),
         name="own",
-    )(idx, vm(recv), full)
+    )(vm(recv), hb(full))
 
     def grads_kernel(
-        idx_ref, recv_ref, w_hbm, pre_ref, x_ref, joined_ref, send_ref, mixed_ref, wide, s_buf, w_buf, sem
+        recv_ref, w_hbm, pre_ref, x_ref, joined_ref, send_ref, mixed_ref, wide, s_buf, w_buf, sem
     ):
-        load = fetch(w_hbm, w_buf, sem, 1 - idx_ref[0], 3)
+        load = fetch(w_hbm, w_buf, sem, 1 - pair_id(), 3)
         load.start()
         unpack(recv_ref, wide, x_ref, s_buf)
         load.wait()
@@ -266,7 +351,7 @@
             pltpu.VMEM((slots, half + LANE), BF16),
             pltpu.VMEM((slots, LANE), F32),
         ),
-        in_specs=[sspec(), vspec(), aspec(), vspec()],
+        in_specs=[vspec(), aspec(), vspec()],
         out_specs=(vspec(),) * 4,
         scratch_shapes=[
             pltpu.VMEM((experts * disp, LANE), F32),
@@ -276,12 +361,12 @@
         ],
         compiler_params=params(),
         name="grads",
-    )(idx, vm(recv_other), full, vm(pre))
+    )(vm(recv_other), hb(full), vm(pre))
 
     sent = lax.ppermute(send, "pair", swap)
 
-    def keep_kernel(idx_ref, joined_ref, w_hbm, keep_ref, w_buf, sem):
-        load = fetch(w_hbm, w_buf, sem, idx_ref[0], 2)
+    def keep_kernel(joined_ref, w_hbm, keep_ref, w_buf, sem):
+        load = fetch(w_hbm, w_buf, sem, pair_id(), 2)
         load.start()
         load.wait()
         keep_ref[...] = dot_nt(joined_ref[:, :fh], w_buf[0]) + dot_nt(joined_ref[:, fh:], w_buf[1])
@@ -289,18 +374,18 @@
     keep = pl.pallas_call(
         keep_kernel,
         out_shape=pltpu.VMEM((slots, half), F32),
-        in_specs=[sspec(), vspec(), aspec()],
+        in_specs=[vspec(), aspec()],
         out_specs=vspec(),
         scratch_shapes=[pltpu.VMEM((2, half, fh), BF16), pltpu.SemaphoreType.DMA(())],
         compiler_params=params(),
         name="keep",
-    )(idx, vm(joined), full)
-
-    def weight_kernel(idx_ref, own_ref, oth_ref, joined_ref, *refs):
+    )(vm(joined), hb(full))
+
+    def weight_kernel(own_ref, oth_ref, joined_ref, *refs):
         outs = refs[:dps]
         x_all = refs[dps]
-        p = idx_ref[0]
-        y = idx_ref[1]
+        p = pair_id()
+        y = dp_id()
         x_all[:, pl.ds(pl.multiple_of(p * half, half), half)] = own_ref[...]
         x_all[:, pl.ds(pl.multiple_of((1 - p) * half, half), half)] = oth_ref[...]
         for k in range(dps):
@@ -310,12 +395,12 @@
     sums = pl.pallas_call(
         weight_kernel,
         out_shape=(pltpu.VMEM((shard, 2 * fh), BF16),) * dps,
-        in_specs=[sspec()] + [vspec()] * 3,
+        in_specs=[vspec()] * 3,
         out_specs=(vspec(),) * dps,
         scratch_shapes=[pltpu.VMEM((slots, width), BF16)],
         compiler_params=params(),
         name="weight",
-    )(idx, vm(x_own), vm(x_other), vm(joined))
+    )(vm(x_own), vm(x_other), vm(joined))
 
     def pack_kernel(keep_ref, mixed_ref, sent_ref, out_ref, scr):
         for c in range(hc):
@@ -326,17 +411,21 @@
                     s * experts : (s + 1) * experts
                 ]
         tail = sent_ref[:, half:].astype(F32)
-        full = mixed_ref[...] + tail + pltpu.roll(tail, LANE // 2, 1)
-        high = full.astype(BF16).astype(F32)
-        both = jnp.where(iota((slots, LANE), 1) < LANE // 2, high, full - high)
-        for s in range(8):
-            part = both[s * experts : (s + 1) * experts] if s < cap else jnp.zeros((experts, LANE), F32)
-            scr[pl.ds(cap * hc + s, experts, stride=back), :] = part
-        out_ref[...] = scr[...].astype(BF16)
+        full_mixed = mixed_ref[...] + tail + pltpu.roll(tail, LANE // 2, 1)
+        high_mixed = full_mixed.astype(BF16).astype(F32)
+        lane = iota((experts, LANE), 1)
+        line = jnp.zeros((experts, LANE), F32)
+        for s in range(cap):
+            span = slice(s * experts, (s + 1) * experts)
+            line = jnp.where(lane == s, high_mixed[span], line)
+            line = jnp.where(lane == LANE // 2 + s, full_mixed[span] - high_mixed[span], line)
+        scr[pl.ds(cap * hc, experts, stride=back), :] = line
+        scr[pl.ds(cap * hc + 1, experts, stride=back), :] = jnp.zeros((experts, LANE), F32)
+        out_ref[...] = scr[...].reshape(experts * back // 2, 2, LANE).astype(BF16)
 
     packed = pl.pallas_call(
         pack_kernel,
-        out_shape=jax.ShapeDtypeStruct((experts * back, LANE), BF16),
+        out_shape=jax.ShapeDtypeStruct((experts * back // 2, 2, LANE), BF16),
         in_specs=[vspec()] * 3,
         out_specs=vspec(),
         scratch_shapes=[pltpu.VMEM((experts * back, LANE), F32)],
@@ -344,57 +433,103 @@
         name="pack",
     )(vm(keep), vm(mixed), vm(sent))
 
-    returned = exchange(packed, back)
+    returned = exchange(packed, back, 2)
 
     moved = [sums[0]]
     for k in range(1, dps):
         moved.append(lax.ppermute(sums[k], "dp", [(i, (i + k) % dps) for i in range(dps)]))
-    weight_sum = moved[0].astype(F32)
-    for piece in moved[1:]:
-        weight_sum = weight_sum + piece.astype(F32)
-    weight_sum = weight_sum.astype(BF16)
-    gate_out = weight_sum[:, :fh][None]
-    up_out = weight_sum[:, fh:][None]
-
-    def combine_kernel(back_ref, hot_ref, delta_ref, mix_ref, out_ref, wide, grads, small):
-        wide[...] = back_ref[...].astype(F32)
+
+    def total_kernel(*refs):
+        gate_ref, up_ref = refs[dps:]
+        total = refs[0][...].astype(F32)
+        for ref in refs[1:dps]:
+            total = total + ref[...].astype(F32)
+        total = total.astype(BF16)
+        gate_ref[0] = total[:, :fh]
+        up_ref[0] = total[:, fh:]
+
+    gate_out, up_out = pl.pallas_call(
+        total_kernel,
+        out_shape=(jax.ShapeDtypeStruct((1, shard, fh), BF16),) * 2,
+        in_specs=[vspec()] * dps,
+        out_specs=(vspec(),) * 2,
+        compiler_params=params(),
+        name="total",
+    )(*[vm(x) for x in moved])
+
+    def combine_kernel(
+        back_ref, hot_hbm, delta_hbm, mix_hbm, out_ref,
+        wide, grads, small, hot_ref, delta_ref, mix_ref, sems,
+    ):
+        loads = [
+            pltpu.make_async_copy(hot_hbm, hot_ref, sems.at[0]),
+            pltpu.make_async_copy(mix_hbm, mix_ref, sems.at[1]),
+            pltpu.make_async_copy(delta_hbm, delta_ref, sems.at[2]),
+        ]
+        for load in loads:
+            load.start()
+        wide[...] = back_ref[...].astype(F32).reshape(experts * back, LANE)
+        lane = jnp.bitwise_and(iota((experts, LANE), 1), LANE // 2 - 1)
+        line = wide[pl.ds(cap * hc, experts, stride=back), :]
         for s in range(cap):
             span = slice(s * experts, (s + 1) * experts)
             for c in range(hc):
                 val = wide[pl.ds(s * hc + c, experts, stride=back), :]
                 grads[span, c * LANE : (c + 1) * LANE] = val.astype(BF16)
-            small[span, :] = wide[pl.ds(cap * hc + s, experts, stride=back), :].astype(BF16)
+            small[span, :] = jnp.where(lane == s, line, 0.0).astype(BF16)
         grads[slots:, :] = jnp.zeros((3 * LANE - slots, half), BF16)
         small[slots:, :] = jnp.zeros((3 * LANE - slots, LANE), BF16)
+        for load in loads:
+            load.wait()
         hot0 = hot_ref[:rows, :]
         hot1 = hot_ref[rows:, :]
-        u0 = dot(hot0, small[...])
-        u1 = dot(hot1, small[...])
-        u0 = u0[:, 0:1] + u0[:, LANE // 2 : LANE // 2 + 1]
-        u1 = u1[:, 0:1] + u1[:, LANE // 2 : LANE // 2 + 1]
+        u0 = jnp.sum(dot(hot0, small[...]), axis=1, keepdims=True)
+        u1 = jnp.sum(dot(hot1, small[...]), axis=1, keepdims=True)
         logit = mix_ref[:, 3:4] * u0 - mix_ref[:, 2:3] * u1
         out_ref[...] = (dot(hot0 + hot1, grads[...]) + logit * delta_ref[...]).astype(BF16)
 
     row_half = pl.pallas_call(
         combine_kernel,
-        out_shape=jax.ShapeDtypeStruct((rows, half), BF16),
-        in_specs=[vspec()] * 4,
+        out_shape=pltpu.VMEM((rows, half), BF16),
+        in_specs=[vspec()] + [aspec()] * 3,
         out_specs=vspec(),
         scratch_shapes=[
             pltpu.VMEM((experts * back, LANE), F32),
             pltpu.VMEM((3 * LANE, half), BF16),
             pltpu.VMEM((3 * LANE, LANE), BF16),
+            pltpu.VMEM((2 * rows, 3 * LANE), BF16),
+            pltpu.VMEM((rows, half), F32),
+            pltpu.VMEM((rows, LANE), F32),
+            pltpu.SemaphoreType.DMA((3,)),
         ],
         compiler_params=params(),
         name="combine",
-    )(vm(returned), hots, delta, mix_cols)
+    )(vm(returned), hb(hots), hb(delta), hb(mix_cols))
 
     row_half_other = lax.ppermute(row_half, "pair", swap)
-    row_grad = jnp.where(
-        pair == 0,
-        jnp.concatenate([row_half, row_half_other], axis=1),
-        jnp.concatenate([row_half_other, row_half], axis=1),
-    )
+
+    def join_kernel(own_ref, oth_ref, out_hbm, sems):
+        p = pair_id()
+        copies = [
+            pltpu.make_async_copy(
+                src, out_hbm.at[:, pl.ds(pl.multiple_of(h * half, half), half)], sems.at[i]
+            )
+            for i, (src, h) in enumerate(((own_ref, p), (oth_ref, 1 - p)))
+        ]
+        for copy in copies:
+            copy.start()
+        for copy in copies:
+            copy.wait()
+
+    row_grad = pl.pallas_call(
+        join_kernel,
+        out_shape=jax.ShapeDtypeStruct((rows, width), BF16),
+        in_specs=[vspec()] * 2,
+        out_specs=aspec(),
+        scratch_shapes=[pltpu.SemaphoreType.DMA((2,))],
+        compiler_params=params(),
+        name="join",
+    )(vm(row_half), vm(row_half_other))
     return (row_grad, gate_out, up_out)
 
 

time: 230 us -> 207 us (0.900)
  waiting for transfers between devices: 139 us -> 49.4 us
  blocking collectives: 0 us -> 79.4 us
  starting transfers between devices: 59.2 us -> 50.2 us
  local copies, waits for them, and re-layouts: 7.77 us -> 0.01 us
  Pallas kernels: 19.3 us -> 26.5 us
  other arithmetic: 3.05 us -> 0 us
    all_to_all x0 -> x1, blocking collectives: none -> 79.4 us  [exchange(): lax.all_to_all(x, 'expert', split_axis=0, concat_axis=0, tiled=True)]
    all_to_all x2 -> x1, waiting for transfers between devices: 86.9 us -> 22.8 us  [exchange(): lax.all_to_all(x, 'expert', split_axis=0, concat_axis=0, tiled=True)]
    ppermute x3 -> x6, waiting for transfers between devices: 51.7 us -> 26.6 us  [the longest x1 11 us: local(): low_far = lax.ppermute(low_prev, 'dp', ahead)]
    all_to_all x2 -> x1, starting transfers between devices: 25.9 us -> 6.72 us  [exchange(): lax.all_to_all(x, 'expert', split_axis=0, concat_axis=0, tiled=True)]
    ppermute x3 -> x6, starting transfers between devices: 9.51 us -> 18.3 us  [the longest x1 4.57 us: local(): high_far = lax.ppermute(high_next, 'dp', behind)]
    pallas_call x3 -> x6, Pallas kernels: 2.71 us -> 9.76 us  [the longest x1 2.51 us: local(): pl.pallas_call(total_kernel, out_shape=(jax.ShapeDtypeStruct((1, shard, f...]
    unnamed x22 -> x2, local copies, waits for them, and re-layouts: 5.75 us -> 0.01 us
  transfers between devices with their start and end apart: 11 -> 13, of which waited for: 5 -> 5; matrix products, arithmetic and copies ran while one was open for 2% -> 0% of each run, Pallas kernels for 5% -> 8%
where the time goes in v2:
time: 207 us
  blocking collectives  79.4 us (38%)
  starting transfers between devices  50.2 us (24%)
  waiting for transfers between devices  49.4 us (24%)
  Pallas kernels  26.5 us (13%)
    all_to_all x1, blocking collectives, exchange(): lax.all_to_all(x, 'expert', split_axis=0, concat_axis=0, tiled=True)  79.4 us
    all_to_all x1, waiting for transfers between devices, exchange(): lax.all_to_all(x, 'expert', split_axis=0, concat_axis=0, tiled=True)  22.8 us
    ppermute x1, waiting for transfers between devices, local(): low_far = lax.ppermute(low_prev, 'dp', ahead)  11 us
    ppermute x3, starting transfers between devices, local(): lax.ppermute(sums[k], 'dp', [(i, (i + k) % dps) for i in range(dps)])  9.72 us
    ppermute x1, waiting for transfers between devices, local(): low_next = lax.ppermute(low, 'dp', behind)  7.73 us
    ppermute x1, starting transfers between devices, local(): recv_other = lax.ppermute(recv, 'pair', swap)  7.53 us
    all_to_all x1, starting transfers between devices, exchange(): lax.all_to_all(x, 'expert', split_axis=0, concat_axis=0, tiled=True)  6.72 us
    ppermute x1, waiting for transfers between devices, local(): low_prev = lax.ppermute(low, 'dp', ahead)  6.23 us
  transfers between devices with their start and end apart: 13, of which 5 were waited for; matrix products, arithmetic and copies ran while one was open for 0% of the time, Pallas kernels for 8%

profile of v2, /device:TPU:1, one launch (start us, length us, event | category | flops | bytes accessed | tf_op | source)
XLA Modules:
  0.0 206.5 jit_solution(15336157859950676897)
XLA Ops:
  0.6 3.2 %dispatch.1 = (bf16[5120,128]{1,0:T(8,128)(2,1)S(1)}, f32[8,128]{1,0:T(8,128)S(1)}) custom-call(bf16[256,2048]{1,0:T(8,128)(2,1)} %bytes_hbm.1, s32[1,128]{1,0:T(1,128)} %bitcast.14, s32[2,128]{1,0:T(2,128)} %bitcast.13, bf16[128,2048]{1,0:T(8,128)(2,1)} %cot_hbm.1, bf16[64,2048]{1,0:T(8,128)(2,1)} %bitcast.11), custom_call_target="tpu_custom_call" | custom-call | tf_op jit(solution)/shard_map/dispatch/pallas_call | solution.py:132
  3.8 79.4 %all_to_all.10 = bf16[64,80,128]{2,1,0:T(8,128)(2,1)S(1)} all-to-all(bf16[64,80,128]{2,1,0:T(8,128)(2,1)S(1)} %bitcast.10), channel_id=1, replica_groups=mesh['expert'=64,'dp'=4,'pair'=2] {'expert'}, dimensions={0} | all-to-all | bytes 2621440 | tf_op jit(solution)/shard_map/all_to_all | solution.py:163
  83.2 7.5 %collective-permute-start = (bf16[5120,128]{1,0:T(8,128)(2,1)S(1)}, bf16[5120,128]{1,0:T(8,128)(2,1)S(1)}, u32[]{:S(2)}, u32[]{:S(2)}) collective-permute-start(bf16[5120,128]{1,0:T(8,128)(2,1)S(1)} %bitcast.7), channel_id=1, source_target_pairs={{0,1},{1,0},{2,3},{3,2},{4,5},{5,4},{6,7},{7,6},{8,9},{9,8},{10,11... | collective-permute-start | bytes 3932168 | tf_op jit(solution)/shard_map/ppermute | solution.py:274
  90.8 1.4 stack.1
  92.2 3.2 %collective-permute-start.3 = (bf16[3,256,384]{2,1,0:T(8,128)(2,1)S(1)}, bf16[3,256,384]{2,1,0:T(8,128)(2,1)S(1)}, u32[]{:S(2)}, u32[]{:S(2)}) collective-permute-start(bf16[3,256,384]{2,1,0:T(8,128)(2,1)S(1)} %get-tuple-element.23.refs_0_), channel_id=1, source_target_pairs={{0,2},{2,4},{4,6},{6,0},{1,3},{3,5},{5,7},{7,1},{8,10},{10,12},{12... | collective-permute-start | bytes 1769480 | tf_op jit(solution)/shard_map/ppermute | solution.py:238
  95.4 3.3 %collective-permute-start.2 = (bf16[3,256,384]{2,1,0:T(8,128)(2,1)S(1)}, bf16[3,256,384]{2,1,0:T(8,128)(2,1)S(1)}, u32[]{:S(2)}, u32[]{:S(2)}) collective-permute-start(bf16[3,256,384]{2,1,0:T(8,128)(2,1)S(1)} %get-tuple-element.24.refs_1_), channel_id=1, source_target_pairs={{0,6},{2,0},{4,2},{6,4},{1,7},{3,1},{5,3},{7,5},{8,14},{10,8},{12,... | collective-permute-start | bytes 1769480 | tf_op jit(solution)/shard_map/ppermute | solution.py:239
  98.7 3.4 %collective-permute-start.1 = (bf16[3,256,384]{2,1,0:T(8,128)(2,1)S(1)}, bf16[3,256,384]{2,1,0:T(8,128)(2,1)S(1)}, u32[]{:S(2)}, u32[]{:S(2)}) collective-permute-start(bf16[3,256,384]{2,1,0:T(8,128)(2,1)S(1)} %get-tuple-element.23.refs_0_), channel_id=1, source_target_pairs={{0,6},{2,0},{4,2},{6,4},{1,7},{3,1},{5,3},{7,5},{8,14},{10,8},{12,... | collective-permute-start | bytes 1769480 | tf_op jit(solution)/shard_map/ppermute | solution.py:241
  102.1 1.9 collective-permute-start.6
  104.0 6.2 %collective-permute-done.3.refs_6_ = bf16[3,256,384]{2,1,0:T(8,128)(2,1)S(1)} collective-permute-done((bf16[3,256,384]{2,1,0:T(8,128)(2,1)S(1)}, bf16[3,256,384]{2,1,0:T(8,128)(2,1)S(1)}, u32[]{:S(2)}, u32[]{:S(2)}) %collective-permute-start.3) | collective-permute-done | bytes 589856 | tf_op jit(solution)/shard_map/ppermute | solution.py:238
  110.3 1.9 collective-permute-start.4
  112.2 0.0 collective-permute-done.2.refs_3_
  112.2 4.6 %collective-permute-start.5 = (bf16[3,256,384]{2,1,0:T(8,128)(2,1)S(1)}, bf16[3,256,384]{2,1,0:T(8,128)(2,1)S(1)}, u32[]{:S(2)}, u32[]{:S(2)}) collective-permute-start(bf16[3,256,384]{2,1,0:T(8,128)(2,1)S(1)} %collective-permute-done.2.refs_3_), channel_id=1, source_target_pairs={{0,6},{2,0},{4,2},{6,4},{1,7},{3,1},{5,3},{7,5},{8,14},{10,8},{12,... | collective-permute-start | bytes 1769480 | tf_op jit(solution)/shard_map/ppermute | solution.py:243
  116.8 7.7 %collective-permute-done.1.refs_2_ = bf16[3,256,384]{2,1,0:T(8,128)(2,1)S(1)} collective-permute-done((bf16[3,256,384]{2,1,0:T(8,128)(2,1)S(1)}, bf16[3,256,384]{2,1,0:T(8,128)(2,1)S(1)}, u32[]{:S(2)}, u32[]{:S(2)}) %collective-permute-start.1) | collective-permute-done | bytes 589856 | tf_op jit(solution)/shard_map/ppermute | solution.py:241
  124.5 0.0 collective-permute-done.6.refs_7_
  124.5 11.0 %collective-permute-done.4.refs_4_ = bf16[3,256,384]{2,1,0:T(8,128)(2,1)S(1)} collective-permute-done((bf16[3,256,384]{2,1,0:T(8,128)(2,1)S(1)}, bf16[3,256,384]{2,1,0:T(8,128)(2,1)S(1)}, u32[]{:S(2)}, u32[]{:S(2)}) %collective-permute-start.4) | collective-permute-done | bytes 589856 | tf_op jit(solution)/shard_map/ppermute | solution.py:242
  135.5 1.6 collective-permute-done.5.refs_5_
  137.1 2.3 %assemble.1.w_hbm = bf16[3,2048,384]{2,1,0:T(8,128)(2,1)} custom-call(bf16[3,256,384]{2,1,0:T(8,128)(2,1)S(1)} %get-tuple-element.23.refs_0_, bf16[3,256,384]{2,1,0:T(8,128)(2,1)S(1)} %get-tuple-element.24.refs_1_, bf16[3,256,384]{2,1,0:T(8,128)(2,1)S(1)} %collective-permute-done.1.refs_2_, bf16[3,256,384]{2,1,0:T(8,128)(2,1)S(1)} %collective-permute-done.2.refs_3_, ...), custom_call_target="tpu_custom_call" | custom-call | tf_op jit(solution)/shard_map/assemble/pallas_call | solution.py:263
  139.4 2.9 %own.1 = (bf16[320,1024]{1,0:T(8,128)(2,1)S(1)}, f32[3,320,384]{2,1,0:T(8,128)S(1)}) custom-call(bf16[5120,128]{1,0:T(8,128)(2,1)S(1)} %bitcast.8, bf16[3,2048,384]{2,1,0:T(8,128)(2,1)} %assemble.1.w_hbm), custom_call_target="tpu_custom_call" | custom-call | tf_op jit(solution)/shard_map/own/pallas_call | solution.py:299
  142.3 0.0 collective-permute-done.recv_ref
  142.3 3.7 %grads.1 = (bf16[320,1024]{1,0:T(8,128)(2,1)S(1)}, bf16[320,768]{1,0:T(8,128)(2,1)S(1)}, bf16[320,1152]{1,0:T(8,128)(2,1)S(1)}, f32[320,128]{1,0:T(8,128)S(1)}) custom-call(bf16[5120,128]{1,0:T(8,128)(2,1)S(1)} %collective-permute-done.recv_ref, bf16[3,2048,384]{2,1,0:T(8,128)(2,1)} %assemble.1.w_hbm, f32[3,320,384]{2,1,0:T(8,128)S(1)} %get-tuple-element.25.pre_ref), custom_call_target="tpu_custom_call" | custom-call | tf_op jit(solution)/shard_map/grads/pallas_call | solution.py:346
  146.1 3.1 %collective-permute-start.7 = (bf16[320,1152]{1,0:T(8,128)(2,1)S(1)}, bf16[320,1152]{1,0:T(8,128)(2,1)S(1)}, u32[]{:S(2)}, u32[]{:S(2)}) collective-permute-start(bf16[320,1152]{1,0:T(8,128)(2,1)S(1)} %get-tuple-element.28), channel_id=1, source_target_pairs={{0,1},{1,0},{2,3},{3,2},{4,5},{5,4},{6,7},{7,6},{8,9},{9,8},{10,11... | collective-permute-start | bytes 2211848 | tf_op jit(solution)/shard_map/ppermute | solution.py:366
  149.1 2.3 %keep.1.keep_ref = f32[320,1024]{1,0:T(8,128)S(1)} custom-call(bf16[320,768]{1,0:T(8,128)(2,1)S(1)} %get-tuple-element.26.joined_ref, bf16[3,2048,384]{2,1,0:T(8,128)(2,1)} %assemble.1.w_hbm), custom_call_target="tpu_custom_call" | custom-call | tf_op jit(solution)/shard_map/keep/pallas_call | solution.py:374
  151.4 0.0 collective-permute-done.7.sent_ref
  151.4 1.8 pack.1
  153.2 0.0 copy-start
  153.2 6.7 %all-to-all-start.1 = ((bf16[64,21,2,128]{3,2,1,0:T(2,128)(2,1)}), bf16[64,21,2,128]{3,2,1,0:T(2,128)(2,1)S(1)}, u32[]{:S(2)}, u32[]{:S(2)}) async-start(bf16[64,21,2,128]{3,2,1,0:T(2,128)(2,1)} %bitcast.5), calls=%async_computation.1 | async-start | bytes 1376256 | tf_op jit(solution)/shard_map/all_to_all | solution.py:163
  160.0 2.8 %weight.1 = (bf16[512,768]{1,0:T(8,128)(2,1)S(1)}, bf16[512,768]{1,0:T(8,128)(2,1)}, bf16[512,768]{1,0:T(8,128)(2,1)}, bf16[512,768]{1,0:T(8,128)(2,1)}) custom-call(bf16[320,1024]{1,0:T(8,128)(2,1)S(1)} %get-tuple-element.33.own_ref, bf16[320,1024]{1,0:T(8,128)(2,1)S(1)} %get-tuple-element.34.oth_ref, bf16[320,768]{1,0:T(8,128)(2,1)S(1)} %get-tuple-element.26.joined_ref), custom_call_target="tpu_custom_call" | custom-call | tf_op jit(solution)/shard_map/weight/pallas_call | solution.py:395
  162.8 4.4 %collective-permute-start.10 = (bf16[512,768]{1,0:T(8,128)(2,1)}, bf16[512,768]{1,0:T(8,128)(2,1)S(1)}, u32[]{:S(2)}, u32[]{:S(2)}) collective-permute-start(bf16[512,768]{1,0:T(8,128)(2,1)} %get-tuple-element.37), channel_id=1, source_target_pairs={{0,4},{2,6},{4,0},{6,2},{1,5},{3,7},{5,1},{7,3},{8,12},{10,14},{12... | collective-permute-start | bytes 2359304 | tf_op jit(solution)/shard_map/ppermute | solution.py:440
  167.3 3.0 %collective-permute-start.11 = (bf16[512,768]{1,0:T(8,128)(2,1)}, bf16[512,768]{1,0:T(8,128)(2,1)}, u32[]{:S(2)}, u32[]{:S(2)}) collective-permute-start(bf16[512,768]{1,0:T(8,128)(2,1)} %get-tuple-element.38), channel_id=1, source_target_pairs={{0,6},{2,0},{4,2},{6,4},{1,7},{3,1},{5,3},{7,5},{8,14},{10,8},{12,... | collective-permute-start | bytes 2359304 | tf_op jit(solution)/shard_map/ppermute | solution.py:440
  170.2 2.3 %collective-permute-start.9 = (bf16[512,768]{1,0:T(8,128)(2,1)}, bf16[512,768]{1,0:T(8,128)(2,1)}, u32[]{:S(2)}, u32[]{:S(2)}) collective-permute-start(bf16[512,768]{1,0:T(8,128)(2,1)} %get-tuple-element.36), channel_id=1, source_target_pairs={{0,2},{2,4},{4,6},{6,0},{1,3},{3,5},{5,7},{7,1},{8,10},{10,12},{12... | collective-permute-start | bytes 2359304 | tf_op jit(solution)/shard_map/ppermute | solution.py:440
  172.6 0.0 copy-done
  172.6 1.1 aux.1
  173.7 22.8 %all-to-all-done.1 = bf16[64,21,2,128]{3,2,1,0:T(2,128)(2,1)S(1)} async-done(((bf16[64,21,2,128]{3,2,1,0:T(2,128)(2,1)}), bf16[64,21,2,128]{3,2,1,0:T(2,128)(2,1)S(1)}, u32[]{:S(2)}, u32[]{:S(2)}) %all-to-all-start.1) | async-done | bytes 688160 | tf_op jit(solution)/shard_map/all_to_all | solution.py:163
  196.5 1.7 combine.1.own_ref
  198.2 4.8 %collective-permute-start.8 = (bf16[128,1024]{1,0:T(8,128)(2,1)S(1)}, bf16[128,1024]{1,0:T(8,128)(2,1)S(1)}, u32[]{:S(2)}, u32[]{:S(2)}) collective-permute-start(bf16[128,1024]{1,0:T(8,128)(2,1)S(1)} %combine.1.own_ref), channel_id=1, source_target_pairs={{0,1},{1,0},{2,3},{3,2},{4,5},{5,4},{6,7},{7,6},{8,9},{9,8},{10,11... | collective-permute-start | bytes 786440 | tf_op jit(solution)/shard_map/ppermute | solution.py:509
  203.0 0.0 collective-permute-done.10.refs_2_
  203.0 0.0 collective-permute-done.11.refs_3_
  203.0 0.0 collective-permute-done.9.refs_1_
  203.1 2.5 %total.1 = (bf16[1,512,384]{2,1,0:T(8,128)(2,1)}, bf16[1,512,384]{2,1,0:T(8,128)(2,1)}) custom-call(bf16[512,768]{1,0:T(8,128)(2,1)S(1)} %get-tuple-element.35.refs_0_, bf16[512,768]{1,0:T(8,128)(2,1)} %collective-permute-done.9.refs_1_, bf16[512,768]{1,0:T(8,128)(2,1)S(1)} %collective-permute-done.10.refs_2_, bf16[512,768]{1,0:T(8,128)(2,1)} %collective-permute-done.11.refs_3_), custom_call_target="tpu_custom_call" | custom-call | tf_op jit(solution)/shard_map/total/pallas_call | solution.py:451
  205.6 0.0 collective-permute-done.8.oth_ref
  205.6 0.8 join.1
Async XLA Ops:
  83.2 59.1 %collective-permute-start = (bf16[5120,128]{1,0:T(8,128)(2,1)S(1)}, bf16[5120,128]{1,0:T(8,128)(2,1)S(1)}, u32[]{:S(2)}, u32[]{:S(2)}) collective-permute-start(bf16[5120,128]{1,0:T(8,128)(2,1)S(1)} %bitcast.7), channel_id=1, source_target_pairs={{0,1},{1,0},{2,3},{3,2},{4,5},{5,4},{6,7},{7,6},{8,9},{9,8},{10,11... | collective-permute-start | bytes 3932168 | tf_op jit(solution)/shard_map/ppermute | solution.py:274
  92.2 18.1 %collective-permute-start.3 = (bf16[3,256,384]{2,1,0:T(8,128)(2,1)S(1)}, bf16[3,256,384]{2,1,0:T(8,128)(2,1)S(1)}, u32[]{:S(2)}, u32[]{:S(2)}) collective-permute-start(bf16[3,256,384]{2,1,0:T(8,128)(2,1)S(1)} %get-tuple-element.23.refs_0_), channel_id=1, source_target_pairs={{0,2},{2,4},{4,6},{6,0},{1,3},{3,5},{5,7},{7,1},{8,10},{10,12},{12... | collective-permute-start | bytes 1769480 | tf_op jit(solution)/shard_map/ppermute | solution.py:238
  95.4 16.8 %collective-permute-start.2 = (bf16[3,256,384]{2,1,0:T(8,128)(2,1)S(1)}, bf16[3,256,384]{2,1,0:T(8,128)(2,1)S(1)}, u32[]{:S(2)}, u32[]{:S(2)}) collective-permute-start(bf16[3,256,384]{2,1,0:T(8,128)(2,1)S(1)} %get-tuple-element.24.refs_1_), channel_id=1, source_target_pairs={{0,6},{2,0},{4,2},{6,4},{1,7},{3,1},{5,3},{7,5},{8,14},{10,8},{12,... | collective-permute-start | bytes 1769480 | tf_op jit(solution)/shard_map/ppermute | solution.py:239
  98.7 25.8 %collective-permute-start.1 = (bf16[3,256,384]{2,1,0:T(8,128)(2,1)S(1)}, bf16[3,256,384]{2,1,0:T(8,128)(2,1)S(1)}, u32[]{:S(2)}, u32[]{:S(2)}) collective-permute-start(bf16[3,256,384]{2,1,0:T(8,128)(2,1)S(1)} %get-tuple-element.23.refs_0_), channel_id=1, source_target_pairs={{0,6},{2,0},{4,2},{6,4},{1,7},{3,1},{5,3},{7,5},{8,14},{10,8},{12,... | collective-permute-start | bytes 1769480 | tf_op jit(solution)/shard_map/ppermute | solution.py:241
  102.1 22.4 %collective-permute-start.6 = (bf16[3,256,384]{2,1,0:T(8,128)(2,1)S(1)}, bf16[3,256,384]{2,1,0:T(8,128)(2,1)S(1)}, u32[]{:S(2)}, u32[]{:S(2)}) collective-permute-start(bf16[3,256,384]{2,1,0:T(8,128)(2,1)S(1)} %get-tuple-element.24.refs_1_), channel_id=1, source_target_pairs={{0,2},{2,4},{4,6},{6,0},{1,3},{3,5},{5,7},{7,1},{8,10},{10,12},{12... | collective-permute-start | bytes 1769480 | tf_op jit(solution)/shard_map/ppermute | solution.py:240
  110.3 25.3 %collective-permute-start.4 = (bf16[3,256,384]{2,1,0:T(8,128)(2,1)S(1)}, bf16[3,256,384]{2,1,0:T(8,128)(2,1)S(1)}, u32[]{:S(2)}, u32[]{:S(2)}) collective-permute-start(bf16[3,256,384]{2,1,0:T(8,128)(2,1)S(1)} %collective-permute-done.3.refs_6_), channel_id=1, source_target_pairs={{0,2},{2,4},{4,6},{6,0},{1,3},{3,5},{5,7},{7,1},{8,10},{10,12},{12... | collective-permute-start | bytes 1769480 | tf_op jit(solution)/shard_map/ppermute | solution.py:242
  112.2 24.9 %collective-permute-start.5 = (bf16[3,256,384]{2,1,0:T(8,128)(2,1)S(1)}, bf16[3,256,384]{2,1,0:T(8,128)(2,1)S(1)}, u32[]{:S(2)}, u32[]{:S(2)}) collective-permute-start(bf16[3,256,384]{2,1,0:T(8,128)(2,1)S(1)} %collective-permute-done.2.refs_3_), channel_id=1, source_target_pairs={{0,6},{2,0},{4,2},{6,4},{1,7},{3,1},{5,3},{7,5},{8,14},{10,8},{12,... | collective-permute-start | bytes 1769480 | tf_op jit(solution)/shard_map/ppermute | solution.py:243
  146.1 5.4 %collective-permute-start.7 = (bf16[320,1152]{1,0:T(8,128)(2,1)S(1)}, bf16[320,1152]{1,0:T(8,128)(2,1)S(1)}, u32[]{:S(2)}, u32[]{:S(2)}) collective-permute-start(bf16[320,1152]{1,0:T(8,128)(2,1)S(1)} %get-tuple-element.28), channel_id=1, source_target_pairs={{0,1},{1,0},{2,3},{3,2},{4,5},{5,4},{6,7},{7,6},{8,9},{9,8},{10,11... | collective-permute-start | bytes 2211848 | tf_op jit(solution)/shard_map/ppermute | solution.py:366
  153.2 19.3 %copy-start = (bf16[2048,64]{0,1:T(8,128)(2,1)S(1)}, bf16[2048,64]{0,1:T(8,128)(2,1)}, u32[]{:S(2)}) copy-start(bf16[2048,64]{0,1:T(8,128)(2,1)} %param.12) | copy-start | bytes 786436
  153.2 43.3 %all-to-all-start.1 = ((bf16[64,21,2,128]{3,2,1,0:T(2,128)(2,1)}), bf16[64,21,2,128]{3,2,1,0:T(2,128)(2,1)S(1)}, u32[]{:S(2)}, u32[]{:S(2)}) async-start(bf16[64,21,2,128]{3,2,1,0:T(2,128)(2,1)} %bitcast.5), calls=%async_computation.1 | async-start | bytes 1376256 | tf_op jit(solution)/shard_map/all_to_all | solution.py:163
  162.8 40.2 %collective-permute-start.10 = (bf16[512,768]{1,0:T(8,128)(2,1)}, bf16[512,768]{1,0:T(8,128)(2,1)S(1)}, u32[]{:S(2)}, u32[]{:S(2)}) collective-permute-start(bf16[512,768]{1,0:T(8,128)(2,1)} %get-tuple-element.37), channel_id=1, source_target_pairs={{0,4},{2,6},{4,0},{6,2},{1,5},{3,7},{5,1},{7,3},{8,12},{10,14},{12... | collective-permute-start | bytes 2359304 | tf_op jit(solution)/shard_map/ppermute | solution.py:440
  167.3 35.8 %collective-permute-start.11 = (bf16[512,768]{1,0:T(8,128)(2,1)}, bf16[512,768]{1,0:T(8,128)(2,1)}, u32[]{:S(2)}, u32[]{:S(2)}) collective-permute-start(bf16[512,768]{1,0:T(8,128)(2,1)} %get-tuple-element.38), channel_id=1, source_target_pairs={{0,6},{2,0},{4,2},{6,4},{1,7},{3,1},{5,3},{7,5},{8,14},{10,8},{12,... | collective-permute-start | bytes 2359304 | tf_op jit(solution)/shard_map/ppermute | solution.py:440
  170.2 32.8 %collective-permute-start.9 = (bf16[512,768]{1,0:T(8,128)(2,1)}, bf16[512,768]{1,0:T(8,128)(2,1)}, u32[]{:S(2)}, u32[]{:S(2)}) collective-permute-start(bf16[512,768]{1,0:T(8,128)(2,1)} %get-tuple-element.36), channel_id=1, source_target_pairs={{0,2},{2,4},{4,6},{6,0},{1,3},{3,5},{5,7},{7,1},{8,10},{10,12},{12... | collective-permute-start | bytes 2359304 | tf_op jit(solution)/shard_map/ppermute | solution.py:440
  198.2 7.4 %collective-permute-start.8 = (bf16[128,1024]{1,0:T(8,128)(2,1)S(1)}, bf16[128,1024]{1,0:T(8,128)(2,1)S(1)}, u32[]{:S(2)}, u32[]{:S(2)}) collective-permute-start(bf16[128,1024]{1,0:T(8,128)(2,1)S(1)} %combine.1.own_ref), channel_id=1, source_target_pairs={{0,1},{1,0},{2,3},{3,2},{4,5},{5,4},{6,7},{7,6},{8,9},{9,8},{10,11... | collective-permute-start | bytes 786440 | tf_op jit(solution)/shard_map/ppermute | solution.py:509

commit v3 on v2

--- a/solution.py
+++ b/solution.py
@@ -73,8 +73,8 @@
     part = shard // 2
 
     def dispatch_kernel(
-        bytes_hbm, pos_hbm, picks_hbm, cot_hbm, router_hbm, out_ref, meta_ref,
-        bytes_ref, pos_ref, picks_ref, cot_ref, router_ref, bnd, scr, sems,
+        bytes_hbm, pos_hbm, picks_hbm, cot_hbm, router_hbm, out_hbm, meta_ref,
+        bytes_ref, pos_ref, picks_ref, cot_ref, router_ref, bnd, scr, buf, sems,
     ):
         off = pl.multiple_of(pair_id() * half, half)
         loads = [
@@ -101,8 +101,27 @@
         rank1 = jnp.sum(hot1 * counts, axis=0, keepdims=True)
         target0 = rank0 * experts + p0.astype(F32)
         target1 = rank1 * experts + p1.astype(F32)
+        slot_ids = iota((slots, rows), 0).astype(F32)
+        sel0 = slot_ids == target0
+        sel1 = slot_ids == target1
+
+        def emit(t, send):
+            for s in range(cap):
+                for c in range(hc):
+                    scr[t, pl.ds(s * hc + c, experts, stride=cap * hc), :] = send[
+                        s * experts : (s + 1) * experts, c * LANE : (c + 1) * LANE
+                    ]
+            buf[t] = scr[t].astype(BF16).reshape(experts, cap * hc, LANE)
+            store = pltpu.make_async_copy(
+                buf.at[t], out_hbm.at[:, pl.ds(t * cap * hc, cap * hc), :], sems.at[5 + t]
+            )
+            store.start()
+            return store
+
         loads[2].wait()
         bnd[...] = dot_tn(pos_hot, bytes_ref[...]).astype(BF16)
+        take = (jnp.where(sel0, 1.0, 0.0) + jnp.where(sel1, 1.0, 0.0)).astype(BF16)
+        stores = [emit(0, dot(take, bnd[:, pl.ds(off, half)]))]
         loads[3].wait()
         logits = dot_nt(router_ref[...], bnd[...])
         l0 = jnp.sum(hot0 * logits, axis=0, keepdims=True)
@@ -111,32 +130,23 @@
         mix1 = 1.0 - mix0
         low0 = mix0.astype(BF16).astype(F32)
         low1 = mix1.astype(BF16).astype(F32)
-        slot_ids = iota((slots, rows), 0).astype(F32)
-        sel0 = slot_ids == target0
-        sel1 = slot_ids == target1
-        take = (jnp.where(sel0, 1.0, 0.0) + jnp.where(sel1, 1.0, 0.0)).astype(BF16)
         take_mix = (jnp.where(sel0, low0, 0.0) + jnp.where(sel1, low1, 0.0)).astype(BF16)
         loads[4].wait()
-        send = (dot(take, bnd[:, pl.ds(off, half)]), dot(take_mix, cot_ref[...]))
-        for s in range(cap):
-            for t in range(2):
-                for c in range(hc):
-                    scr[pl.ds((s * 2 + t) * hc + c, experts, stride=disp), :] = send[t][
-                        s * experts : (s + 1) * experts, c * LANE : (c + 1) * LANE
-                    ]
-        out_ref[...] = scr[...].astype(BF16)
+        stores.append(emit(1, dot(take_mix, cot_ref[...])))
         meta_ref[...] = jnp.concatenate(
             [target0, target1, mix0, mix1, p0.astype(F32), p1.astype(F32), mix0, mix1], axis=0
         )
+        for store in stores:
+            store.wait()
 
     payload, meta = pl.pallas_call(
         dispatch_kernel,
         out_shape=(
-            jax.ShapeDtypeStruct((experts * disp, LANE), BF16),
+            pltpu.HBM((experts, disp, LANE), BF16),
             pltpu.VMEM((8, rows), F32),
         ),
         in_specs=[aspec()] * 5,
-        out_specs=(vspec(), vspec()),
+        out_specs=(aspec(), vspec()),
         scratch_shapes=[
             pltpu.VMEM((byte_count, width), BF16),
             pltpu.VMEM((1, rows), jnp.int32),
@@ -144,8 +154,9 @@
             pltpu.VMEM((rows, half), BF16),
             pltpu.VMEM((experts, width), BF16),
             pltpu.VMEM((rows, width), BF16),
-            pltpu.VMEM((experts * disp, LANE), F32),
-            pltpu.SemaphoreType.DMA((5,)),
+            pltpu.VMEM((2, experts * cap * hc, LANE), F32),
+            pltpu.VMEM((2, experts, cap * hc, LANE), BF16),
+            pltpu.SemaphoreType.DMA((7,)),
         ],
         compiler_params=params(),
         name="dispatch",
@@ -157,12 +168,10 @@
         hb(router_weight.T),
     )
 
-    def exchange(x, count, sub):
-        shape = x.shape
-        x = x.reshape((experts, count // sub) + shape[1:])
-        return lax.all_to_all(x, "expert", split_axis=0, concat_axis=0, tiled=True).reshape(shape)
-
-    recv = exchange(payload, disp, 1)
+    def exchange(x):
+        return lax.all_to_all(x, "expert", split_axis=0, concat_axis=0, tiled=True)
+
+    recv = exchange(payload).reshape(experts * disp, LANE)
 
     def aux_kernel(
         meta_ref, router_ref, hot_hbm, delta_hbm, mix_hbm, hot_ref, delta_ref, mix_ref, sems
@@ -278,7 +287,7 @@
         for s in range(cap):
             for t, dst in ((0, x_dst), (1, s_dst)):
                 for c in range(hc):
-                    val = wide[pl.ds((s * 2 + t) * hc + c, experts, stride=disp), :]
+                    val = wide[pl.ds((t * cap + s) * hc + c, experts, stride=disp), :]
                     dst[s * experts : (s + 1) * experts, c * LANE : (c + 1) * LANE] = val.astype(
                         BF16
                     )
@@ -287,7 +296,7 @@
         row = pl.multiple_of(h * half, half)
         return pltpu.make_async_copy(w_hbm.at[pl.ds(0, count), pl.ds(row, half), :], w_buf, sem)
 
-    def own_kernel(recv_ref, w_hbm, x_ref, pre_ref, wide, s_buf, w_buf, sem):
+    def own_kernel(recv_ref, w_hbm, x_ref, pre_ref, w_buf, wide, s_buf, sem):
         load = fetch(w_hbm, w_buf, sem, pair_id(), 3)
         load.start()
         unpack(recv_ref, wide, x_ref, s_buf)
@@ -296,18 +305,18 @@
         pre_ref[1] = dot(x_ref[...], w_buf[1])
         pre_ref[2] = dot(s_buf[...], w_buf[2])
 
-    x_own, pre = pl.pallas_call(
+    x_own, pre, w_own = pl.pallas_call(
         own_kernel,
         out_shape=(
             pltpu.VMEM((slots, half), BF16),
             pltpu.VMEM((3, slots, fh), F32),
+            pltpu.VMEM((3, half, fh), BF16),
         ),
         in_specs=[vspec(), aspec()],
-        out_specs=(vspec(),) * 2,
+        out_specs=(vspec(),) * 3,
         scratch_shapes=[
             pltpu.VMEM((experts * disp, LANE), F32),
             pltpu.VMEM((slots, half), BF16),
-            pltpu.VMEM((3, half, fh), BF16),
             pltpu.SemaphoreType.DMA(()),
         ],
         compiler_params=params(),
@@ -365,42 +374,65 @@
 
     sent = lax.ppermute(send, "pair", swap)
 
-    def keep_kernel(joined_ref, w_hbm, keep_ref, w_buf, sem):
-        load = fetch(w_hbm, w_buf, sem, pair_id(), 2)
-        load.start()
-        load.wait()
-        keep_ref[...] = dot_nt(joined_ref[:, :fh], w_buf[0]) + dot_nt(joined_ref[:, fh:], w_buf[1])
+    def keep_kernel(joined_ref, w_ref, keep_ref):
+        keep_ref[...] = dot_nt(joined_ref[:, :fh], w_ref[0]) + dot_nt(joined_ref[:, fh:], w_ref[1])
 
     keep = pl.pallas_call(
         keep_kernel,
         out_shape=pltpu.VMEM((slots, half), F32),
-        in_specs=[vspec(), aspec()],
+        in_specs=[vspec()] * 2,
         out_specs=vspec(),
-        scratch_shapes=[pltpu.VMEM((2, half, fh), BF16), pltpu.SemaphoreType.DMA(())],
         compiler_params=params(),
         name="keep",
-    )(vm(joined), hb(full))
-
-    def weight_kernel(own_ref, oth_ref, joined_ref, *refs):
-        outs = refs[:dps]
-        x_all = refs[dps]
+    )(vm(joined), vm(w_own))
+
+    def weight_kernel(own_ref, oth_ref, joined_ref, mine, next_low, next_high, far_low, far_high, prev_low, prev_high, x_all):
         p = pair_id()
         y = dp_id()
         x_all[:, pl.ds(pl.multiple_of(p * half, half), half)] = own_ref[...]
         x_all[:, pl.ds(pl.multiple_of((1 - p) * half, half), half)] = oth_ref[...]
-        for k in range(dps):
+        for k, dst in (
+            (2, (far_low, far_high)),
+            (1, (next_low, next_high)),
+            (3, (prev_low, prev_high)),
+            (0, (mine.at[:part], mine.at[part:])),
+        ):
             col = pl.multiple_of(((y + k) % dps) * shard, shard)
-            outs[k][...] = dot_tn(x_all[:, pl.ds(col, shard)], joined_ref[...]).astype(BF16)
-
-    sums = pl.pallas_call(
+            block = dot_tn(x_all[:, pl.ds(col, shard)], joined_ref[...]).astype(BF16)
+            dst[0][...] = block[:part]
+            dst[1][...] = block[part:]
+
+    mine, next_low, next_high, far_low, far_high, prev_low, prev_high = pl.pallas_call(
         weight_kernel,
-        out_shape=(pltpu.VMEM((shard, 2 * fh), BF16),) * dps,
+        out_shape=(pltpu.VMEM((shard, 2 * fh), BF16),)
+        + (pltpu.VMEM((part, 2 * fh), BF16),) * 6,
         in_specs=[vspec()] * 3,
-        out_specs=(vspec(),) * dps,
+        out_specs=(vspec(),) * 7,
         scratch_shapes=[pltpu.VMEM((slots, width), BF16)],
         compiler_params=params(),
         name="weight",
     )(vm(x_own), vm(x_other), vm(joined))
+
+    far_low = lax.ppermute(far_low, "dp", ahead)
+    far_high = lax.ppermute(far_high, "dp", behind)
+    got_high = lax.ppermute(next_high, "dp", ahead)
+    got_low = lax.ppermute(prev_low, "dp", behind)
+
+    def add_kernel(a_ref, b_ref, c_ref, d_ref, low_ref, high_ref):
+        low_ref[...] = (a_ref[...].astype(F32) + b_ref[...].astype(F32)).astype(BF16)
+        high_ref[...] = (c_ref[...].astype(F32) + d_ref[...].astype(F32)).astype(BF16)
+
+    sum_low, sum_high = pl.pallas_call(
+        add_kernel,
+        out_shape=(pltpu.VMEM((part, 2 * fh), BF16),) * 2,
+        in_specs=[vspec()] * 4,
+        out_specs=(vspec(),) * 2,
+        compiler_params=params(),
+        name="add",
+    )(vm(next_low), vm(far_low), vm(prev_high), vm(far_high))
+
+    sum_low = lax.ppermute(sum_low, "dp", ahead)
+    sum_high = lax.ppermute(sum_high, "dp", behind)
 
     def pack_kernel(keep_ref, mixed_ref, sent_ref, out_ref, scr):
         for c in range(hc):
@@ -433,29 +465,23 @@
         name="pack",
     )(vm(keep), vm(mixed), vm(sent))
 
-    returned = exchange(packed, back, 2)
-
-    moved = [sums[0]]
-    for k in range(1, dps):
-        moved.append(lax.ppermute(sums[k], "dp", [(i, (i + k) % dps) for i in range(dps)]))
-
-    def total_kernel(*refs):
-        gate_ref, up_ref = refs[dps:]
-        total = refs[0][...].astype(F32)
-        for ref in refs[1:dps]:
-            total = total + ref[...].astype(F32)
-        total = total.astype(BF16)
-        gate_ref[0] = total[:, :fh]
-        up_ref[0] = total[:, fh:]
+    returned = exchange(packed.reshape(experts, back // 2, 2, LANE)).reshape(packed.shape)
+
+    def total_kernel(mine_ref, a_ref, b_ref, c_ref, d_ref, gate_ref, up_ref):
+        for span, one, two in ((slice(0, part), a_ref, b_ref), (slice(part, shard), c_ref, d_ref)):
+            total = mine_ref[span, :].astype(F32) + one[...].astype(F32) + two[...].astype(F32)
+            total = total.astype(BF16)
+            gate_ref[0, span, :] = total[:, :fh]
+            up_ref[0, span, :] = total[:, fh:]
 
     gate_out, up_out = pl.pallas_call(
         total_kernel,
         out_shape=(jax.ShapeDtypeStruct((1, shard, fh), BF16),) * 2,
-        in_specs=[vspec()] * dps,
+        in_specs=[vspec()] * 5,
         out_specs=(vspec(),) * 2,
         compiler_params=params(),
         name="total",
-    )(*[vm(x) for x in moved])
+    )(*[vm(x) for x in (mine, sum_low, got_low, got_high, sum_high)])
 
     def combine_kernel(
         back_ref, hot_hbm, delta_hbm, mix_hbm, out_ref,

time: 207 us -> 206 us (level)
  starting transfers between devices: 50.2 us -> 60 us
  waiting for transfers between devices: 49.4 us -> 40 us
    all_to_all x1, waiting for transfers between devices: 22.8 us -> 8.08 us  [exchange(): return lax.all_to_all(x, 'expert', split_axis=0, concat_axis=0, tiled=True)]
    ppermute x3 -> x6, starting transfers between devices: 9.72 us -> 19.4 us  [the longest x1 4.57 us: local(): got_low = lax.ppermute(prev_low, 'dp', behind)]
    ppermute x3 -> x6, waiting for transfers between devices: 0.01 us -> 4.4 us  [the longest x1 4.39 us: local(): far_low = lax.ppermute(far_low, 'dp', ahead)]
    pallas_call x1 -> x2, Pallas kernels: 3.19 us -> 4.86 us  [the longest x1 3.84 us: local(): pl.pallas_call(dispatch_kernel, out_shape=(pltpu.HBM((experts, disp, LANE...]
  transfers between devices with their start and end apart: 13 -> 16, of which waited for: 5 -> 7; matrix products, arithmetic and copies ran while one was open for 0% -> 0% of each run, Pallas kernels for 8% -> 7%
where the time goes in v3:
time: 206 us; the launch traced here: 205 us
  blocking collectives  79.6 us (39%)
  starting transfers between devices  60 us (29%)
  waiting for transfers between devices  40 us (19%)
  Pallas kernels  24.8 us (12%)
    all_to_all x1, blocking collectives, exchange(): return lax.all_to_all(x, 'expert', split_axis=0, concat_axis=0, tiled=True)  79.6 us
    ppermute x1, waiting for transfers between devices, local(): low_far = lax.ppermute(low_prev, 'dp', ahead)  11.1 us
    all_to_all x1, waiting for transfers between devices, exchange(): return lax.all_to_all(x, 'expert', split_axis=0, concat_axis=0, tiled=True)  8.08 us
    ppermute x1, waiting for transfers between devices, local(): low_next = lax.ppermute(low, 'dp', behind)  7.71 us
    ppermute x1, starting transfers between devices, local(): recv_other = lax.ppermute(recv, 'pair', swap)  7.52 us
    all_to_all x1, starting transfers between devices, exchange(): return lax.all_to_all(x, 'expert', split_axis=0, concat_axis=0, tiled=True)  6.61 us
    ppermute x1, waiting for transfers between devices, local(): low_prev = lax.ppermute(low, 'dp', ahead)  6.24 us
    ppermute x1, starting transfers between devices, local(): row_half_other = lax.ppermute(row_half, 'pair', swap)  5.03 us
  transfers between devices with their start and end apart: 16, of which 7 were waited for; matrix products, arithmetic and copies ran while one was open for 0% of the time, Pallas kernels for 7%

profile of v3, /device:TPU:1, one launch (start us, length us, event | category | flops | bytes accessed | tf_op | source)
XLA Modules:
  0.0 205.4 jit_solution(13670308189751778896)
XLA Ops:
  0.6 3.8 %dispatch.1 = (bf16[64,80,128]{2,1,0:T(8,128)(2,1)}, f32[8,128]{1,0:T(8,128)S(1)}) custom-call(bf16[256,2048]{1,0:T(8,128)(2,1)} %bytes_hbm.1, s32[1,128]{1,0:T(1,128)} %bitcast.12, s32[2,128]{1,0:T(2,128)} %bitcast.11, bf16[128,2048]{1,0:T(8,128)(2,1)} %cot_hbm.1, bf16[64,2048]{1,0:T(8,128)(2,1)} %bitcast.9), custom_call_target="tpu_custom_call" | custom-call | tf_op jit(solution)/shard_map/dispatch/pallas_call | solution.py:142
  4.5 79.6 %all_to_all.10 = bf16[64,80,128]{2,1,0:T(8,128)(2,1)S(1)} all-to-all(bf16[64,80,128]{2,1,0:T(8,128)(2,1)} %get-tuple-element.28), channel_id=1, replica_groups=mesh['expert'=64,'dp'=4,'pair'=2] {'expert'}, dimensions={0} | all-to-all | bytes 2621440 | tf_op jit(solution)/shard_map/all_to_all | solution.py:172
  84.1 7.5 %collective-permute-start = (bf16[5120,128]{1,0:T(8,128)(2,1)S(1)}, bf16[5120,128]{1,0:T(8,128)(2,1)S(1)}, u32[]{:S(2)}, u32[]{:S(2)}) collective-permute-start(bf16[5120,128]{1,0:T(8,128)(2,1)S(1)} %bitcast.6), channel_id=1, source_target_pairs={{0,1},{1,0},{2,3},{3,2},{4,5},{5,4},{6,7},{7,6},{8,9},{9,8},{10,11... | collective-permute-start | bytes 3932168 | tf_op jit(solution)/shard_map/ppermute | solution.py:283
  91.6 1.4 stack.1
  93.0 3.2 %collective-permute-start.3 = (bf16[3,256,384]{2,1,0:T(8,128)(2,1)S(1)}, bf16[3,256,384]{2,1,0:T(8,128)(2,1)S(1)}, u32[]{:S(2)}, u32[]{:S(2)}) collective-permute-start(bf16[3,256,384]{2,1,0:T(8,128)(2,1)S(1)} %get-tuple-element.29.refs_0_), channel_id=1, source_target_pairs={{0,2},{2,4},{4,6},{6,0},{1,3},{3,5},{5,7},{7,1},{8,10},{10,12},{12... | collective-permute-start | bytes 1769480 | tf_op jit(solution)/shard_map/ppermute | solution.py:247
  96.2 3.4 %collective-permute-start.2 = (bf16[3,256,384]{2,1,0:T(8,128)(2,1)S(1)}, bf16[3,256,384]{2,1,0:T(8,128)(2,1)S(1)}, u32[]{:S(2)}, u32[]{:S(2)}) collective-permute-start(bf16[3,256,384]{2,1,0:T(8,128)(2,1)S(1)} %get-tuple-element.30.refs_1_), channel_id=1, source_target_pairs={{0,6},{2,0},{4,2},{6,4},{1,7},{3,1},{5,3},{7,5},{8,14},{10,8},{12,... | collective-permute-start | bytes 1769480 | tf_op jit(solution)/shard_map/ppermute | solution.py:248
  99.6 3.4 %collective-permute-start.1 = (bf16[3,256,384]{2,1,0:T(8,128)(2,1)S(1)}, bf16[3,256,384]{2,1,0:T(8,128)(2,1)S(1)}, u32[]{:S(2)}, u32[]{:S(2)}) collective-permute-start(bf16[3,256,384]{2,1,0:T(8,128)(2,1)S(1)} %get-tuple-element.29.refs_0_), channel_id=1, source_target_pairs={{0,6},{2,0},{4,2},{6,4},{1,7},{3,1},{5,3},{7,5},{8,14},{10,8},{12,... | collective-permute-start | bytes 1769480 | tf_op jit(solution)/shard_map/ppermute | solution.py:250
  103.0 1.9 collective-permute-start.6
  104.9 6.2 %collective-permute-done.3.refs_6_ = bf16[3,256,384]{2,1,0:T(8,128)(2,1)S(1)} collective-permute-done((bf16[3,256,384]{2,1,0:T(8,128)(2,1)S(1)}, bf16[3,256,384]{2,1,0:T(8,128)(2,1)S(1)}, u32[]{:S(2)}, u32[]{:S(2)}) %collective-permute-start.3) | collective-permute-done | bytes 589856 | tf_op jit(solution)/shard_map/ppermute | solution.py:247
  111.1 1.9 collective-permute-start.4
  113.0 0.0 collective-permute-done.2.refs_3_
  113.1 4.6 %collective-permute-start.5 = (bf16[3,256,384]{2,1,0:T(8,128)(2,1)S(1)}, bf16[3,256,384]{2,1,0:T(8,128)(2,1)S(1)}, u32[]{:S(2)}, u32[]{:S(2)}) collective-permute-start(bf16[3,256,384]{2,1,0:T(8,128)(2,1)S(1)} %collective-permute-done.2.refs_3_), channel_id=1, source_target_pairs={{0,6},{2,0},{4,2},{6,4},{1,7},{3,1},{5,3},{7,5},{8,14},{10,8},{12,... | collective-permute-start | bytes 1769480 | tf_op jit(solution)/shard_map/ppermute | solution.py:252
  117.6 7.7 %collective-permute-done.1.refs_2_ = bf16[3,256,384]{2,1,0:T(8,128)(2,1)S(1)} collective-permute-done((bf16[3,256,384]{2,1,0:T(8,128)(2,1)S(1)}, bf16[3,256,384]{2,1,0:T(8,128)(2,1)S(1)}, u32[]{:S(2)}, u32[]{:S(2)}) %collective-permute-start.1) | collective-permute-done | bytes 589856 | tf_op jit(solution)/shard_map/ppermute | solution.py:250
  125.3 0.0 collective-permute-done.6.refs_7_
  125.3 11.1 %collective-permute-done.4.refs_4_ = bf16[3,256,384]{2,1,0:T(8,128)(2,1)S(1)} collective-permute-done((bf16[3,256,384]{2,1,0:T(8,128)(2,1)S(1)}, bf16[3,256,384]{2,1,0:T(8,128)(2,1)S(1)}, u32[]{:S(2)}, u32[]{:S(2)}) %collective-permute-start.4) | collective-permute-done | bytes 589856 | tf_op jit(solution)/shard_map/ppermute | solution.py:251
  136.4 1.6 collective-permute-done.5.refs_5_
  138.0 2.2 %assemble.1.w_hbm = bf16[3,2048,384]{2,1,0:T(8,128)(2,1)} custom-call(bf16[3,256,384]{2,1,0:T(8,128)(2,1)S(1)} %get-tuple-element.29.refs_0_, bf16[3,256,384]{2,1,0:T(8,128)(2,1)S(1)} %get-tuple-element.30.refs_1_, bf16[3,256,384]{2,1,0:T(8,128)(2,1)S(1)} %collective-permute-done.1.refs_2_, bf16[3,256,384]{2,1,0:T(8,128)(2,1)S(1)} %collective-permute-done.2.refs_3_, ...), custom_call_target="tpu_custom_call" | custom-call | tf_op jit(solution)/shard_map/assemble/pallas_call | solution.py:272
  140.2 2.9 %own.1 = (bf16[320,1024]{1,0:T(8,128)(2,1)S(1)}, f32[3,320,384]{2,1,0:T(8,128)S(1)}, bf16[3,1024,384]{2,1,0:T(8,128)(2,1)S(1)}) custom-call(bf16[5120,128]{1,0:T(8,128)(2,1)S(1)} %bitcast.7, bf16[3,2048,384]{2,1,0:T(8,128)(2,1)} %assemble.1.w_hbm), custom_call_target="tpu_custom_call" | custom-call | tf_op jit(solution)/shard_map/own/pallas_call | solution.py:308
  143.1 0.0 collective-permute-done.recv_ref
  143.1 3.7 %grads.1 = (bf16[320,1024]{1,0:T(8,128)(2,1)S(1)}, bf16[320,768]{1,0:T(8,128)(2,1)S(1)}, bf16[320,1152]{1,0:T(8,128)(2,1)S(1)}, f32[320,128]{1,0:T(8,128)S(1)}) custom-call(bf16[5120,128]{1,0:T(8,128)(2,1)S(1)} %collective-permute-done.recv_ref, bf16[3,2048,384]{2,1,0:T(8,128)(2,1)} %assemble.1.w_hbm, f32[3,320,384]{2,1,0:T(8,128)S(1)} %get-tuple-element.31.pre_ref), custom_call_target="tpu_custom_call" | custom-call | tf_op jit(solution)/shard_map/grads/pallas_call | solution.py:355
  146.9 3.1 %collective-permute-start.7 = (bf16[320,1152]{1,0:T(8,128)(2,1)S(1)}, bf16[320,1152]{1,0:T(8,128)(2,1)S(1)}, u32[]{:S(2)}, u32[]{:S(2)}) collective-permute-start(bf16[320,1152]{1,0:T(8,128)(2,1)S(1)} %get-tuple-element.35), channel_id=1, source_target_pairs={{0,1},{1,0},{2,3},{3,2},{4,5},{5,4},{6,7},{7,6},{8,9},{9,8},{10,11... | collective-permute-start | bytes 2211848 | tf_op jit(solution)/shard_map/ppermute | solution.py:375
  149.9 0.9 keep.1.keep_ref
  150.8 0.9 collective-permute-done.7.sent_ref
  151.8 1.8 pack.1
  153.6 6.6 %all-to-all-start.1 = ((bf16[64,21,2,128]{3,2,1,0:T(2,128)(2,1)}), bf16[64,21,2,128]{3,2,1,0:T(2,128)(2,1)S(1)}, u32[]{:S(2)}, u32[]{:S(2)}) async-start(bf16[64,21,2,128]{3,2,1,0:T(2,128)(2,1)} %bitcast.4), calls=%async_computation.1 | async-start | bytes 1376256 | tf_op jit(solution)/shard_map/all_to_all | solution.py:172
  160.2 0.0 copy-start
  160.2 2.3 %weight.1 = (bf16[512,768]{1,0:T(8,128)(2,1)S(1)}, bf16[256,768]{1,0:T(8,128)(2,1)S(1)}, bf16[256,768]{1,0:T(8,128)(2,1)}, bf16[256,768]{1,0:T(8,128)(2,1)S(1)},...) custom-call(bf16[320,1024]{1,0:T(8,128)(2,1)S(1)} %get-tuple-element.40.own_ref, ...), custom_call_target="tpu_custom_call" | custom-call | tf_op jit(solution)/shard_map/weight/pallas_call | solution.py:405
  162.5 4.5 %collective-permute-start.10 = (bf16[256,768]{1,0:T(8,128)(2,1)S(1)}, bf16[256,768]{1,0:T(8,128)(2,1)S(1)}, u32[]{:S(2)}, u32[]{:S(2)}) collective-permute-start(bf16[256,768]{1,0:T(8,128)(2,1)S(1)} %get-tuple-element.46), channel_id=1, source_target_pairs={{0,6},{2,0},{4,2},{6,4},{1,7},{3,1},{5,3},{7,5},{8,14},{10,8},{12,... | collective-permute-start | bytes 1179656 | tf_op jit(solution)/shard_map/ppermute | solution.py:417
  167.1 1.9 collective-permute-start.9
  169.0 4.6 %collective-permute-start.12 = (bf16[256,768]{1,0:T(8,128)(2,1)}, bf16[256,768]{1,0:T(8,128)(2,1)S(1)}, u32[]{:S(2)}, u32[]{:S(2)}) collective-permute-start(bf16[256,768]{1,0:T(8,128)(2,1)} %get-tuple-element.48), channel_id=1, source_target_pairs={{0,6},{2,0},{4,2},{6,4},{1,7},{3,1},{5,3},{7,5},{8,14},{10,8},{12,... | collective-permute-start | bytes 1179656 | tf_op jit(solution)/shard_map/ppermute | solution.py:419
  173.6 1.9 collective-permute-start.13
  175.5 0.0 collective-permute-done.10.d_ref
  175.5 4.4 %collective-permute-done.9.b_ref = bf16[256,768]{1,0:T(8,128)(2,1)S(1)} collective-permute-done((bf16[256,768]{1,0:T(8,128)(2,1)S(1)}, bf16[256,768]{1,0:T(8,128)(2,1)S(1)}, u32[]{:S(2)}, u32[]{:S(2)}) %collective-permute-start.9) | collective-permute-done | bytes 393248 | tf_op jit(solution)/shard_map/ppermute | solution.py:416
  179.9 1.0 add.1
  180.9 1.9 collective-permute-start.11
  182.8 4.6 %collective-permute-start.14 = (bf16[256,768]{1,0:T(8,128)(2,1)}, bf16[256,768]{1,0:T(8,128)(2,1)S(1)}, u32[]{:S(2)}, u32[]{:S(2)}) collective-permute-start(bf16[256,768]{1,0:T(8,128)(2,1)} %get-tuple-element.50), channel_id=1, source_target_pairs={{0,6},{2,0},{4,2},{6,4},{1,7},{3,1},{5,3},{7,5},{8,14},{10,8},{12,... | collective-permute-start | bytes 1179656 | tf_op jit(solution)/shard_map/ppermute | solution.py:435
  187.4 0.0 copy-done
  187.4 1.1 aux.1
  188.5 8.1 %all-to-all-done.1 = bf16[64,21,2,128]{3,2,1,0:T(2,128)(2,1)S(1)} async-done(((bf16[64,21,2,128]{3,2,1,0:T(2,128)(2,1)}), bf16[64,21,2,128]{3,2,1,0:T(2,128)(2,1)S(1)}, u32[]{:S(2)}, u32[]{:S(2)}) %all-to-all-start.1) | async-done | bytes 688160 | tf_op jit(solution)/shard_map/all_to_all | solution.py:172
  196.6 1.7 combine.1.own_ref
  198.3 5.0 %collective-permute-start.8 = (bf16[128,1024]{1,0:T(8,128)(2,1)S(1)}, bf16[128,1024]{1,0:T(8,128)(2,1)S(1)}, u32[]{:S(2)}, u32[]{:S(2)}) collective-permute-start(bf16[128,1024]{1,0:T(8,128)(2,1)S(1)} %combine.1.own_ref), channel_id=1, source_target_pairs={{0,1},{1,0},{2,3},{3,2},{4,5},{5,4},{6,7},{7,6},{8,9},{9,8},{10,11... | collective-permute-start | bytes 786440 | tf_op jit(solution)/shard_map/ppermute | solution.py:535
  203.3 0.0 collective-permute-done.12.b_ref
  203.3 0.0 collective-permute-done.13.c_ref
  203.3 0.0 collective-permute-done.11.a_ref
  203.3 0.0 collective-permute-done.14.d_ref
  203.4 1.1 total.1
  204.4 0.0 collective-permute-done.8.oth_ref
  204.5 0.8 join.1
Async XLA Ops:
  84.1 59.0 %collective-permute-start = (bf16[5120,128]{1,0:T(8,128)(2,1)S(1)}, bf16[5120,128]{1,0:T(8,128)(2,1)S(1)}, u32[]{:S(2)}, u32[]{:S(2)}) collective-permute-start(bf16[5120,128]{1,0:T(8,128)(2,1)S(1)} %bitcast.6), channel_id=1, source_target_pairs={{0,1},{1,0},{2,3},{3,2},{4,5},{5,4},{6,7},{7,6},{8,9},{9,8},{10,11... | collective-permute-start | bytes 3932168 | tf_op jit(solution)/shard_map/ppermute | solution.py:283
  93.0 18.1 %collective-permute-start.3 = (bf16[3,256,384]{2,1,0:T(8,128)(2,1)S(1)}, bf16[3,256,384]{2,1,0:T(8,128)(2,1)S(1)}, u32[]{:S(2)}, u32[]{:S(2)}) collective-permute-start(bf16[3,256,384]{2,1,0:T(8,128)(2,1)S(1)} %get-tuple-element.29.refs_0_), channel_id=1, source_target_pairs={{0,2},{2,4},{4,6},{6,0},{1,3},{3,5},{5,7},{7,1},{8,10},{10,12},{12... | collective-permute-start | bytes 1769480 | tf_op jit(solution)/shard_map/ppermute | solution.py:247
  96.2 16.8 %collective-permute-start.2 = (bf16[3,256,384]{2,1,0:T(8,128)(2,1)S(1)}, bf16[3,256,384]{2,1,0:T(8,128)(2,1)S(1)}, u32[]{:S(2)}, u32[]{:S(2)}) collective-permute-start(bf16[3,256,384]{2,1,0:T(8,128)(2,1)S(1)} %get-tuple-element.30.refs_1_), channel_id=1, source_target_pairs={{0,6},{2,0},{4,2},{6,4},{1,7},{3,1},{5,3},{7,5},{8,14},{10,8},{12,... | collective-permute-start | bytes 1769480 | tf_op jit(solution)/shard_map/ppermute | solution.py:248
  99.6 25.8 %collective-permute-start.1 = (bf16[3,256,384]{2,1,0:T(8,128)(2,1)S(1)}, bf16[3,256,384]{2,1,0:T(8,128)(2,1)S(1)}, u32[]{:S(2)}, u32[]{:S(2)}) collective-permute-start(bf16[3,256,384]{2,1,0:T(8,128)(2,1)S(1)} %get-tuple-element.29.refs_0_), channel_id=1, source_target_pairs={{0,6},{2,0},{4,2},{6,4},{1,7},{3,1},{5,3},{7,5},{8,14},{10,8},{12,... | collective-permute-start | bytes 1769480 | tf_op jit(solution)/shard_map/ppermute | solution.py:250
  103.0 22.4 %collective-permute-start.6 = (bf16[3,256,384]{2,1,0:T(8,128)(2,1)S(1)}, bf16[3,256,384]{2,1,0:T(8,128)(2,1)S(1)}, u32[]{:S(2)}, u32[]{:S(2)}) collective-permute-start(bf16[3,256,384]{2,1,0:T(8,128)(2,1)S(1)} %get-tuple-element.30.refs_1_), channel_id=1, source_target_pairs={{0,2},{2,4},{4,6},{6,0},{1,3},{3,5},{5,7},{7,1},{8,10},{10,12},{12... | collective-permute-start | bytes 1769480 | tf_op jit(solution)/shard_map/ppermute | solution.py:249
  111.1 25.3 %collective-permute-start.4 = (bf16[3,256,384]{2,1,0:T(8,128)(2,1)S(1)}, bf16[3,256,384]{2,1,0:T(8,128)(2,1)S(1)}, u32[]{:S(2)}, u32[]{:S(2)}) collective-permute-start(bf16[3,256,384]{2,1,0:T(8,128)(2,1)S(1)} %collective-permute-done.3.refs_6_), channel_id=1, source_target_pairs={{0,2},{2,4},{4,6},{6,0},{1,3},{3,5},{5,7},{7,1},{8,10},{10,12},{12... | collective-permute-start | bytes 1769480 | tf_op jit(solution)/shard_map/ppermute | solution.py:251
  113.1 24.9 %collective-permute-start.5 = (bf16[3,256,384]{2,1,0:T(8,128)(2,1)S(1)}, bf16[3,256,384]{2,1,0:T(8,128)(2,1)S(1)}, u32[]{:S(2)}, u32[]{:S(2)}) collective-permute-start(bf16[3,256,384]{2,1,0:T(8,128)(2,1)S(1)} %collective-permute-done.2.refs_3_), channel_id=1, source_target_pairs={{0,6},{2,0},{4,2},{6,4},{1,7},{3,1},{5,3},{7,5},{8,14},{10,8},{12,... | collective-permute-start | bytes 1769480 | tf_op jit(solution)/shard_map/ppermute | solution.py:252
  146.9 4.9 %collective-permute-start.7 = (bf16[320,1152]{1,0:T(8,128)(2,1)S(1)}, bf16[320,1152]{1,0:T(8,128)(2,1)S(1)}, u32[]{:S(2)}, u32[]{:S(2)}) collective-permute-start(bf16[320,1152]{1,0:T(8,128)(2,1)S(1)} %get-tuple-element.35), channel_id=1, source_target_pairs={{0,1},{1,0},{2,3},{3,2},{4,5},{5,4},{6,7},{7,6},{8,9},{9,8},{10,11... | collective-permute-start | bytes 2211848 | tf_op jit(solution)/shard_map/ppermute | solution.py:375
  153.6 43.0 %all-to-all-start.1 = ((bf16[64,21,2,128]{3,2,1,0:T(2,128)(2,1)}), bf16[64,21,2,128]{3,2,1,0:T(2,128)(2,1)S(1)}, u32[]{:S(2)}, u32[]{:S(2)}) async-start(bf16[64,21,2,128]{3,2,1,0:T(2,128)(2,1)} %bitcast.4), calls=%async_computation.1 | async-start | bytes 1376256 | tf_op jit(solution)/shard_map/all_to_all | solution.py:172
  160.2 27.2 %copy-start = (bf16[2048,64]{0,1:T(8,128)(2,1)S(1)}, bf16[2048,64]{0,1:T(8,128)(2,1)}, u32[]{:S(2)}) copy-start(bf16[2048,64]{0,1:T(8,128)(2,1)} %param.12) | copy-start | bytes 786436
  162.5 13.0 %collective-permute-start.10 = (bf16[256,768]{1,0:T(8,128)(2,1)S(1)}, bf16[256,768]{1,0:T(8,128)(2,1)S(1)}, u32[]{:S(2)}, u32[]{:S(2)}) collective-permute-start(bf16[256,768]{1,0:T(8,128)(2,1)S(1)} %get-tuple-element.46), channel_id=1, source_target_pairs={{0,6},{2,0},{4,2},{6,4},{1,7},{3,1},{5,3},{7,5},{8,14},{10,8},{12,... | collective-permute-start | bytes 1179656 | tf_op jit(solution)/shard_map/ppermute | solution.py:417
  167.1 12.8 %collective-permute-start.9 = (bf16[256,768]{1,0:T(8,128)(2,1)S(1)}, bf16[256,768]{1,0:T(8,128)(2,1)S(1)}, u32[]{:S(2)}, u32[]{:S(2)}) collective-permute-start(bf16[256,768]{1,0:T(8,128)(2,1)S(1)} %get-tuple-element.44), channel_id=1, source_target_pairs={{0,2},{2,4},{4,6},{6,0},{1,3},{3,5},{5,7},{7,1},{8,10},{10,12},{12... | collective-permute-start | bytes 1179656 | tf_op jit(solution)/shard_map/ppermute | solution.py:416
  169.0 34.3 %collective-permute-start.12 = (bf16[256,768]{1,0:T(8,128)(2,1)}, bf16[256,768]{1,0:T(8,128)(2,1)S(1)}, u32[]{:S(2)}, u32[]{:S(2)}) collective-permute-start(bf16[256,768]{1,0:T(8,128)(2,1)} %get-tuple-element.48), channel_id=1, source_target_pairs={{0,6},{2,0},{4,2},{6,4},{1,7},{3,1},{5,3},{7,5},{8,14},{10,8},{12,... | collective-permute-start | bytes 1179656 | tf_op jit(solution)/shard_map/ppermute | solution.py:419
  173.6 29.8 %collective-permute-start.13 = (bf16[256,768]{1,0:T(8,128)(2,1)}, bf16[256,768]{1,0:T(8,128)(2,1)S(1)}, u32[]{:S(2)}, u32[]{:S(2)}) collective-permute-start(bf16[256,768]{1,0:T(8,128)(2,1)} %get-tuple-element.49), channel_id=1, source_target_pairs={{0,2},{2,4},{4,6},{6,0},{1,3},{3,5},{5,7},{7,1},{8,10},{10,12},{12... | collective-permute-start | bytes 1179656 | tf_op jit(solution)/shard_map/ppermute | solution.py:418
  180.9 22.4 %collective-permute-start.11 = (bf16[256,768]{1,0:T(8,128)(2,1)}, bf16[256,768]{1,0:T(8,128)(2,1)S(1)}, u32[]{:S(2)}, u32[]{:S(2)}) collective-permute-start(bf16[256,768]{1,0:T(8,128)(2,1)} %get-tuple-element.47), channel_id=1, source_target_pairs={{0,2},{2,4},{4,6},{6,0},{1,3},{3,5},{5,7},{7,1},{8,10},{10,12},{12... | collective-permute-start | bytes 1179656 | tf_op jit(solution)/shard_map/ppermute | solution.py:434
  182.8 20.5 %collective-permute-start.14 = (bf16[256,768]{1,0:T(8,128)(2,1)}, bf16[256,768]{1,0:T(8,128)(2,1)S(1)}, u32[]{:S(2)}, u32[]{:S(2)}) collective-permute-start(bf16[256,768]{1,0:T(8,128)(2,1)} %get-tuple-element.50), channel_id=1, source_target_pairs={{0,6},{2,0},{4,2},{6,4},{1,7},{3,1},{5,3},{7,5},{8,14},{10,8},{12,... | collective-permute-start | bytes 1179656 | tf_op jit(solution)/shard_map/ppermute | solution.py:435
  198.3 6.2 %collective-permute-start.8 = (bf16[128,1024]{1,0:T(8,128)(2,1)S(1)}, bf16[128,1024]{1,0:T(8,128)(2,1)S(1)}, u32[]{:S(2)}, u32[]{:S(2)}) collective-permute-start(bf16[128,1024]{1,0:T(8,128)(2,1)S(1)} %combine.1.own_ref), channel_id=1, source_target_pairs={{0,1},{1,0},{2,3},{3,2},{4,5},{5,4},{6,7},{7,6},{8,9},{9,8},{10,11... | collective-permute-start | bytes 786440 | tf_op jit(solution)/shard_map/ppermute | solution.py:535

commit v4 on v3

--- a/solution.py
+++ b/solution.py
@@ -108,10 +108,12 @@
         def emit(t, send):
             for s in range(cap):
                 for c in range(hc):
-                    scr[t, pl.ds(s * hc + c, experts, stride=cap * hc), :] = send[
+                    scr[t, pl.ds(s * hc + c, experts, stride=cap * hc + 1), :] = send[
                         s * experts : (s + 1) * experts, c * LANE : (c + 1) * LANE
                     ]
-            buf[t] = scr[t].astype(BF16).reshape(experts, cap * hc, LANE)
+            for e in range(experts):
+                row = e * (cap * hc + 1)
+                buf[t, e] = scr[t, row : row + cap * hc, :].astype(BF16)
             store = pltpu.make_async_copy(
                 buf.at[t], out_hbm.at[:, pl.ds(t * cap * hc, cap * hc), :], sems.at[5 + t]
             )
@@ -154,7 +156,7 @@
             pltpu.VMEM((rows, half), BF16),
             pltpu.VMEM((experts, width), BF16),
             pltpu.VMEM((rows, width), BF16),
-            pltpu.VMEM((2, experts * cap * hc, LANE), F32),
+            pltpu.VMEM((2, experts * (cap * hc + 1), LANE), F32),
             pltpu.VMEM((2, experts, cap * hc, LANE), BF16),
             pltpu.SemaphoreType.DMA((7,)),
         ],
@@ -283,11 +285,14 @@
     recv_other = lax.ppermute(recv, "pair", swap)
 
     def unpack(ref, wide, x_dst, s_dst):
-        wide[...] = ref[...].astype(F32)
+        for e in range(experts):
+            wide[e * (disp + 1) : e * (disp + 1) + disp, :] = ref[
+                e * disp : (e + 1) * disp, :
+            ].astype(F32)
         for s in range(cap):
             for t, dst in ((0, x_dst), (1, s_dst)):
                 for c in range(hc):
-                    val = wide[pl.ds((t * cap + s) * hc + c, experts, stride=disp), :]
+                    val = wide[pl.ds((t * cap + s) * hc + c, experts, stride=disp + 1), :]
                     dst[s * experts : (s + 1) * experts, c * LANE : (c + 1) * LANE] = val.astype(
                         BF16
                     )
@@ -315,7 +320,7 @@
         in_specs=[vspec(), aspec()],
         out_specs=(vspec(),) * 3,
         scratch_shapes=[
-            pltpu.VMEM((experts * disp, LANE), F32),
+            pltpu.VMEM((experts * (disp + 1), LANE), F32),
             pltpu.VMEM((slots, half), BF16),
             pltpu.SemaphoreType.DMA(()),
         ],
@@ -363,7 +368,7 @@
         in_specs=[vspec(), aspec(), vspec()],
         out_specs=(vspec(),) * 4,
         scratch_shapes=[
-            pltpu.VMEM((experts * disp, LANE), F32),
+            pltpu.VMEM((experts * (disp + 1), LANE), F32),
             pltpu.VMEM((slots, half), BF16),
             pltpu.VMEM((3, half, fh), BF16),
             pltpu.SemaphoreType.DMA(()),
@@ -434,14 +439,12 @@
     sum_low = lax.ppermute(sum_low, "dp", ahead)
     sum_high = lax.ppermute(sum_high, "dp", behind)
 
-    def pack_kernel(keep_ref, mixed_ref, sent_ref, out_ref, scr):
-        for c in range(hc):
-            lanes = slice(c * LANE, (c + 1) * LANE)
-            total = keep_ref[:, lanes] + sent_ref[:, lanes].astype(F32)
-            for s in range(cap):
-                scr[pl.ds(s * hc + c, experts, stride=back), :] = total[
-                    s * experts : (s + 1) * experts
-                ]
+    def pack_kernel(keep_ref, mixed_ref, sent_ref, out_ref):
+        for s in range(cap):
+            span = slice(s * experts, (s + 1) * experts)
+            total = keep_ref[span, :] + sent_ref[span, :half].astype(F32)
+            total = total.reshape(experts, hc, LANE).astype(BF16)
+            out_ref[:, s * hc // 2 : (s + 1) * hc // 2] = total.reshape(experts, hc // 2, 2, LANE)
         tail = sent_ref[:, half:].astype(F32)
         full_mixed = mixed_ref[...] + tail + pltpu.roll(tail, LANE // 2, 1)
         high_mixed = full_mixed.astype(BF16).astype(F32)
@@ -451,21 +454,19 @@
             span = slice(s * experts, (s + 1) * experts)
             line = jnp.where(lane == s, high_mixed[span], line)
             line = jnp.where(lane == LANE // 2 + s, full_mixed[span] - high_mixed[span], line)
-        scr[pl.ds(cap * hc, experts, stride=back), :] = line
-        scr[pl.ds(cap * hc + 1, experts, stride=back), :] = jnp.zeros((experts, LANE), F32)
-        out_ref[...] = scr[...].reshape(experts * back // 2, 2, LANE).astype(BF16)
+        line = jnp.stack([line, jnp.zeros((experts, LANE), F32)], axis=1)
+        out_ref[:, back // 2 - 1 :] = line.reshape(experts, 1, 2, LANE).astype(BF16)
 
     packed = pl.pallas_call(
         pack_kernel,
-        out_shape=jax.ShapeDtypeStruct((experts * back // 2, 2, LANE), BF16),
+        out_shape=jax.ShapeDtypeStruct((experts, back // 2, 2, LANE), BF16),
         in_specs=[vspec()] * 3,
         out_specs=vspec(),
-        scratch_shapes=[pltpu.VMEM((experts * back, LANE), F32)],
         compiler_params=params(),
         name="pack",
     )(vm(keep), vm(mixed), vm(sent))
 
-    returned = exchange(packed.reshape(experts, back // 2, 2, LANE)).reshape(packed.shape)
+    returned = exchange(packed)
 
     def total_kernel(mine_ref, a_ref, b_ref, c_ref, d_ref, gate_ref, up_ref):
         for span, one, two in ((slice(0, part), a_ref, b_ref), (slice(part, shard), c_ref, d_ref)):
@@ -485,7 +486,7 @@
 
     def combine_kernel(
         back_ref, hot_hbm, delta_hbm, mix_hbm, out_ref,
-        wide, grads, small, hot_ref, delta_ref, mix_ref, sems,
+        grads, small, hot_ref, delta_ref, mix_ref, sems,
     ):
         loads = [
             pltpu.make_async_copy(hot_hbm, hot_ref, sems.at[0]),
@@ -494,14 +495,12 @@
         ]
         for load in loads:
             load.start()
-        wide[...] = back_ref[...].astype(F32).reshape(experts * back, LANE)
         lane = jnp.bitwise_and(iota((experts, LANE), 1), LANE // 2 - 1)
-        line = wide[pl.ds(cap * hc, experts, stride=back), :]
+        line = back_ref[:, back // 2 - 1 :].astype(F32).reshape(experts, 2 * LANE)[:, :LANE]
         for s in range(cap):
             span = slice(s * experts, (s + 1) * experts)
-            for c in range(hc):
-                val = wide[pl.ds(s * hc + c, experts, stride=back), :]
-                grads[span, c * LANE : (c + 1) * LANE] = val.astype(BF16)
+            block = back_ref[:, s * hc // 2 : (s + 1) * hc // 2].astype(F32)
+            grads[span, :] = block.reshape(experts, half).astype(BF16)
             small[span, :] = jnp.where(lane == s, line, 0.0).astype(BF16)
         grads[slots:, :] = jnp.zeros((3 * LANE - slots, half), BF16)
         small[slots:, :] = jnp.zeros((3 * LANE - slots, LANE), BF16)
@@ -520,7 +519,6 @@
         in_specs=[vspec()] + [aspec()] * 3,
         out_specs=vspec(),
         scratch_shapes=[
-            pltpu.VMEM((experts * back, LANE), F32),
             pltpu.VMEM((3 * LANE, half), BF16),
             pltpu.VMEM((3 * LANE, LANE), BF16),
             pltpu.VMEM((2 * rows, 3 * LANE), BF16),

time: 206 us -> 206 us (level)
  no operation moved by 1% of the time
where the time goes in v4:
time: 206 us; the launch traced here: 205 us
  blocking collectives  79.6 us (39%)
  starting transfers between devices  60 us (29%)
  waiting for transfers between devices  40.1 us (19%)
  Pallas kernels  24.6 us (12%)
    all_to_all x1, blocking collectives, exchange(): return lax.all_to_all(x, 'expert', split_axis=0, concat_axis=0, tiled=True)  79.6 us
    ppermute x1, waiting for transfers between devices, local(): low_far = lax.ppermute(low_prev, 'dp', ahead)  11.1 us
    all_to_all x1, waiting for transfers between devices, exchange(): return lax.all_to_all(x, 'expert', split_axis=0, concat_axis=0, tiled=True)  8.11 us
    ppermute x1, waiting for transfers between devices, local(): low_next = lax.ppermute(low, 'dp', behind)  7.71 us
    ppermute x1, starting transfers between devices, local(): recv_other = lax.ppermute(recv, 'pair', swap)  7.52 us
    all_to_all x1, starting transfers between devices, exchange(): return lax.all_to_all(x, 'expert', split_axis=0, concat_axis=0, tiled=True)  6.43 us
    ppermute x1, waiting for transfers between devices, local(): low_prev = lax.ppermute(low, 'dp', ahead)  6.24 us
    ppermute x1, starting transfers between devices, local(): row_half_other = lax.ppermute(row_half, 'pair', swap)  5.21 us
  transfers between devices with their start and end apart: 16, of which 7 were waited for; matrix products, arithmetic and copies ran while one was open for 0% of the time, Pallas kernels for 7%

profile of v4, /device:TPU:1, one launch (start us, length us, event | category | flops | bytes accessed | tf_op | source)
XLA Modules:
  0.0 205.2 jit_solution(11227260666668372530)
XLA Ops:
  0.6 3.8 %dispatch.1 = (bf16[64,80,128]{2,1,0:T(8,128)(2,1)}, f32[8,128]{1,0:T(8,128)S(1)}) custom-call(bf16[256,2048]{1,0:T(8,128)(2,1)} %bytes_hbm.1, s32[1,128]{1,0:T(1,128)} %bitcast.9, s32[2,128]{1,0:T(2,128)} %bitcast.8, bf16[128,2048]{1,0:T(8,128)(2,1)} %cot_hbm.1, bf16[64,2048]{1,0:T(8,128)(2,1)} %bitcast.6), custom_call_target="tpu_custom_call" | custom-call | tf_op jit(solution)/shard_map/dispatch/pallas_call | solution.py:144
  4.4 79.6 %all_to_all.10 = bf16[64,80,128]{2,1,0:T(8,128)(2,1)S(1)} all-to-all(bf16[64,80,128]{2,1,0:T(8,128)(2,1)} %get-tuple-element.28), channel_id=1, replica_groups=mesh['expert'=64,'dp'=4,'pair'=2] {'expert'}, dimensions={0} | all-to-all | bytes 2621440 | tf_op jit(solution)/shard_map/all_to_all | solution.py:174
  84.0 7.5 %collective-permute-start = (bf16[5120,128]{1,0:T(8,128)(2,1)S(1)}, bf16[5120,128]{1,0:T(8,128)(2,1)S(1)}, u32[]{:S(2)}, u32[]{:S(2)}) collective-permute-start(bf16[5120,128]{1,0:T(8,128)(2,1)S(1)} %bitcast.4), channel_id=1, source_target_pairs={{0,1},{1,0},{2,3},{3,2},{4,5},{5,4},{6,7},{7,6},{8,9},{9,8},{10,11... | collective-permute-start | bytes 3932168 | tf_op jit(solution)/shard_map/ppermute | solution.py:285
  91.6 1.4 stack.1
  93.0 3.2 %collective-permute-start.3 = (bf16[3,256,384]{2,1,0:T(8,128)(2,1)S(1)}, bf16[3,256,384]{2,1,0:T(8,128)(2,1)S(1)}, u32[]{:S(2)}, u32[]{:S(2)}) collective-permute-start(bf16[3,256,384]{2,1,0:T(8,128)(2,1)S(1)} %get-tuple-element.29.refs_0_), channel_id=1, source_target_pairs={{0,2},{2,4},{4,6},{6,0},{1,3},{3,5},{5,7},{7,1},{8,10},{10,12},{12... | collective-permute-start | bytes 1769480 | tf_op jit(solution)/shard_map/ppermute | solution.py:249
  96.2 3.4 %collective-permute-start.2 = (bf16[3,256,384]{2,1,0:T(8,128)(2,1)S(1)}, bf16[3,256,384]{2,1,0:T(8,128)(2,1)S(1)}, u32[]{:S(2)}, u32[]{:S(2)}) collective-permute-start(bf16[3,256,384]{2,1,0:T(8,128)(2,1)S(1)} %get-tuple-element.30.refs_1_), channel_id=1, source_target_pairs={{0,6},{2,0},{4,2},{6,4},{1,7},{3,1},{5,3},{7,5},{8,14},{10,8},{12,... | collective-permute-start | bytes 1769480 | tf_op jit(solution)/shard_map/ppermute | solution.py:250
  99.5 3.4 %collective-permute-start.1 = (bf16[3,256,384]{2,1,0:T(8,128)(2,1)S(1)}, bf16[3,256,384]{2,1,0:T(8,128)(2,1)S(1)}, u32[]{:S(2)}, u32[]{:S(2)}) collective-permute-start(bf16[3,256,384]{2,1,0:T(8,128)(2,1)S(1)} %get-tuple-element.29.refs_0_), channel_id=1, source_target_pairs={{0,6},{2,0},{4,2},{6,4},{1,7},{3,1},{5,3},{7,5},{8,14},{10,8},{12,... | collective-permute-start | bytes 1769480 | tf_op jit(solution)/shard_map/ppermute | solution.py:252
  102.9 1.9 collective-permute-start.6
  104.8 6.2 %collective-permute-done.3.refs_6_ = bf16[3,256,384]{2,1,0:T(8,128)(2,1)S(1)} collective-permute-done((bf16[3,256,384]{2,1,0:T(8,128)(2,1)S(1)}, bf16[3,256,384]{2,1,0:T(8,128)(2,1)S(1)}, u32[]{:S(2)}, u32[]{:S(2)}) %collective-permute-start.3) | collective-permute-done | bytes 589856 | tf_op jit(solution)/shard_map/ppermute | solution.py:249
  111.1 1.9 collective-permute-start.4
  113.0 0.0 collective-permute-done.2.refs_3_
  113.0 4.6 %collective-permute-start.5 = (bf16[3,256,384]{2,1,0:T(8,128)(2,1)S(1)}, bf16[3,256,384]{2,1,0:T(8,128)(2,1)S(1)}, u32[]{:S(2)}, u32[]{:S(2)}) collective-permute-start(bf16[3,256,384]{2,1,0:T(8,128)(2,1)S(1)} %collective-permute-done.2.refs_3_), channel_id=1, source_target_pairs={{0,6},{2,0},{4,2},{6,4},{1,7},{3,1},{5,3},{7,5},{8,14},{10,8},{12,... | collective-permute-start | bytes 1769480 | tf_op jit(solution)/shard_map/ppermute | solution.py:254
  117.6 7.7 %collective-permute-done.1.refs_2_ = bf16[3,256,384]{2,1,0:T(8,128)(2,1)S(1)} collective-permute-done((bf16[3,256,384]{2,1,0:T(8,128)(2,1)S(1)}, bf16[3,256,384]{2,1,0:T(8,128)(2,1)S(1)}, u32[]{:S(2)}, u32[]{:S(2)}) %collective-permute-start.1) | collective-permute-done | bytes 589856 | tf_op jit(solution)/shard_map/ppermute | solution.py:252
  125.3 0.0 collective-permute-done.6.refs_7_
  125.3 11.1 %collective-permute-done.4.refs_4_ = bf16[3,256,384]{2,1,0:T(8,128)(2,1)S(1)} collective-permute-done((bf16[3,256,384]{2,1,0:T(8,128)(2,1)S(1)}, bf16[3,256,384]{2,1,0:T(8,128)(2,1)S(1)}, u32[]{:S(2)}, u32[]{:S(2)}) %collective-permute-start.4) | collective-permute-done | bytes 589856 | tf_op jit(solution)/shard_map/ppermute | solution.py:253
  136.4 1.6 collective-permute-done.5.refs_5_
  137.9 2.2 %assemble.1.w_hbm = bf16[3,2048,384]{2,1,0:T(8,128)(2,1)} custom-call(bf16[3,256,384]{2,1,0:T(8,128)(2,1)S(1)} %get-tuple-element.29.refs_0_, bf16[3,256,384]{2,1,0:T(8,128)(2,1)S(1)} %get-tuple-element.30.refs_1_, bf16[3,256,384]{2,1,0:T(8,128)(2,1)S(1)} %collective-permute-done.1.refs_2_, bf16[3,256,384]{2,1,0:T(8,128)(2,1)S(1)} %collective-permute-done.2.refs_3_, ...), custom_call_target="tpu_custom_call" | custom-call | tf_op jit(solution)/shard_map/assemble/pallas_call | solution.py:274
  140.2 2.9 %own.1 = (bf16[320,1024]{1,0:T(8,128)(2,1)S(1)}, f32[3,320,384]{2,1,0:T(8,128)S(1)}, bf16[3,1024,384]{2,1,0:T(8,128)(2,1)S(1)}) custom-call(bf16[5120,128]{1,0:T(8,128)(2,1)S(1)} %bitcast.5, bf16[3,2048,384]{2,1,0:T(8,128)(2,1)} %assemble.1.w_hbm), custom_call_target="tpu_custom_call" | custom-call | tf_op jit(solution)/shard_map/own/pallas_call | solution.py:313
  143.1 0.0 collective-permute-done.recv_ref
  143.1 3.7 %grads.1 = (bf16[320,1024]{1,0:T(8,128)(2,1)S(1)}, bf16[320,768]{1,0:T(8,128)(2,1)S(1)}, bf16[320,1152]{1,0:T(8,128)(2,1)S(1)}, f32[320,128]{1,0:T(8,128)S(1)}) custom-call(bf16[5120,128]{1,0:T(8,128)(2,1)S(1)} %collective-permute-done.recv_ref, bf16[3,2048,384]{2,1,0:T(8,128)(2,1)} %assemble.1.w_hbm, f32[3,320,384]{2,1,0:T(8,128)S(1)} %get-tuple-element.31.pre_ref), custom_call_target="tpu_custom_call" | custom-call | tf_op jit(solution)/shard_map/grads/pallas_call | solution.py:360
  146.8 3.1 %collective-permute-start.7 = (bf16[320,1152]{1,0:T(8,128)(2,1)S(1)}, bf16[320,1152]{1,0:T(8,128)(2,1)S(1)}, u32[]{:S(2)}, u32[]{:S(2)}) collective-permute-start(bf16[320,1152]{1,0:T(8,128)(2,1)S(1)} %get-tuple-element.35), channel_id=1, source_target_pairs={{0,1},{1,0},{2,3},{3,2},{4,5},{5,4},{6,7},{7,6},{8,9},{9,8},{10,11... | collective-permute-start | bytes 2211848 | tf_op jit(solution)/shard_map/ppermute | solution.py:380
  149.9 0.9 keep.1.keep_ref
  150.8 0.9 collective-permute-done.7.sent_ref
  151.7 1.7 pack.1
  153.4 6.4 %all-to-all-start.1 = ((bf16[64,21,2,128]{3,2,1,0:T(2,128)(2,1)}), bf16[64,21,2,128]{3,2,1,0:T(2,128)(2,1)S(1)}, u32[]{:S(2)}, u32[]{:S(2)}) async-start(bf16[64,21,2,128]{3,2,1,0:T(2,128)(2,1)} %pack.1), calls=%async_computation.1 | async-start | bytes 1376256 | tf_op jit(solution)/shard_map/all_to_all | solution.py:174
  159.9 0.0 copy-start
  159.9 2.3 %weight.1 = (bf16[512,768]{1,0:T(8,128)(2,1)S(1)}, bf16[256,768]{1,0:T(8,128)(2,1)S(1)}, bf16[256,768]{1,0:T(8,128)(2,1)}, bf16[256,768]{1,0:T(8,128)(2,1)S(1)},...) custom-call(bf16[320,1024]{1,0:T(8,128)(2,1)S(1)} %get-tuple-element.40.own_ref, ...), custom_call_target="tpu_custom_call" | custom-call | tf_op jit(solution)/shard_map/weight/pallas_call | solution.py:410
  162.2 4.5 %collective-permute-start.10 = (bf16[256,768]{1,0:T(8,128)(2,1)S(1)}, bf16[256,768]{1,0:T(8,128)(2,1)S(1)}, u32[]{:S(2)}, u32[]{:S(2)}) collective-permute-start(bf16[256,768]{1,0:T(8,128)(2,1)S(1)} %get-tuple-element.46), channel_id=1, source_target_pairs={{0,6},{2,0},{4,2},{6,4},{1,7},{3,1},{5,3},{7,5},{8,14},{10,8},{12,... | collective-permute-start | bytes 1179656 | tf_op jit(solution)/shard_map/ppermute | solution.py:422
  166.7 1.9 collective-permute-start.9
  168.7 4.6 %collective-permute-start.12 = (bf16[256,768]{1,0:T(8,128)(2,1)}, bf16[256,768]{1,0:T(8,128)(2,1)S(1)}, u32[]{:S(2)}, u32[]{:S(2)}) collective-permute-start(bf16[256,768]{1,0:T(8,128)(2,1)} %get-tuple-element.48), channel_id=1, source_target_pairs={{0,6},{2,0},{4,2},{6,4},{1,7},{3,1},{5,3},{7,5},{8,14},{10,8},{12,... | collective-permute-start | bytes 1179656 | tf_op jit(solution)/shard_map/ppermute | solution.py:424
  173.2 1.9 collective-permute-start.13
  175.2 0.0 collective-permute-done.10.d_ref
  175.2 4.4 %collective-permute-done.9.b_ref = bf16[256,768]{1,0:T(8,128)(2,1)S(1)} collective-permute-done((bf16[256,768]{1,0:T(8,128)(2,1)S(1)}, bf16[256,768]{1,0:T(8,128)(2,1)S(1)}, u32[]{:S(2)}, u32[]{:S(2)}) %collective-permute-start.9) | collective-permute-done | bytes 393248 | tf_op jit(solution)/shard_map/ppermute | solution.py:421
  179.6 1.0 add.1
  180.6 1.9 collective-permute-start.11
  182.5 4.6 %collective-permute-start.14 = (bf16[256,768]{1,0:T(8,128)(2,1)}, bf16[256,768]{1,0:T(8,128)(2,1)S(1)}, u32[]{:S(2)}, u32[]{:S(2)}) collective-permute-start(bf16[256,768]{1,0:T(8,128)(2,1)} %get-tuple-element.50), channel_id=1, source_target_pairs={{0,6},{2,0},{4,2},{6,4},{1,7},{3,1},{5,3},{7,5},{8,14},{10,8},{12,... | collective-permute-start | bytes 1179656 | tf_op jit(solution)/shard_map/ppermute | solution.py:440
  187.1 0.0 copy-done
  187.1 1.1 aux.1
  188.2 8.1 %all-to-all-done.1.back_ref = bf16[64,21,2,128]{3,2,1,0:T(2,128)(2,1)S(1)} async-done(((bf16[64,21,2,128]{3,2,1,0:T(2,128)(2,1)}), bf16[64,21,2,128]{3,2,1,0:T(2,128)(2,1)S(1)}, u32[]{:S(2)}, u32[]{:S(2)}) %all-to-all-start.1) | async-done | bytes 688160 | tf_op jit(solution)/shard_map/all_to_all | solution.py:174
  196.3 1.7 combine.1.own_ref
  198.0 5.2 %collective-permute-start.8 = (bf16[128,1024]{1,0:T(8,128)(2,1)S(1)}, bf16[128,1024]{1,0:T(8,128)(2,1)S(1)}, u32[]{:S(2)}, u32[]{:S(2)}) collective-permute-start(bf16[128,1024]{1,0:T(8,128)(2,1)S(1)} %combine.1.own_ref), channel_id=1, source_target_pairs={{0,1},{1,0},{2,3},{3,2},{4,5},{5,4},{6,7},{7,6},{8,9},{9,8},{10,11... | collective-permute-start | bytes 786440 | tf_op jit(solution)/shard_map/ppermute | solution.py:533
  203.2 0.0 collective-permute-done.12.b_ref
  203.2 0.0 collective-permute-done.13.c_ref
  203.2 0.0 collective-permute-done.11.a_ref
  203.2 0.0 collective-permute-done.14.d_ref
  203.2 1.1 total.1
  204.3 0.0 collective-permute-done.8.oth_ref
  204.4 0.8 join.1
Async XLA Ops:
  84.0 59.0 %collective-permute-start = (bf16[5120,128]{1,0:T(8,128)(2,1)S(1)}, bf16[5120,128]{1,0:T(8,128)(2,1)S(1)}, u32[]{:S(2)}, u32[]{:S(2)}) collective-permute-start(bf16[5120,128]{1,0:T(8,128)(2,1)S(1)} %bitcast.4), channel_id=1, source_target_pairs={{0,1},{1,0},{2,3},{3,2},{4,5},{5,4},{6,7},{7,6},{8,9},{9,8},{10,11... | collective-permute-start | bytes 3932168 | tf_op jit(solution)/shard_map/ppermute | solution.py:285
  93.0 18.1 %collective-permute-start.3 = (bf16[3,256,384]{2,1,0:T(8,128)(2,1)S(1)}, bf16[3,256,384]{2,1,0:T(8,128)(2,1)S(1)}, u32[]{:S(2)}, u32[]{:S(2)}) collective-permute-start(bf16[3,256,384]{2,1,0:T(8,128)(2,1)S(1)} %get-tuple-element.29.refs_0_), channel_id=1, source_target_pairs={{0,2},{2,4},{4,6},{6,0},{1,3},{3,5},{5,7},{7,1},{8,10},{10,12},{12... | collective-permute-start | bytes 1769480 | tf_op jit(solution)/shard_map/ppermute | solution.py:249
  96.2 16.8 %collective-permute-start.2 = (bf16[3,256,384]{2,1,0:T(8,128)(2,1)S(1)}, bf16[3,256,384]{2,1,0:T(8,128)(2,1)S(1)}, u32[]{:S(2)}, u32[]{:S(2)}) collective-permute-start(bf16[3,256,384]{2,1,0:T(8,128)(2,1)S(1)} %get-tuple-element.30.refs_1_), channel_id=1, source_target_pairs={{0,6},{2,0},{4,2},{6,4},{1,7},{3,1},{5,3},{7,5},{8,14},{10,8},{12,... | collective-permute-start | bytes 1769480 | tf_op jit(solution)/shard_map/ppermute | solution.py:250
  99.5 25.8 %collective-permute-start.1 = (bf16[3,256,384]{2,1,0:T(8,128)(2,1)S(1)}, bf16[3,256,384]{2,1,0:T(8,128)(2,1)S(1)}, u32[]{:S(2)}, u32[]{:S(2)}) collective-permute-start(bf16[3,256,384]{2,1,0:T(8,128)(2,1)S(1)} %get-tuple-element.29.refs_0_), channel_id=1, source_target_pairs={{0,6},{2,0},{4,2},{6,4},{1,7},{3,1},{5,3},{7,5},{8,14},{10,8},{12,... | collective-permute-start | bytes 1769480 | tf_op jit(solution)/shard_map/ppermute | solution.py:252
  102.9 22.4 %collective-permute-start.6 = (bf16[3,256,384]{2,1,0:T(8,128)(2,1)S(1)}, bf16[3,256,384]{2,1,0:T(8,128)(2,1)S(1)}, u32[]{:S(2)}, u32[]{:S(2)}) collective-permute-start(bf16[3,256,384]{2,1,0:T(8,128)(2,1)S(1)} %get-tuple-element.30.refs_1_), channel_id=1, source_target_pairs={{0,2},{2,4},{4,6},{6,0},{1,3},{3,5},{5,7},{7,1},{8,10},{10,12},{12... | collective-permute-start | bytes 1769480 | tf_op jit(solution)/shard_map/ppermute | solution.py:251
  111.1 25.3 %collective-permute-start.4 = (bf16[3,256,384]{2,1,0:T(8,128)(2,1)S(1)}, bf16[3,256,384]{2,1,0:T(8,128)(2,1)S(1)}, u32[]{:S(2)}, u32[]{:S(2)}) collective-permute-start(bf16[3,256,384]{2,1,0:T(8,128)(2,1)S(1)} %collective-permute-done.3.refs_6_), channel_id=1, source_target_pairs={{0,2},{2,4},{4,6},{6,0},{1,3},{3,5},{5,7},{7,1},{8,10},{10,12},{12... | collective-permute-start | bytes 1769480 | tf_op jit(solution)/shard_map/ppermute | solution.py:253
  113.0 24.9 %collective-permute-start.5 = (bf16[3,256,384]{2,1,0:T(8,128)(2,1)S(1)}, bf16[3,256,384]{2,1,0:T(8,128)(2,1)S(1)}, u32[]{:S(2)}, u32[]{:S(2)}) collective-permute-start(bf16[3,256,384]{2,1,0:T(8,128)(2,1)S(1)} %collective-permute-done.2.refs_3_), channel_id=1, source_target_pairs={{0,6},{2,0},{4,2},{6,4},{1,7},{3,1},{5,3},{7,5},{8,14},{10,8},{12,... | collective-permute-start | bytes 1769480 | tf_op jit(solution)/shard_map/ppermute | solution.py:254
  146.8 4.9 %collective-permute-start.7 = (bf16[320,1152]{1,0:T(8,128)(2,1)S(1)}, bf16[320,1152]{1,0:T(8,128)(2,1)S(1)}, u32[]{:S(2)}, u32[]{:S(2)}) collective-permute-start(bf16[320,1152]{1,0:T(8,128)(2,1)S(1)} %get-tuple-element.35), channel_id=1, source_target_pairs={{0,1},{1,0},{2,3},{3,2},{4,5},{5,4},{6,7},{7,6},{8,9},{9,8},{10,11... | collective-permute-start | bytes 2211848 | tf_op jit(solution)/shard_map/ppermute | solution.py:380
  153.4 42.9 %all-to-all-start.1 = ((bf16[64,21,2,128]{3,2,1,0:T(2,128)(2,1)}), bf16[64,21,2,128]{3,2,1,0:T(2,128)(2,1)S(1)}, u32[]{:S(2)}, u32[]{:S(2)}) async-start(bf16[64,21,2,128]{3,2,1,0:T(2,128)(2,1)} %pack.1), calls=%async_computation.1 | async-start | bytes 1376256 | tf_op jit(solution)/shard_map/all_to_all | solution.py:174
  159.9 27.2 %copy-start = (bf16[2048,64]{0,1:T(8,128)(2,1)S(1)}, bf16[2048,64]{0,1:T(8,128)(2,1)}, u32[]{:S(2)}) copy-start(bf16[2048,64]{0,1:T(8,128)(2,1)} %param.12) | copy-start | bytes 786436
  162.2 13.0 %collective-permute-start.10 = (bf16[256,768]{1,0:T(8,128)(2,1)S(1)}, bf16[256,768]{1,0:T(8,128)(2,1)S(1)}, u32[]{:S(2)}, u32[]{:S(2)}) collective-permute-start(bf16[256,768]{1,0:T(8,128)(2,1)S(1)} %get-tuple-element.46), channel_id=1, source_target_pairs={{0,6},{2,0},{4,2},{6,4},{1,7},{3,1},{5,3},{7,5},{8,14},{10,8},{12,... | collective-permute-start | bytes 1179656 | tf_op jit(solution)/shard_map/ppermute | solution.py:422
  166.7 12.8 %collective-permute-start.9 = (bf16[256,768]{1,0:T(8,128)(2,1)S(1)}, bf16[256,768]{1,0:T(8,128)(2,1)S(1)}, u32[]{:S(2)}, u32[]{:S(2)}) collective-permute-start(bf16[256,768]{1,0:T(8,128)(2,1)S(1)} %get-tuple-element.44), channel_id=1, source_target_pairs={{0,2},{2,4},{4,6},{6,0},{1,3},{3,5},{5,7},{7,1},{8,10},{10,12},{12... | collective-permute-start | bytes 1179656 | tf_op jit(solution)/shard_map/ppermute | solution.py:421
  168.7 34.6 %collective-permute-start.12 = (bf16[256,768]{1,0:T(8,128)(2,1)}, bf16[256,768]{1,0:T(8,128)(2,1)S(1)}, u32[]{:S(2)}, u32[]{:S(2)}) collective-permute-start(bf16[256,768]{1,0:T(8,128)(2,1)} %get-tuple-element.48), channel_id=1, source_target_pairs={{0,6},{2,0},{4,2},{6,4},{1,7},{3,1},{5,3},{7,5},{8,14},{10,8},{12,... | collective-permute-start | bytes 1179656 | tf_op jit(solution)/shard_map/ppermute | solution.py:424
  173.2 30.0 %collective-permute-start.13 = (bf16[256,768]{1,0:T(8,128)(2,1)}, bf16[256,768]{1,0:T(8,128)(2,1)S(1)}, u32[]{:S(2)}, u32[]{:S(2)}) collective-permute-start(bf16[256,768]{1,0:T(8,128)(2,1)} %get-tuple-element.49), channel_id=1, source_target_pairs={{0,2},{2,4},{4,6},{6,0},{1,3},{3,5},{5,7},{7,1},{8,10},{10,12},{12... | collective-permute-start | bytes 1179656 | tf_op jit(solution)/shard_map/ppermute | solution.py:423
  180.6 22.7 %collective-permute-start.11 = (bf16[256,768]{1,0:T(8,128)(2,1)}, bf16[256,768]{1,0:T(8,128)(2,1)S(1)}, u32[]{:S(2)}, u32[]{:S(2)}) collective-permute-start(bf16[256,768]{1,0:T(8,128)(2,1)} %get-tuple-element.47), channel_id=1, source_target_pairs={{0,2},{2,4},{4,6},{6,0},{1,3},{3,5},{5,7},{7,1},{8,10},{10,12},{12... | collective-permute-start | bytes 1179656 | tf_op jit(solution)/shard_map/ppermute | solution.py:439
  182.5 20.7 %collective-permute-start.14 = (bf16[256,768]{1,0:T(8,128)(2,1)}, bf16[256,768]{1,0:T(8,128)(2,1)S(1)}, u32[]{:S(2)}, u32[]{:S(2)}) collective-permute-start(bf16[256,768]{1,0:T(8,128)(2,1)} %get-tuple-element.50), channel_id=1, source_target_pairs={{0,6},{2,0},{4,2},{6,4},{1,7},{3,1},{5,3},{7,5},{8,14},{10,8},{12,... | collective-permute-start | bytes 1179656 | tf_op jit(solution)/shard_map/ppermute | solution.py:440
  198.0 6.4 %collective-permute-start.8 = (bf16[128,1024]{1,0:T(8,128)(2,1)S(1)}, bf16[128,1024]{1,0:T(8,128)(2,1)S(1)}, u32[]{:S(2)}, u32[]{:S(2)}) collective-permute-start(bf16[128,1024]{1,0:T(8,128)(2,1)S(1)} %combine.1.own_ref), channel_id=1, source_target_pairs={{0,1},{1,0},{2,3},{3,2},{4,5},{5,4},{6,7},{7,6},{8,9},{9,8},{10,11... | collective-permute-start | bytes 786440 | tf_op jit(solution)/shard_map/ppermute | solution.py:533

commit v5 on v4

--- a/solution.py
+++ b/solution.py
@@ -9,7 +9,7 @@
 F32 = jnp.float32
 BF16 = jnp.bfloat16
 LANE = 128
-VMEM_LIMIT = 24 * 1024 * 1024
+VMEM_LIMIT = 32 * 1024 * 1024
 
 
 def vm(x):
@@ -282,6 +282,7 @@
     )(*[vm(x) for x in pieces])
 
     swap = [(0, 1), (1, 0)]
+    full_other = lax.ppermute(full, "pair", swap)
     recv_other = lax.ppermute(recv, "pair", swap)
 
     def unpack(ref, wide, x_dst, s_dst):
@@ -297,15 +298,22 @@
                         BF16
                     )
 
-    def fetch(w_hbm, w_buf, sem, h, count):
+    def fetch(own_hbm, oth_hbm, w_buf, sems, h):
         row = pl.multiple_of(h * half, half)
-        return pltpu.make_async_copy(w_hbm.at[pl.ds(0, count), pl.ds(row, half), :], w_buf, sem)
-
-    def own_kernel(recv_ref, w_hbm, x_ref, pre_ref, w_buf, wide, s_buf, sem):
-        load = fetch(w_hbm, w_buf, sem, pair_id(), 3)
-        load.start()
+        return [
+            pltpu.make_async_copy(
+                src.at[:, pl.ds(row, half), :], w_buf.at[:, :, pl.ds(i * fh, fh)], sems.at[i]
+            )
+            for i, src in enumerate((own_hbm, oth_hbm))
+        ]
+
+    def own_kernel(recv_ref, own_hbm, oth_hbm, x_ref, pre_ref, w_buf, wide, s_buf, sems):
+        loads = fetch(own_hbm, oth_hbm, w_buf, sems, pair_id())
+        for load in loads:
+            load.start()
         unpack(recv_ref, wide, x_ref, s_buf)
-        load.wait()
+        for load in loads:
+            load.wait()
         pre_ref[0] = dot(x_ref[...], w_buf[0])
         pre_ref[1] = dot(x_ref[...], w_buf[1])
         pre_ref[2] = dot(s_buf[...], w_buf[2])
@@ -314,27 +322,30 @@
         own_kernel,
         out_shape=(
             pltpu.VMEM((slots, half), BF16),
-            pltpu.VMEM((3, slots, fh), F32),
-            pltpu.VMEM((3, half, fh), BF16),
+            pltpu.VMEM((3, slots, 2 * fh), F32),
+            pltpu.VMEM((3, half, 2 * fh), BF16),
         ),
-        in_specs=[vspec(), aspec()],
+        in_specs=[vspec(), aspec(), aspec()],
         out_specs=(vspec(),) * 3,
         scratch_shapes=[
             pltpu.VMEM((experts * (disp + 1), LANE), F32),
             pltpu.VMEM((slots, half), BF16),
-            pltpu.SemaphoreType.DMA(()),
+            pltpu.SemaphoreType.DMA((2,)),
         ],
         compiler_params=params(),
         name="own",
-    )(vm(recv), hb(full))
+    )(vm(recv), hb(full), hb(full_other))
 
     def grads_kernel(
-        recv_ref, w_hbm, pre_ref, x_ref, joined_ref, send_ref, mixed_ref, wide, s_buf, w_buf, sem
+        recv_ref, own_hbm, oth_hbm, pre_ref, w_own_ref, x_ref, joined_ref, out_ref,
+        wide, s_buf, w_buf, sems,
     ):
-        load = fetch(w_hbm, w_buf, sem, 1 - pair_id(), 3)
-        load.start()
+        loads = fetch(own_hbm, oth_hbm, w_buf, sems, 1 - pair_id())
+        for load in loads:
+            load.start()
         unpack(recv_ref, wide, x_ref, s_buf)
-        load.wait()
+        for load in loads:
+            load.wait()
         gate = pre_ref[0] + dot(x_ref[...], w_buf[0])
         up = pre_ref[1] + dot(x_ref[...], w_buf[1])
         grad = pre_ref[2] + dot(s_buf[...], w_buf[2])
@@ -345,51 +356,41 @@
         mixed = jnp.sum(hidden * grad, axis=1, keepdims=True)
         gate_grad = (grad * up * slope).astype(BF16)
         up_grad = (grad * activ).astype(BF16)
-        joined_ref[:, :fh] = gate_grad
-        joined_ref[:, fh:] = up_grad
-        send_ref[:, :half] = (
-            dot_nt(gate_grad, w_buf[0]) + dot_nt(up_grad, w_buf[1])
-        ).astype(BF16)
-        wide_mixed = jnp.broadcast_to(mixed, (slots, LANE))
-        high = wide_mixed.astype(BF16).astype(F32)
-        mixed_ref[...] = wide_mixed
-        send_ref[:, half:] = jnp.where(
-            iota((slots, LANE), 1) < LANE // 2, high, wide_mixed - high
-        ).astype(BF16)
-
-    x_other, joined, send, mixed = pl.pallas_call(
+        joined_ref[:, :fh] = gate_grad[:, :fh]
+        joined_ref[:, fh:] = up_grad[:, :fh]
+        pick = dot_nt(gate_grad, w_own_ref[0]) + dot_nt(up_grad, w_own_ref[1])
+        for s in range(cap):
+            total = pick[s * experts : (s + 1) * experts].reshape(experts, hc, LANE).astype(BF16)
+            out_ref[:, s * hc // 2 : (s + 1) * hc // 2] = total.reshape(experts, hc // 2, 2, LANE)
+        mixed = jnp.broadcast_to(mixed, (slots, LANE))
+        high_mixed = mixed.astype(BF16).astype(F32)
+        lane = iota((experts, LANE), 1)
+        line = jnp.zeros((experts, LANE), F32)
+        for s in range(cap):
+            span = slice(s * experts, (s + 1) * experts)
+            line = jnp.where(lane == s, high_mixed[span], line)
+            line = jnp.where(lane == LANE // 2 + s, mixed[span] - high_mixed[span], line)
+        line = jnp.stack([line, jnp.zeros((experts, LANE), F32)], axis=1)
+        out_ref[:, back // 2 - 1 :] = line.reshape(experts, 1, 2, LANE).astype(BF16)
+
+    x_other, joined, packed = pl.pallas_call(
         grads_kernel,
         out_shape=(
             pltpu.VMEM((slots, half), BF16),
             pltpu.VMEM((slots, 2 * fh), BF16),
-            pltpu.VMEM((slots, half + LANE), BF16),
-            pltpu.VMEM((slots, LANE), F32),
+            jax.ShapeDtypeStruct((experts, back // 2, 2, LANE), BF16),
         ),
-        in_specs=[vspec(), aspec(), vspec()],
-        out_specs=(vspec(),) * 4,
+        in_specs=[vspec(), aspec(), aspec(), vspec(), vspec()],
+        out_specs=(vspec(),) * 3,
         scratch_shapes=[
             pltpu.VMEM((experts * (disp + 1), LANE), F32),
             pltpu.VMEM((slots, half), BF16),
-            pltpu.VMEM((3, half, fh), BF16),
-            pltpu.SemaphoreType.DMA(()),
+            pltpu.VMEM((3, half, 2 * fh), BF16),
+            pltpu.SemaphoreType.DMA((2,)),
         ],
         compiler_params=params(),
         name="grads",
-    )(vm(recv_other), hb(full), vm(pre))
-
-    sent = lax.ppermute(send, "pair", swap)
-
-    def keep_kernel(joined_ref, w_ref, keep_ref):
-        keep_ref[...] = dot_nt(joined_ref[:, :fh], w_ref[0]) + dot_nt(joined_ref[:, fh:], w_ref[1])
-
-    keep = pl.pallas_call(
-        keep_kernel,
-        out_shape=pltpu.VMEM((slots, half), F32),
-        in_specs=[vspec()] * 2,
-        out_specs=vspec(),
-        compiler_params=params(),
-        name="keep",
-    )(vm(joined), vm(w_own))
+    )(vm(recv_other), hb(full), hb(full_other), vm(pre), vm(w_own))
 
     def weight_kernel(own_ref, oth_ref, joined_ref, mine, next_low, next_high, far_low, far_high, prev_low, prev_high, x_all):
         p = pair_id()
@@ -439,33 +440,6 @@
     sum_low = lax.ppermute(sum_low, "dp", ahead)
     sum_high = lax.ppermute(sum_high, "dp", behind)
 
-    def pack_kernel(keep_ref, mixed_ref, sent_ref, out_ref):
-        for s in range(cap):
-            span = slice(s * experts, (s + 1) * experts)
-            total = keep_ref[span, :] + sent_ref[span, :half].astype(F32)
-            total = total.reshape(experts, hc, LANE).astype(BF16)
-            out_ref[:, s * hc // 2 : (s + 1) * hc // 2] = total.reshape(experts, hc // 2, 2, LANE)
-        tail = sent_ref[:, half:].astype(F32)
-        full_mixed = mixed_ref[...] + tail + pltpu.roll(tail, LANE // 2, 1)
-        high_mixed = full_mixed.astype(BF16).astype(F32)
-        lane = iota((experts, LANE), 1)
-        line = jnp.zeros((experts, LANE), F32)
-        for s in range(cap):
-            span = slice(s * experts, (s + 1) * experts)
-            line = jnp.where(lane == s, high_mixed[span], line)
-            line = jnp.where(lane == LANE // 2 + s, full_mixed[span] - high_mixed[span], line)
-        line = jnp.stack([line, jnp.zeros((experts, LANE), F32)], axis=1)
-        out_ref[:, back // 2 - 1 :] = line.reshape(experts, 1, 2, LANE).astype(BF16)
-
-    packed = pl.pallas_call(
-        pack_kernel,
-        out_shape=jax.ShapeDtypeStruct((experts, back // 2, 2, LANE), BF16),
-        in_specs=[vspec()] * 3,
-        out_specs=vspec(),
-        compiler_params=params(),
-        name="pack",
-    )(vm(keep), vm(mixed), vm(sent))
-
     returned = exchange(packed)
 
     def total_kernel(mine_ref, a_ref, b_ref, c_ref, d_ref, gate_ref, up_ref):

time: 206 us -> 156 us (0.76)
  blocking collectives: 79.6 us -> 0 us
  starting transfers between devices: 60 us -> 80.2 us
  waiting for transfers between devices: 40.1 us -> 47 us
  Pallas kernels: 24.6 us -> 27.1 us
    all_to_all x1 -> x0, blocking collectives: 79.6 us -> none  [exchange(): return lax.all_to_all(x, 'expert', split_axis=0, concat_axis=0, tiled=True)]
    all_to_all x1 -> x2, starting transfers between devices: 6.43 us -> 25.7 us  [exchange(): return lax.all_to_all(x, 'expert', split_axis=0, concat_axis=0, tiled=True)]
    all_to_all x1 -> x2, waiting for transfers between devices: 8.11 us -> 16.5 us  [exchange(): return lax.all_to_all(x, 'expert', split_axis=0, concat_axis=0, tiled=True)]
    pallas_call x1, Pallas kernels: 3.74 us -> 7.52 us  [local(): pl.pallas_call(grads_kernel, out_shape=(pltpu.VMEM((slots, half), BF16),...]
    pallas_call x2 -> x0, Pallas kernels: 2.57 us -> none  [the longest x1 1.7 us: local(): pl.pallas_call(pack_kernel, out_shape=jax.ShapeDtypeStruct((experts, back...]
  transfers between devices with their start and end apart: 16 -> 17, of which waited for: 7 -> 7; matrix products, arithmetic and copies ran while one was open for 0% -> 0% of each run, Pallas kernels for 7% -> 10%
where the time goes in v5:
time: 156 us; the launch traced here: 155 us
  starting transfers between devices  80.2 us (51%)
  waiting for transfers between devices  47 us (30%)
  Pallas kernels  27.1 us (17%)
    all_to_all x2, starting transfers between devices, exchange(): return lax.all_to_all(x, 'expert', split_axis=0, concat_axis=0, tiled=True)  25.7 us
    all_to_all x2, waiting for transfers between devices, exchange(): return lax.all_to_all(x, 'expert', split_axis=0, concat_axis=0, tiled=True)  16.5 us
    ppermute x1, waiting for transfers between devices, local(): low_far = lax.ppermute(low_prev, 'dp', ahead)  11.1 us
    ppermute x1, waiting for transfers between devices, local(): low_next = lax.ppermute(low, 'dp', behind)  7.71 us
    pallas_call x1, Pallas kernels, local(): pl.pallas_call(grads_kernel, out_shape=(pltpu.VMEM((slots, half), BF16),...  7.52 us
    ppermute x1, starting transfers between devices, local(): recv_other = lax.ppermute(recv, 'pair', swap)  7.52 us
    ppermute x1, waiting for transfers between devices, local(): low_prev = lax.ppermute(low, 'dp', ahead)  5.33 us
    ppermute x1, starting transfers between devices, local(): row_half_other = lax.ppermute(row_half, 'pair', swap)  5.12 us
  transfers between devices with their start and end apart: 17, of which 7 were waited for; matrix products, arithmetic and copies ran while one was open for 0% of the time, Pallas kernels for 10%

profile of v5, /device:TPU:1, one launch (start us, length us, event | category | flops | bytes accessed | tf_op | source)
XLA Modules:
  0.0 155.1 jit_solution(15674339140180032000)
XLA Ops:
  0.6 3.8 %dispatch.1 = (bf16[64,80,128]{2,1,0:T(8,128)(2,1)}, f32[8,128]{1,0:T(8,128)S(1)}) custom-call(bf16[256,2048]{1,0:T(8,128)(2,1)} %bytes_hbm.1, s32[1,128]{1,0:T(1,128)} %bitcast.9, s32[2,128]{1,0:T(2,128)} %bitcast.8, bf16[128,2048]{1,0:T(8,128)(2,1)} %cot_hbm.1, bf16[64,2048]{1,0:T(8,128)(2,1)} %bitcast.6), custom_call_target="tpu_custom_call" | custom-call | tf_op jit(solution)/shard_map/dispatch/pallas_call | solution.py:144
  4.4 19.1 %all-to-all-start = ((bf16[64,80,128]{2,1,0:T(8,128)(2,1)}), bf16[64,80,128]{2,1,0:T(8,128)(2,1)S(1)}, u32[]{:S(2)}, u32[]{:S(2)}) async-start(bf16[64,80,128]{2,1,0:T(8,128)(2,1)} %get-tuple-element.27), calls=%async_computation | async-start | bytes 2621440 | tf_op jit(solution)/shard_map/all_to_all | solution.py:174
  23.5 1.4 stack.1
  24.9 3.2 %collective-permute-start.3 = (bf16[3,256,384]{2,1,0:T(8,128)(2,1)S(1)}, bf16[3,256,384]{2,1,0:T(8,128)(2,1)S(1)}, u32[]{:S(2)}, u32[]{:S(2)}) collective-permute-start(bf16[3,256,384]{2,1,0:T(8,128)(2,1)S(1)} %get-tuple-element.28.refs_0_), channel_id=1, source_target_pairs={{0,2},{2,4},{4,6},{6,0},{1,3},{3,5},{5,7},{7,1},{8,10},{10,12},{12... | collective-permute-start | bytes 1769480 | tf_op jit(solution)/shard_map/ppermute | solution.py:249
  28.1 3.4 %collective-permute-start.2 = (bf16[3,256,384]{2,1,0:T(8,128)(2,1)S(1)}, bf16[3,256,384]{2,1,0:T(8,128)(2,1)S(1)}, u32[]{:S(2)}, u32[]{:S(2)}) collective-permute-start(bf16[3,256,384]{2,1,0:T(8,128)(2,1)S(1)} %get-tuple-element.29.refs_1_), channel_id=1, source_target_pairs={{0,6},{2,0},{4,2},{6,4},{1,7},{3,1},{5,3},{7,5},{8,14},{10,8},{12,... | collective-permute-start | bytes 1769480 | tf_op jit(solution)/shard_map/ppermute | solution.py:250
  31.5 3.4 %collective-permute-start.1 = (bf16[3,256,384]{2,1,0:T(8,128)(2,1)S(1)}, bf16[3,256,384]{2,1,0:T(8,128)(2,1)S(1)}, u32[]{:S(2)}, u32[]{:S(2)}) collective-permute-start(bf16[3,256,384]{2,1,0:T(8,128)(2,1)S(1)} %get-tuple-element.28.refs_0_), channel_id=1, source_target_pairs={{0,6},{2,0},{4,2},{6,4},{1,7},{3,1},{5,3},{7,5},{8,14},{10,8},{12,... | collective-permute-start | bytes 1769480 | tf_op jit(solution)/shard_map/ppermute | solution.py:252
  34.9 1.9 %collective-permute-start.6 = (bf16[3,256,384]{2,1,0:T(8,128)(2,1)S(1)}, bf16[3,256,384]{2,1,0:T(8,128)(2,1)S(1)}, u32[]{:S(2)}, u32[]{:S(2)}) collective-permute-start(bf16[3,256,384]{2,1,0:T(8,128)(2,1)S(1)} %get-tuple-element.29.refs_1_), channel_id=1, source_target_pairs={{0,2},{2,4},{4,6},{6,0},{1,3},{3,5},{5,7},{7,1},{8,10},{10,12},{12... | collective-permute-start | bytes 1769480 | tf_op jit(solution)/shard_map/ppermute | solution.py:251
  36.8 5.3 %collective-permute-done.3.refs_6_ = bf16[3,256,384]{2,1,0:T(8,128)(2,1)S(1)} collective-permute-done((bf16[3,256,384]{2,1,0:T(8,128)(2,1)S(1)}, bf16[3,256,384]{2,1,0:T(8,128)(2,1)S(1)}, u32[]{:S(2)}, u32[]{:S(2)}) %collective-permute-start.3) | collective-permute-done | bytes 589856 | tf_op jit(solution)/shard_map/ppermute | solution.py:249
  42.1 1.9 %collective-permute-start.4 = (bf16[3,256,384]{2,1,0:T(8,128)(2,1)S(1)}, bf16[3,256,384]{2,1,0:T(8,128)(2,1)S(1)}, u32[]{:S(2)}, u32[]{:S(2)}) collective-permute-start(bf16[3,256,384]{2,1,0:T(8,128)(2,1)S(1)} %collective-permute-done.3.refs_6_), channel_id=1, source_target_pairs={{0,2},{2,4},{4,6},{6,0},{1,3},{3,5},{5,7},{7,1},{8,10},{10,12},{12... | collective-permute-start | bytes 1769480 | tf_op jit(solution)/shard_map/ppermute | solution.py:253
  44.1 0.0 collective-permute-done.2.refs_3_
  44.1 4.6 %collective-permute-start.5 = (bf16[3,256,384]{2,1,0:T(8,128)(2,1)S(1)}, bf16[3,256,384]{2,1,0:T(8,128)(2,1)S(1)}, u32[]{:S(2)}, u32[]{:S(2)}) collective-permute-start(bf16[3,256,384]{2,1,0:T(8,128)(2,1)S(1)} %collective-permute-done.2.refs_3_), channel_id=1, source_target_pairs={{0,6},{2,0},{4,2},{6,4},{1,7},{3,1},{5,3},{7,5},{8,14},{10,8},{12,... | collective-permute-start | bytes 1769480 | tf_op jit(solution)/shard_map/ppermute | solution.py:254
  48.7 7.7 %collective-permute-done.1.refs_2_ = bf16[3,256,384]{2,1,0:T(8,128)(2,1)S(1)} collective-permute-done((bf16[3,256,384]{2,1,0:T(8,128)(2,1)S(1)}, bf16[3,256,384]{2,1,0:T(8,128)(2,1)S(1)}, u32[]{:S(2)}, u32[]{:S(2)}) %collective-permute-start.1) | collective-permute-done | bytes 589856 | tf_op jit(solution)/shard_map/ppermute | solution.py:252
  56.4 0.0 collective-permute-done.6.refs_7_
  56.4 11.1 %collective-permute-done.4.refs_4_ = bf16[3,256,384]{2,1,0:T(8,128)(2,1)S(1)} collective-permute-done((bf16[3,256,384]{2,1,0:T(8,128)(2,1)S(1)}, bf16[3,256,384]{2,1,0:T(8,128)(2,1)S(1)}, u32[]{:S(2)}, u32[]{:S(2)}) %collective-permute-start.4) | collective-permute-done | bytes 589856 | tf_op jit(solution)/shard_map/ppermute | solution.py:253
  67.4 1.6 %collective-permute-done.5.refs_5_ = bf16[3,256,384]{2,1,0:T(8,128)(2,1)S(1)} collective-permute-done((bf16[3,256,384]{2,1,0:T(8,128)(2,1)S(1)}, bf16[3,256,384]{2,1,0:T(8,128)(2,1)S(1)}, u32[]{:S(2)}, u32[]{:S(2)}) %collective-permute-start.5) | collective-permute-done | bytes 589856 | tf_op jit(solution)/shard_map/ppermute | solution.py:254
  69.0 2.2 %assemble.1.own_hbm = bf16[3,2048,384]{2,1,0:T(8,128)(2,1)} custom-call(bf16[3,256,384]{2,1,0:T(8,128)(2,1)S(1)} %get-tuple-element.28.refs_0_, bf16[3,256,384]{2,1,0:T(8,128)(2,1)S(1)} %get-tuple-element.29.refs_1_, bf16[3,256,384]{2,1,0:T(8,128)(2,1)S(1)} %collective-permute-done.1.refs_2_, bf16[3,256,384]{2,1,0:T(8,128)(2,1)S(1)} %collective-permute-done.2.refs_3_, ...), custom_call_target="tpu_custom_call" | custom-call | tf_op jit(solution)/shard_map/assemble/pallas_call | solution.py:274
  71.3 4.0 %collective-permute-start.7 = (bf16[3,2048,384]{2,1,0:T(8,128)(2,1)}, bf16[3,2048,384]{2,1,0:T(8,128)(2,1)}, u32[]{:S(2)}, u32[]{:S(2)}) collective-permute-start(bf16[3,2048,384]{2,1,0:T(8,128)(2,1)} %assemble.1.own_hbm), channel_id=1, source_target_pairs={{0,1},{1,0},{2,3},{3,2},{4,5},{5,4},{6,7},{7,6},{8,9},{9,8},{10,11... | collective-permute-start | bytes 14155784 | tf_op jit(solution)/shard_map/ppermute | solution.py:285
  75.2 8.8 %all-to-all-done = bf16[64,80,128]{2,1,0:T(8,128)(2,1)S(1)} async-done(((bf16[64,80,128]{2,1,0:T(8,128)(2,1)}), bf16[64,80,128]{2,1,0:T(8,128)(2,1)S(1)}, u32[]{:S(2)}, u32[]{:S(2)}) %all-to-all-start) | async-done | bytes 1310752 | tf_op jit(solution)/shard_map/all_to_all | solution.py:174
  84.0 7.5 %collective-permute-start = (bf16[5120,128]{1,0:T(8,128)(2,1)S(1)}, bf16[5120,128]{1,0:T(8,128)(2,1)S(1)}, u32[]{:S(2)}, u32[]{:S(2)}) collective-permute-start(bf16[5120,128]{1,0:T(8,128)(2,1)S(1)} %bitcast.4), channel_id=1, source_target_pairs={{0,1},{1,0},{2,3},{3,2},{4,5},{5,4},{6,7},{7,6},{8,9},{9,8},{10,11... | collective-permute-start | bytes 3932168 | tf_op jit(solution)/shard_map/ppermute | solution.py:286
  91.6 0.0 collective-permute-done.7.oth_hbm
  91.6 4.1 %own.1 = (bf16[320,1024]{1,0:T(8,128)(2,1)S(1)}, f32[3,320,768]{2,1,0:T(8,128)S(1)}, bf16[3,1024,768]{2,1,0:T(8,128)(2,1)S(1)}) custom-call(bf16[5120,128]{1,0:T(8,128)(2,1)S(1)} %bitcast.5, bf16[3,2048,384]{2,1,0:T(8,128)(2,1)} %assemble.1.own_hbm, bf16[3,2048,384]{2,1,0:T(8,128)(2,1)} %collective-permute-done.7.oth_hbm), custom_call_target="tpu_custom_call" | custom-call | tf_op jit(solution)/shard_map/own/pallas_call | solution.py:321
  95.7 0.0 collective-permute-done.recv_ref
  95.7 7.5 %grads.1 = (bf16[320,1024]{1,0:T(8,128)(2,1)S(1)}, bf16[320,768]{1,0:T(8,128)(2,1)S(1)}, bf16[64,21,2,128]{3,2,1,0:T(2,128)(2,1)}) custom-call(bf16[5120,128]{1,0:T(8,128)(2,1)S(1)} %collective-permute-done.recv_ref, bf16[3,2048,384]{2,1,0:T(8,128)(2,1)} %assemble.1.own_hbm, bf16[3,2048,384]{2,1,0:T(8,128)(2,1)} %collective-permute-done.7.oth_hbm, ...), custom_call_target="tpu_custom_call" | custom-call | tf_op jit(solution)/shard_map/grads/pallas_call | solution.py:376
  103.2 0.0 copy-start
  103.2 6.6 %all-to-all-start.1 = ((bf16[64,21,2,128]{3,2,1,0:T(2,128)(2,1)}), bf16[64,21,2,128]{3,2,1,0:T(2,128)(2,1)S(1)}, u32[]{:S(2)}, u32[]{:S(2)}) async-start(bf16[64,21,2,128]{3,2,1,0:T(2,128)(2,1)} %get-tuple-element.32), calls=%async_computation.1 | async-start | bytes 1376256 | tf_op jit(solution)/shard_map/all_to_all | solution.py:174
  109.8 2.3 %weight.1 = (bf16[512,768]{1,0:T(8,128)(2,1)S(1)}, bf16[256,768]{1,0:T(8,128)(2,1)S(1)}, bf16[256,768]{1,0:T(8,128)(2,1)}, bf16[256,768]{1,0:T(8,128)(2,1)S(1)},...) custom-call(bf16[320,1024]{1,0:T(8,128)(2,1)S(1)} %get-tuple-element.37.own_ref, ...), custom_call_target="tpu_custom_call" | custom-call | tf_op jit(solution)/shard_map/weight/pallas_call | solution.py:411
  112.2 4.6 %collective-permute-start.10 = (bf16[256,768]{1,0:T(8,128)(2,1)S(1)}, bf16[256,768]{1,0:T(8,128)(2,1)S(1)}, u32[]{:S(2)}, u32[]{:S(2)}) collective-permute-start(bf16[256,768]{1,0:T(8,128)(2,1)S(1)} %get-tuple-element.44), channel_id=1, source_target_pairs={{0,6},{2,0},{4,2},{6,4},{1,7},{3,1},{5,3},{7,5},{8,14},{10,8},{12,... | collective-permute-start | bytes 1179656 | tf_op jit(solution)/shard_map/ppermute | solution.py:423
  116.8 1.9 %collective-permute-start.9 = (bf16[256,768]{1,0:T(8,128)(2,1)S(1)}, bf16[256,768]{1,0:T(8,128)(2,1)S(1)}, u32[]{:S(2)}, u32[]{:S(2)}) collective-permute-start(bf16[256,768]{1,0:T(8,128)(2,1)S(1)} %get-tuple-element.42), channel_id=1, source_target_pairs={{0,2},{2,4},{4,6},{6,0},{1,3},{3,5},{5,7},{7,1},{8,10},{10,12},{12... | collective-permute-start | bytes 1179656 | tf_op jit(solution)/shard_map/ppermute | solution.py:422
  118.7 4.6 %collective-permute-start.12 = (bf16[256,768]{1,0:T(8,128)(2,1)}, bf16[256,768]{1,0:T(8,128)(2,1)S(1)}, u32[]{:S(2)}, u32[]{:S(2)}) collective-permute-start(bf16[256,768]{1,0:T(8,128)(2,1)} %get-tuple-element.46), channel_id=1, source_target_pairs={{0,6},{2,0},{4,2},{6,4},{1,7},{3,1},{5,3},{7,5},{8,14},{10,8},{12,... | collective-permute-start | bytes 1179656 | tf_op jit(solution)/shard_map/ppermute | solution.py:425
  123.3 1.9 %collective-permute-start.13 = (bf16[256,768]{1,0:T(8,128)(2,1)}, bf16[256,768]{1,0:T(8,128)(2,1)S(1)}, u32[]{:S(2)}, u32[]{:S(2)}) collective-permute-start(bf16[256,768]{1,0:T(8,128)(2,1)} %get-tuple-element.47), channel_id=1, source_target_pairs={{0,2},{2,4},{4,6},{6,0},{1,3},{3,5},{5,7},{7,1},{8,10},{10,12},{12... | collective-permute-start | bytes 1179656 | tf_op jit(solution)/shard_map/ppermute | solution.py:424
  125.2 0.0 collective-permute-done.10.d_ref
  125.2 4.8 %collective-permute-done.9.b_ref = bf16[256,768]{1,0:T(8,128)(2,1)S(1)} collective-permute-done((bf16[256,768]{1,0:T(8,128)(2,1)S(1)}, bf16[256,768]{1,0:T(8,128)(2,1)S(1)}, u32[]{:S(2)}, u32[]{:S(2)}) %collective-permute-start.9) | collective-permute-done | bytes 393248 | tf_op jit(solution)/shard_map/ppermute | solution.py:422
  130.0 1.0 add.1
  131.0 1.9 %collective-permute-start.11 = (bf16[256,768]{1,0:T(8,128)(2,1)}, bf16[256,768]{1,0:T(8,128)(2,1)S(1)}, u32[]{:S(2)}, u32[]{:S(2)}) collective-permute-start(bf16[256,768]{1,0:T(8,128)(2,1)} %get-tuple-element.45), channel_id=1, source_target_pairs={{0,2},{2,4},{4,6},{6,0},{1,3},{3,5},{5,7},{7,1},{8,10},{10,12},{12... | collective-permute-start | bytes 1179656 | tf_op jit(solution)/shard_map/ppermute | solution.py:440
  132.9 4.6 %collective-permute-start.14 = (bf16[256,768]{1,0:T(8,128)(2,1)}, bf16[256,768]{1,0:T(8,128)(2,1)S(1)}, u32[]{:S(2)}, u32[]{:S(2)}) collective-permute-start(bf16[256,768]{1,0:T(8,128)(2,1)} %get-tuple-element.48), channel_id=1, source_target_pairs={{0,6},{2,0},{4,2},{6,4},{1,7},{3,1},{5,3},{7,5},{8,14},{10,8},{12,... | collective-permute-start | bytes 1179656 | tf_op jit(solution)/shard_map/ppermute | solution.py:441
  137.5 0.0 copy-done
  137.5 1.1 aux.1
  138.6 7.8 %all-to-all-done.1.back_ref = bf16[64,21,2,128]{3,2,1,0:T(2,128)(2,1)S(1)} async-done(((bf16[64,21,2,128]{3,2,1,0:T(2,128)(2,1)}), bf16[64,21,2,128]{3,2,1,0:T(2,128)(2,1)S(1)}, u32[]{:S(2)}, u32[]{:S(2)}) %all-to-all-start.1) | async-done | bytes 688160 | tf_op jit(solution)/shard_map/all_to_all | solution.py:174
  146.4 1.7 %combine.1.own_ref = bf16[128,1024]{1,0:T(8,128)(2,1)S(1)} custom-call(bf16[64,21,2,128]{3,2,1,0:T(2,128)(2,1)S(1)} %all-to-all-done.1.back_ref, bf16[256,384]{1,0:T(8,128)(2,1)} %get-tuple-element.34.hot_hbm, f32[128,1024]{1,0:T(8,128)} %get-tuple-element.35.delta_hbm, f32[128,128]{1,0:T(8,128)} %get-tuple-element.36.mix_hbm), custom_call_target="tpu_custom_call" | custom-call | tf_op jit(solution)/shard_map/combine/pallas_call | solution.py:490
  148.1 5.1 %collective-permute-start.8 = (bf16[128,1024]{1,0:T(8,128)(2,1)S(1)}, bf16[128,1024]{1,0:T(8,128)(2,1)S(1)}, u32[]{:S(2)}, u32[]{:S(2)}) collective-permute-start(bf16[128,1024]{1,0:T(8,128)(2,1)S(1)} %combine.1.own_ref), channel_id=1, source_target_pairs={{0,1},{1,0},{2,3},{3,2},{4,5},{5,4},{6,7},{7,6},{8,9},{9,8},{10,11... | collective-permute-start | bytes 786440 | tf_op jit(solution)/shard_map/ppermute | solution.py:507
  153.2 0.0 collective-permute-done.12.b_ref
  153.2 0.0 collective-permute-done.13.c_ref
  153.2 0.0 collective-permute-done.11.a_ref
  153.2 0.0 collective-permute-done.14.d_ref
  153.2 1.1 total.1
  154.3 0.0 collective-permute-done.8.oth_ref
  154.3 0.8 join.1
Async XLA Ops:
  4.4 79.6 %all-to-all-start = ((bf16[64,80,128]{2,1,0:T(8,128)(2,1)}), bf16[64,80,128]{2,1,0:T(8,128)(2,1)S(1)}, u32[]{:S(2)}, u32[]{:S(2)}) async-start(bf16[64,80,128]{2,1,0:T(8,128)(2,1)} %get-tuple-element.27), calls=%async_computation | async-start | bytes 2621440 | tf_op jit(solution)/shard_map/all_to_all | solution.py:174
  24.9 17.2 %collective-permute-start.3 = (bf16[3,256,384]{2,1,0:T(8,128)(2,1)S(1)}, bf16[3,256,384]{2,1,0:T(8,128)(2,1)S(1)}, u32[]{:S(2)}, u32[]{:S(2)}) collective-permute-start(bf16[3,256,384]{2,1,0:T(8,128)(2,1)S(1)} %get-tuple-element.28.refs_0_), channel_id=1, source_target_pairs={{0,2},{2,4},{4,6},{6,0},{1,3},{3,5},{5,7},{7,1},{8,10},{10,12},{12... | collective-permute-start | bytes 1769480 | tf_op jit(solution)/shard_map/ppermute | solution.py:249
  28.1 15.9 %collective-permute-start.2 = (bf16[3,256,384]{2,1,0:T(8,128)(2,1)S(1)}, bf16[3,256,384]{2,1,0:T(8,128)(2,1)S(1)}, u32[]{:S(2)}, u32[]{:S(2)}) collective-permute-start(bf16[3,256,384]{2,1,0:T(8,128)(2,1)S(1)} %get-tuple-element.29.refs_1_), channel_id=1, source_target_pairs={{0,6},{2,0},{4,2},{6,4},{1,7},{3,1},{5,3},{7,5},{8,14},{10,8},{12,... | collective-permute-start | bytes 1769480 | tf_op jit(solution)/shard_map/ppermute | solution.py:250
  31.5 24.8 %collective-permute-start.1 = (bf16[3,256,384]{2,1,0:T(8,128)(2,1)S(1)}, bf16[3,256,384]{2,1,0:T(8,128)(2,1)S(1)}, u32[]{:S(2)}, u32[]{:S(2)}) collective-permute-start(bf16[3,256,384]{2,1,0:T(8,128)(2,1)S(1)} %get-tuple-element.28.refs_0_), channel_id=1, source_target_pairs={{0,6},{2,0},{4,2},{6,4},{1,7},{3,1},{5,3},{7,5},{8,14},{10,8},{12,... | collective-permute-start | bytes 1769480 | tf_op jit(solution)/shard_map/ppermute | solution.py:252
  34.9 21.5 %collective-permute-start.6 = (bf16[3,256,384]{2,1,0:T(8,128)(2,1)S(1)}, bf16[3,256,384]{2,1,0:T(8,128)(2,1)S(1)}, u32[]{:S(2)}, u32[]{:S(2)}) collective-permute-start(bf16[3,256,384]{2,1,0:T(8,128)(2,1)S(1)} %get-tuple-element.29.refs_1_), channel_id=1, source_target_pairs={{0,2},{2,4},{4,6},{6,0},{1,3},{3,5},{5,7},{7,1},{8,10},{10,12},{12... | collective-permute-start | bytes 1769480 | tf_op jit(solution)/shard_map/ppermute | solution.py:251
  42.1 25.3 %collective-permute-start.4 = (bf16[3,256,384]{2,1,0:T(8,128)(2,1)S(1)}, bf16[3,256,384]{2,1,0:T(8,128)(2,1)S(1)}, u32[]{:S(2)}, u32[]{:S(2)}) collective-permute-start(bf16[3,256,384]{2,1,0:T(8,128)(2,1)S(1)} %collective-permute-done.3.refs_6_), channel_id=1, source_target_pairs={{0,2},{2,4},{4,6},{6,0},{1,3},{3,5},{5,7},{7,1},{8,10},{10,12},{12... | collective-permute-start | bytes 1769480 | tf_op jit(solution)/shard_map/ppermute | solution.py:253
  44.1 24.9 %collective-permute-start.5 = (bf16[3,256,384]{2,1,0:T(8,128)(2,1)S(1)}, bf16[3,256,384]{2,1,0:T(8,128)(2,1)S(1)}, u32[]{:S(2)}, u32[]{:S(2)}) collective-permute-start(bf16[3,256,384]{2,1,0:T(8,128)(2,1)S(1)} %collective-permute-done.2.refs_3_), channel_id=1, source_target_pairs={{0,6},{2,0},{4,2},{6,4},{1,7},{3,1},{5,3},{7,5},{8,14},{10,8},{12,... | collective-permute-start | bytes 1769480 | tf_op jit(solution)/shard_map/ppermute | solution.py:254
  71.3 20.3 %collective-permute-start.7 = (bf16[3,2048,384]{2,1,0:T(8,128)(2,1)}, bf16[3,2048,384]{2,1,0:T(8,128)(2,1)}, u32[]{:S(2)}, u32[]{:S(2)}) collective-permute-start(bf16[3,2048,384]{2,1,0:T(8,128)(2,1)} %assemble.1.own_hbm), channel_id=1, source_target_pairs={{0,1},{1,0},{2,3},{3,2},{4,5},{5,4},{6,7},{7,6},{8,9},{9,8},{10,11... | collective-permute-start | bytes 14155784 | tf_op jit(solution)/shard_map/ppermute | solution.py:285
  84.0 11.7 %collective-permute-start = (bf16[5120,128]{1,0:T(8,128)(2,1)S(1)}, bf16[5120,128]{1,0:T(8,128)(2,1)S(1)}, u32[]{:S(2)}, u32[]{:S(2)}) collective-permute-start(bf16[5120,128]{1,0:T(8,128)(2,1)S(1)} %bitcast.4), channel_id=1, source_target_pairs={{0,1},{1,0},{2,3},{3,2},{4,5},{5,4},{6,7},{7,6},{8,9},{9,8},{10,11... | collective-permute-start | bytes 3932168 | tf_op jit(solution)/shard_map/ppermute | solution.py:286
  103.2 34.3 %copy-start = (bf16[2048,64]{0,1:T(8,128)(2,1)S(1)}, bf16[2048,64]{0,1:T(8,128)(2,1)}, u32[]{:S(2)}) copy-start(bf16[2048,64]{0,1:T(8,128)(2,1)} %param.12) | copy-start | bytes 786436
  103.2 43.1 %all-to-all-start.1 = ((bf16[64,21,2,128]{3,2,1,0:T(2,128)(2,1)}), bf16[64,21,2,128]{3,2,1,0:T(2,128)(2,1)S(1)}, u32[]{:S(2)}, u32[]{:S(2)}) async-start(bf16[64,21,2,128]{3,2,1,0:T(2,128)(2,1)} %get-tuple-element.32), calls=%async_computation.1 | async-start | bytes 1376256 | tf_op jit(solution)/shard_map/all_to_all | solution.py:174
  112.2 13.1 %collective-permute-start.10 = (bf16[256,768]{1,0:T(8,128)(2,1)S(1)}, bf16[256,768]{1,0:T(8,128)(2,1)S(1)}, u32[]{:S(2)}, u32[]{:S(2)}) collective-permute-start(bf16[256,768]{1,0:T(8,128)(2,1)S(1)} %get-tuple-element.44), channel_id=1, source_target_pairs={{0,6},{2,0},{4,2},{6,4},{1,7},{3,1},{5,3},{7,5},{8,14},{10,8},{12,... | collective-permute-start | bytes 1179656 | tf_op jit(solution)/shard_map/ppermute | solution.py:423
  116.8 13.2 %collective-permute-start.9 = (bf16[256,768]{1,0:T(8,128)(2,1)S(1)}, bf16[256,768]{1,0:T(8,128)(2,1)S(1)}, u32[]{:S(2)}, u32[]{:S(2)}) collective-permute-start(bf16[256,768]{1,0:T(8,128)(2,1)S(1)} %get-tuple-element.42), channel_id=1, source_target_pairs={{0,2},{2,4},{4,6},{6,0},{1,3},{3,5},{5,7},{7,1},{8,10},{10,12},{12... | collective-permute-start | bytes 1179656 | tf_op jit(solution)/shard_map/ppermute | solution.py:422
  118.7 34.5 %collective-permute-start.12 = (bf16[256,768]{1,0:T(8,128)(2,1)}, bf16[256,768]{1,0:T(8,128)(2,1)S(1)}, u32[]{:S(2)}, u32[]{:S(2)}) collective-permute-start(bf16[256,768]{1,0:T(8,128)(2,1)} %get-tuple-element.46), channel_id=1, source_target_pairs={{0,6},{2,0},{4,2},{6,4},{1,7},{3,1},{5,3},{7,5},{8,14},{10,8},{12,... | collective-permute-start | bytes 1179656 | tf_op jit(solution)/shard_map/ppermute | solution.py:425
  123.3 29.9 %collective-permute-start.13 = (bf16[256,768]{1,0:T(8,128)(2,1)}, bf16[256,768]{1,0:T(8,128)(2,1)S(1)}, u32[]{:S(2)}, u32[]{:S(2)}) collective-permute-start(bf16[256,768]{1,0:T(8,128)(2,1)} %get-tuple-element.47), channel_id=1, source_target_pairs={{0,2},{2,4},{4,6},{6,0},{1,3},{3,5},{5,7},{7,1},{8,10},{10,12},{12... | collective-permute-start | bytes 1179656 | tf_op jit(solution)/shard_map/ppermute | solution.py:424
  131.0 22.2 %collective-permute-start.11 = (bf16[256,768]{1,0:T(8,128)(2,1)}, bf16[256,768]{1,0:T(8,128)(2,1)S(1)}, u32[]{:S(2)}, u32[]{:S(2)}) collective-permute-start(bf16[256,768]{1,0:T(8,128)(2,1)} %get-tuple-element.45), channel_id=1, source_target_pairs={{0,2},{2,4},{4,6},{6,0},{1,3},{3,5},{5,7},{7,1},{8,10},{10,12},{12... | collective-permute-start | bytes 1179656 | tf_op jit(solution)/shard_map/ppermute | solution.py:440
  132.9 20.3 %collective-permute-start.14 = (bf16[256,768]{1,0:T(8,128)(2,1)}, bf16[256,768]{1,0:T(8,128)(2,1)S(1)}, u32[]{:S(2)}, u32[]{:S(2)}) collective-permute-start(bf16[256,768]{1,0:T(8,128)(2,1)} %get-tuple-element.48), channel_id=1, source_target_pairs={{0,6},{2,0},{4,2},{6,4},{1,7},{3,1},{5,3},{7,5},{8,14},{10,8},{12,... | collective-permute-start | bytes 1179656 | tf_op jit(solution)/shard_map/ppermute | solution.py:441
  148.1 6.3 %collective-permute-start.8 = (bf16[128,1024]{1,0:T(8,128)(2,1)S(1)}, bf16[128,1024]{1,0:T(8,128)(2,1)S(1)}, u32[]{:S(2)}, u32[]{:S(2)}) collective-permute-start(bf16[128,1024]{1,0:T(8,128)(2,1)S(1)} %combine.1.own_ref), channel_id=1, source_target_pairs={{0,1},{1,0},{2,3},{3,2},{4,5},{5,4},{6,7},{7,6},{8,9},{9,8},{10,11... | collective-permute-start | bytes 786440 | tf_op jit(solution)/shard_map/ppermute | solution.py:507

commit v6 on v5

--- a/solution.py
+++ b/solution.py
@@ -300,23 +300,31 @@
 
     def fetch(own_hbm, oth_hbm, w_buf, sems, h):
         row = pl.multiple_of(h * half, half)
-        return [
-            pltpu.make_async_copy(
-                src.at[:, pl.ds(row, half), :], w_buf.at[:, :, pl.ds(i * fh, fh)], sems.at[i]
-            )
-            for i, src in enumerate((own_hbm, oth_hbm))
+        loads = [
+            [
+                pltpu.make_async_copy(
+                    src.at[k, pl.ds(row, half), :], w_buf.at[k, :, pl.ds(i * fh, fh)], sems.at[k, i]
+                )
+                for i, src in enumerate((own_hbm, oth_hbm))
+            ]
+            for k in range(3)
         ]
+        for two in loads:
+            for load in two:
+                load.start()
+        return loads
+
+    def project(loads, k, x, w_buf):
+        for load in loads[k]:
+            load.wait()
+        return dot(x, w_buf[k])
 
     def own_kernel(recv_ref, own_hbm, oth_hbm, x_ref, pre_ref, w_buf, wide, s_buf, sems):
         loads = fetch(own_hbm, oth_hbm, w_buf, sems, pair_id())
-        for load in loads:
-            load.start()
         unpack(recv_ref, wide, x_ref, s_buf)
-        for load in loads:
-            load.wait()
-        pre_ref[0] = dot(x_ref[...], w_buf[0])
-        pre_ref[1] = dot(x_ref[...], w_buf[1])
-        pre_ref[2] = dot(s_buf[...], w_buf[2])
+        pre_ref[0] = project(loads, 0, x_ref[...], w_buf)
+        pre_ref[1] = project(loads, 1, x_ref[...], w_buf)
+        pre_ref[2] = project(loads, 2, s_buf[...], w_buf)
 
     x_own, pre, w_own = pl.pallas_call(
         own_kernel,
@@ -330,7 +338,7 @@
         scratch_shapes=[
             pltpu.VMEM((experts * (disp + 1), LANE), F32),
             pltpu.VMEM((slots, half), BF16),
-            pltpu.SemaphoreType.DMA((2,)),
+            pltpu.SemaphoreType.DMA((3, 2)),
         ],
         compiler_params=params(),
         name="own",
@@ -341,14 +349,10 @@
         wide, s_buf, w_buf, sems,
     ):
         loads = fetch(own_hbm, oth_hbm, w_buf, sems, 1 - pair_id())
-        for load in loads:
-            load.start()
         unpack(recv_ref, wide, x_ref, s_buf)
-        for load in loads:
-            load.wait()
-        gate = pre_ref[0] + dot(x_ref[...], w_buf[0])
-        up = pre_ref[1] + dot(x_ref[...], w_buf[1])
-        grad = pre_ref[2] + dot(s_buf[...], w_buf[2])
+        gate = pre_ref[0] + project(loads, 0, x_ref[...], w_buf)
+        up = pre_ref[1] + project(loads, 1, x_ref[...], w_buf)
+        grad = pre_ref[2] + project(loads, 2, s_buf[...], w_buf)
         sigma = jax.nn.sigmoid(gate)
         activ = gate * sigma
         slope = sigma * (1.0 + gate * (1.0 - sigma))
@@ -386,7 +390,7 @@
             pltpu.VMEM((experts * (disp + 1), LANE), F32),
             pltpu.VMEM((slots, half), BF16),
             pltpu.VMEM((3, half, 2 * fh), BF16),
-            pltpu.SemaphoreType.DMA((2,)),
+            pltpu.SemaphoreType.DMA((3, 2)),
         ],
         compiler_params=params(),
         name="grads",

time: 156 us -> 156 us (level)
  no operation moved by 1% of the time
where the time goes in v6:
time: 156 us; the launch traced here: 155 us
  starting transfers between devices  80.1 us (51%)
  waiting for transfers between devices  46.9 us (30%)
  Pallas kernels  26.7 us (17%)
    all_to_all x2, starting transfers between devices, exchange(): return lax.all_to_all(x, 'expert', split_axis=0, concat_axis=0, tiled=True)  25.9 us
    all_to_all x2, waiting for transfers between devices, exchange(): return lax.all_to_all(x, 'expert', split_axis=0, concat_axis=0, tiled=True)  16.5 us
    ppermute x1, waiting for transfers between devices, local(): low_far = lax.ppermute(low_prev, 'dp', ahead)  11.1 us
    ppermute x1, waiting for transfers between devices, local(): low_next = lax.ppermute(low, 'dp', behind)  7.71 us
    ppermute x1, starting transfers between devices, local(): recv_other = lax.ppermute(recv, 'pair', swap)  7.52 us
    pallas_call x1, Pallas kernels, local(): pl.pallas_call(grads_kernel, out_shape=(pltpu.VMEM((slots, half), BF16),...  7.37 us
    ppermute x1, waiting for transfers between devices, local(): low_prev = lax.ppermute(low, 'dp', ahead)  5.33 us
    ppermute x1, starting transfers between devices, local(): row_half_other = lax.ppermute(row_half, 'pair', swap)  4.9 us
  transfers between devices with their start and end apart: 17, of which 7 were waited for; matrix products, arithmetic and copies ran while one was open for 0% of the time, Pallas kernels for 10%

profile of v6, /device:TPU:1, one launch (start us, length us, event | category | flops | bytes accessed | tf_op | source)
XLA Modules:
  0.0 154.9 jit_solution(14959807276037375004)
XLA Ops:
  0.6 3.8 %dispatch.1 = (bf16[64,80,128]{2,1,0:T(8,128)(2,1)}, f32[8,128]{1,0:T(8,128)S(1)}) custom-call(bf16[256,2048]{1,0:T(8,128)(2,1)} %bytes_hbm.1, s32[1,128]{1,0:T(1,128)} %bitcast.9, s32[2,128]{1,0:T(2,128)} %bitcast.8, bf16[128,2048]{1,0:T(8,128)(2,1)} %cot_hbm.1, bf16[64,2048]{1,0:T(8,128)(2,1)} %bitcast.6), custom_call_target="tpu_custom_call" | custom-call | tf_op jit(solution)/shard_map/dispatch/pallas_call | solution.py:144
  4.4 19.1 %all-to-all-start = ((bf16[64,80,128]{2,1,0:T(8,128)(2,1)}), bf16[64,80,128]{2,1,0:T(8,128)(2,1)S(1)}, u32[]{:S(2)}, u32[]{:S(2)}) async-start(bf16[64,80,128]{2,1,0:T(8,128)(2,1)} %get-tuple-element.27), calls=%async_computation | async-start | bytes 2621440 | tf_op jit(solution)/shard_map/all_to_all | solution.py:174
  23.5 1.4 stack.1
  24.9 3.2 %collective-permute-start.3 = (bf16[3,256,384]{2,1,0:T(8,128)(2,1)S(1)}, bf16[3,256,384]{2,1,0:T(8,128)(2,1)S(1)}, u32[]{:S(2)}, u32[]{:S(2)}) collective-permute-start(bf16[3,256,384]{2,1,0:T(8,128)(2,1)S(1)} %get-tuple-element.28.refs_0_), channel_id=1, source_target_pairs={{0,2},{2,4},{4,6},{6,0},{1,3},{3,5},{5,7},{7,1},{8,10},{10,12},{12... | collective-permute-start | bytes 1769480 | tf_op jit(solution)/shard_map/ppermute | solution.py:249
  28.1 3.4 %collective-permute-start.2 = (bf16[3,256,384]{2,1,0:T(8,128)(2,1)S(1)}, bf16[3,256,384]{2,1,0:T(8,128)(2,1)S(1)}, u32[]{:S(2)}, u32[]{:S(2)}) collective-permute-start(bf16[3,256,384]{2,1,0:T(8,128)(2,1)S(1)} %get-tuple-element.29.refs_1_), channel_id=1, source_target_pairs={{0,6},{2,0},{4,2},{6,4},{1,7},{3,1},{5,3},{7,5},{8,14},{10,8},{12,... | collective-permute-start | bytes 1769480 | tf_op jit(solution)/shard_map/ppermute | solution.py:250
  31.5 3.4 %collective-permute-start.1 = (bf16[3,256,384]{2,1,0:T(8,128)(2,1)S(1)}, bf16[3,256,384]{2,1,0:T(8,128)(2,1)S(1)}, u32[]{:S(2)}, u32[]{:S(2)}) collective-permute-start(bf16[3,256,384]{2,1,0:T(8,128)(2,1)S(1)} %get-tuple-element.28.refs_0_), channel_id=1, source_target_pairs={{0,6},{2,0},{4,2},{6,4},{1,7},{3,1},{5,3},{7,5},{8,14},{10,8},{12,... | collective-permute-start | bytes 1769480 | tf_op jit(solution)/shard_map/ppermute | solution.py:252
  34.9 1.9 %collective-permute-start.6 = (bf16[3,256,384]{2,1,0:T(8,128)(2,1)S(1)}, bf16[3,256,384]{2,1,0:T(8,128)(2,1)S(1)}, u32[]{:S(2)}, u32[]{:S(2)}) collective-permute-start(bf16[3,256,384]{2,1,0:T(8,128)(2,1)S(1)} %get-tuple-element.29.refs_1_), channel_id=1, source_target_pairs={{0,2},{2,4},{4,6},{6,0},{1,3},{3,5},{5,7},{7,1},{8,10},{10,12},{12... | collective-permute-start | bytes 1769480 | tf_op jit(solution)/shard_map/ppermute | solution.py:251
  36.8 5.3 %collective-permute-done.3.refs_6_ = bf16[3,256,384]{2,1,0:T(8,128)(2,1)S(1)} collective-permute-done((bf16[3,256,384]{2,1,0:T(8,128)(2,1)S(1)}, bf16[3,256,384]{2,1,0:T(8,128)(2,1)S(1)}, u32[]{:S(2)}, u32[]{:S(2)}) %collective-permute-start.3) | collective-permute-done | bytes 589856 | tf_op jit(solution)/shard_map/ppermute | solution.py:249
  42.1 1.9 %collective-permute-start.4 = (bf16[3,256,384]{2,1,0:T(8,128)(2,1)S(1)}, bf16[3,256,384]{2,1,0:T(8,128)(2,1)S(1)}, u32[]{:S(2)}, u32[]{:S(2)}) collective-permute-start(bf16[3,256,384]{2,1,0:T(8,128)(2,1)S(1)} %collective-permute-done.3.refs_6_), channel_id=1, source_target_pairs={{0,2},{2,4},{4,6},{6,0},{1,3},{3,5},{5,7},{7,1},{8,10},{10,12},{12... | collective-permute-start | bytes 1769480 | tf_op jit(solution)/shard_map/ppermute | solution.py:253
  44.1 0.0 collective-permute-done.2.refs_3_
  44.1 4.6 %collective-permute-start.5 = (bf16[3,256,384]{2,1,0:T(8,128)(2,1)S(1)}, bf16[3,256,384]{2,1,0:T(8,128)(2,1)S(1)}, u32[]{:S(2)}, u32[]{:S(2)}) collective-permute-start(bf16[3,256,384]{2,1,0:T(8,128)(2,1)S(1)} %collective-permute-done.2.refs_3_), channel_id=1, source_target_pairs={{0,6},{2,0},{4,2},{6,4},{1,7},{3,1},{5,3},{7,5},{8,14},{10,8},{12,... | collective-permute-start | bytes 1769480 | tf_op jit(solution)/shard_map/ppermute | solution.py:254
  48.7 7.7 %collective-permute-done.1.refs_2_ = bf16[3,256,384]{2,1,0:T(8,128)(2,1)S(1)} collective-permute-done((bf16[3,256,384]{2,1,0:T(8,128)(2,1)S(1)}, bf16[3,256,384]{2,1,0:T(8,128)(2,1)S(1)}, u32[]{:S(2)}, u32[]{:S(2)}) %collective-permute-start.1) | collective-permute-done | bytes 589856 | tf_op jit(solution)/shard_map/ppermute | solution.py:252
  56.4 0.0 collective-permute-done.6.refs_7_
  56.4 11.1 %collective-permute-done.4.refs_4_ = bf16[3,256,384]{2,1,0:T(8,128)(2,1)S(1)} collective-permute-done((bf16[3,256,384]{2,1,0:T(8,128)(2,1)S(1)}, bf16[3,256,384]{2,1,0:T(8,128)(2,1)S(1)}, u32[]{:S(2)}, u32[]{:S(2)}) %collective-permute-start.4) | collective-permute-done | bytes 589856 | tf_op jit(solution)/shard_map/ppermute | solution.py:253
  67.4 1.6 %collective-permute-done.5.refs_5_ = bf16[3,256,384]{2,1,0:T(8,128)(2,1)S(1)} collective-permute-done((bf16[3,256,384]{2,1,0:T(8,128)(2,1)S(1)}, bf16[3,256,384]{2,1,0:T(8,128)(2,1)S(1)}, u32[]{:S(2)}, u32[]{:S(2)}) %collective-permute-start.5) | collective-permute-done | bytes 589856 | tf_op jit(solution)/shard_map/ppermute | solution.py:254
  69.0 2.2 %assemble.1.own_hbm = bf16[3,2048,384]{2,1,0:T(8,128)(2,1)} custom-call(bf16[3,256,384]{2,1,0:T(8,128)(2,1)S(1)} %get-tuple-element.28.refs_0_, bf16[3,256,384]{2,1,0:T(8,128)(2,1)S(1)} %get-tuple-element.29.refs_1_, bf16[3,256,384]{2,1,0:T(8,128)(2,1)S(1)} %collective-permute-done.1.refs_2_, bf16[3,256,384]{2,1,0:T(8,128)(2,1)S(1)} %collective-permute-done.2.refs_3_, ...), custom_call_target="tpu_custom_call" | custom-call | tf_op jit(solution)/shard_map/assemble/pallas_call | solution.py:274
  71.3 4.0 %collective-permute-start.7 = (bf16[3,2048,384]{2,1,0:T(8,128)(2,1)}, bf16[3,2048,384]{2,1,0:T(8,128)(2,1)}, u32[]{:S(2)}, u32[]{:S(2)}) collective-permute-start(bf16[3,2048,384]{2,1,0:T(8,128)(2,1)} %assemble.1.own_hbm), channel_id=1, source_target_pairs={{0,1},{1,0},{2,3},{3,2},{4,5},{5,4},{6,7},{7,6},{8,9},{9,8},{10,11... | collective-permute-start | bytes 14155784 | tf_op jit(solution)/shard_map/ppermute | solution.py:285
  75.2 8.8 %all-to-all-done = bf16[64,80,128]{2,1,0:T(8,128)(2,1)S(1)} async-done(((bf16[64,80,128]{2,1,0:T(8,128)(2,1)}), bf16[64,80,128]{2,1,0:T(8,128)(2,1)S(1)}, u32[]{:S(2)}, u32[]{:S(2)}) %all-to-all-start) | async-done | bytes 1310752 | tf_op jit(solution)/shard_map/all_to_all | solution.py:174
  84.0 7.5 %collective-permute-start = (bf16[5120,128]{1,0:T(8,128)(2,1)S(1)}, bf16[5120,128]{1,0:T(8,128)(2,1)S(1)}, u32[]{:S(2)}, u32[]{:S(2)}) collective-permute-start(bf16[5120,128]{1,0:T(8,128)(2,1)S(1)} %bitcast.4), channel_id=1, source_target_pairs={{0,1},{1,0},{2,3},{3,2},{4,5},{5,4},{6,7},{7,6},{8,9},{9,8},{10,11... | collective-permute-start | bytes 3932168 | tf_op jit(solution)/shard_map/ppermute | solution.py:286
  91.6 0.0 collective-permute-done.7.oth_hbm
  91.6 3.9 %own.1 = (bf16[320,1024]{1,0:T(8,128)(2,1)S(1)}, f32[3,320,768]{2,1,0:T(8,128)S(1)}, bf16[3,1024,768]{2,1,0:T(8,128)(2,1)S(1)}) custom-call(bf16[5120,128]{1,0:T(8,128)(2,1)S(1)} %bitcast.5, bf16[3,2048,384]{2,1,0:T(8,128)(2,1)} %assemble.1.own_hbm, bf16[3,2048,384]{2,1,0:T(8,128)(2,1)} %collective-permute-done.7.oth_hbm), custom_call_target="tpu_custom_call" | custom-call | tf_op jit(solution)/shard_map/own/pallas_call | solution.py:329
  95.5 0.0 collective-permute-done.recv_ref
  95.5 7.4 %grads.1 = (bf16[320,1024]{1,0:T(8,128)(2,1)S(1)}, bf16[320,768]{1,0:T(8,128)(2,1)S(1)}, bf16[64,21,2,128]{3,2,1,0:T(2,128)(2,1)}) custom-call(bf16[5120,128]{1,0:T(8,128)(2,1)S(1)} %collective-permute-done.recv_ref, bf16[3,2048,384]{2,1,0:T(8,128)(2,1)} %assemble.1.own_hbm, bf16[3,2048,384]{2,1,0:T(8,128)(2,1)} %collective-permute-done.7.oth_hbm, ...), custom_call_target="tpu_custom_call" | custom-call | tf_op jit(solution)/shard_map/grads/pallas_call | solution.py:380
  102.9 0.0 copy-start
  102.9 6.8 %all-to-all-start.1 = ((bf16[64,21,2,128]{3,2,1,0:T(2,128)(2,1)}), bf16[64,21,2,128]{3,2,1,0:T(2,128)(2,1)S(1)}, u32[]{:S(2)}, u32[]{:S(2)}) async-start(bf16[64,21,2,128]{3,2,1,0:T(2,128)(2,1)} %get-tuple-element.32), calls=%async_computation.1 | async-start | bytes 1376256 | tf_op jit(solution)/shard_map/all_to_all | solution.py:174
  109.7 2.3 %weight.1 = (bf16[512,768]{1,0:T(8,128)(2,1)S(1)}, bf16[256,768]{1,0:T(8,128)(2,1)S(1)}, bf16[256,768]{1,0:T(8,128)(2,1)}, bf16[256,768]{1,0:T(8,128)(2,1)S(1)},...) custom-call(bf16[320,1024]{1,0:T(8,128)(2,1)S(1)} %get-tuple-element.37.own_ref, ...), custom_call_target="tpu_custom_call" | custom-call | tf_op jit(solution)/shard_map/weight/pallas_call | solution.py:415
  112.0 4.6 %collective-permute-start.10 = (bf16[256,768]{1,0:T(8,128)(2,1)S(1)}, bf16[256,768]{1,0:T(8,128)(2,1)S(1)}, u32[]{:S(2)}, u32[]{:S(2)}) collective-permute-start(bf16[256,768]{1,0:T(8,128)(2,1)S(1)} %get-tuple-element.44), channel_id=1, source_target_pairs={{0,6},{2,0},{4,2},{6,4},{1,7},{3,1},{5,3},{7,5},{8,14},{10,8},{12,... | collective-permute-start | bytes 1179656 | tf_op jit(solution)/shard_map/ppermute | solution.py:427
  116.6 1.9 %collective-permute-start.9 = (bf16[256,768]{1,0:T(8,128)(2,1)S(1)}, bf16[256,768]{1,0:T(8,128)(2,1)S(1)}, u32[]{:S(2)}, u32[]{:S(2)}) collective-permute-start(bf16[256,768]{1,0:T(8,128)(2,1)S(1)} %get-tuple-element.42), channel_id=1, source_target_pairs={{0,2},{2,4},{4,6},{6,0},{1,3},{3,5},{5,7},{7,1},{8,10},{10,12},{12... | collective-permute-start | bytes 1179656 | tf_op jit(solution)/shard_map/ppermute | solution.py:426
  118.6 4.6 %collective-permute-start.12 = (bf16[256,768]{1,0:T(8,128)(2,1)}, bf16[256,768]{1,0:T(8,128)(2,1)S(1)}, u32[]{:S(2)}, u32[]{:S(2)}) collective-permute-start(bf16[256,768]{1,0:T(8,128)(2,1)} %get-tuple-element.46), channel_id=1, source_target_pairs={{0,6},{2,0},{4,2},{6,4},{1,7},{3,1},{5,3},{7,5},{8,14},{10,8},{12,... | collective-permute-start | bytes 1179656 | tf_op jit(solution)/shard_map/ppermute | solution.py:429
  123.1 1.9 %collective-permute-start.13 = (bf16[256,768]{1,0:T(8,128)(2,1)}, bf16[256,768]{1,0:T(8,128)(2,1)S(1)}, u32[]{:S(2)}, u32[]{:S(2)}) collective-permute-start(bf16[256,768]{1,0:T(8,128)(2,1)} %get-tuple-element.47), channel_id=1, source_target_pairs={{0,2},{2,4},{4,6},{6,0},{1,3},{3,5},{5,7},{7,1},{8,10},{10,12},{12... | collective-permute-start | bytes 1179656 | tf_op jit(solution)/shard_map/ppermute | solution.py:428
  125.1 0.0 collective-permute-done.10.d_ref
  125.1 4.8 %collective-permute-done.9.b_ref = bf16[256,768]{1,0:T(8,128)(2,1)S(1)} collective-permute-done((bf16[256,768]{1,0:T(8,128)(2,1)S(1)}, bf16[256,768]{1,0:T(8,128)(2,1)S(1)}, u32[]{:S(2)}, u32[]{:S(2)}) %collective-permute-start.9) | collective-permute-done | bytes 393248 | tf_op jit(solution)/shard_map/ppermute | solution.py:426
  129.8 1.0 add.1
  130.8 1.9 %collective-permute-start.11 = (bf16[256,768]{1,0:T(8,128)(2,1)}, bf16[256,768]{1,0:T(8,128)(2,1)S(1)}, u32[]{:S(2)}, u32[]{:S(2)}) collective-permute-start(bf16[256,768]{1,0:T(8,128)(2,1)} %get-tuple-element.45), channel_id=1, source_target_pairs={{0,2},{2,4},{4,6},{6,0},{1,3},{3,5},{5,7},{7,1},{8,10},{10,12},{12... | collective-permute-start | bytes 1179656 | tf_op jit(solution)/shard_map/ppermute | solution.py:444
  132.8 4.6 %collective-permute-start.14 = (bf16[256,768]{1,0:T(8,128)(2,1)}, bf16[256,768]{1,0:T(8,128)(2,1)S(1)}, u32[]{:S(2)}, u32[]{:S(2)}) collective-permute-start(bf16[256,768]{1,0:T(8,128)(2,1)} %get-tuple-element.48), channel_id=1, source_target_pairs={{0,6},{2,0},{4,2},{6,4},{1,7},{3,1},{5,3},{7,5},{8,14},{10,8},{12,... | collective-permute-start | bytes 1179656 | tf_op jit(solution)/shard_map/ppermute | solution.py:445
  137.3 0.0 copy-done
  137.3 1.1 aux.1
  138.5 7.7 %all-to-all-done.1.back_ref = bf16[64,21,2,128]{3,2,1,0:T(2,128)(2,1)S(1)} async-done(((bf16[64,21,2,128]{3,2,1,0:T(2,128)(2,1)}), bf16[64,21,2,128]{3,2,1,0:T(2,128)(2,1)S(1)}, u32[]{:S(2)}, u32[]{:S(2)}) %all-to-all-start.1) | async-done | bytes 688160 | tf_op jit(solution)/shard_map/all_to_all | solution.py:174
  146.2 1.7 %combine.1.own_ref = bf16[128,1024]{1,0:T(8,128)(2,1)S(1)} custom-call(bf16[64,21,2,128]{3,2,1,0:T(2,128)(2,1)S(1)} %all-to-all-done.1.back_ref, bf16[256,384]{1,0:T(8,128)(2,1)} %get-tuple-element.34.hot_hbm, f32[128,1024]{1,0:T(8,128)} %get-tuple-element.35.delta_hbm, f32[128,128]{1,0:T(8,128)} %get-tuple-element.36.mix_hbm), custom_call_target="tpu_custom_call" | custom-call | tf_op jit(solution)/shard_map/combine/pallas_call | solution.py:494
  147.8 4.9 %collective-permute-start.8 = (bf16[128,1024]{1,0:T(8,128)(2,1)S(1)}, bf16[128,1024]{1,0:T(8,128)(2,1)S(1)}, u32[]{:S(2)}, u32[]{:S(2)}) collective-permute-start(bf16[128,1024]{1,0:T(8,128)(2,1)S(1)} %combine.1.own_ref), channel_id=1, source_target_pairs={{0,1},{1,0},{2,3},{3,2},{4,5},{5,4},{6,7},{7,6},{8,9},{9,8},{10,11... | collective-permute-start | bytes 786440 | tf_op jit(solution)/shard_map/ppermute | solution.py:511
  152.7 0.0 collective-permute-done.12.b_ref
  152.8 0.0 collective-permute-done.13.c_ref
  152.8 0.0 collective-permute-done.11.a_ref
  152.8 0.0 collective-permute-done.14.d_ref
  152.8 1.1 total.1
  153.9 0.0 collective-permute-done.8.oth_ref
  153.9 0.8 join.1
Async XLA Ops:
  4.4 79.6 %all-to-all-start = ((bf16[64,80,128]{2,1,0:T(8,128)(2,1)}), bf16[64,80,128]{2,1,0:T(8,128)(2,1)S(1)}, u32[]{:S(2)}, u32[]{:S(2)}) async-start(bf16[64,80,128]{2,1,0:T(8,128)(2,1)} %get-tuple-element.27), calls=%async_computation | async-start | bytes 2621440 | tf_op jit(solution)/shard_map/all_to_all | solution.py:174
  24.9 17.2 %collective-permute-start.3 = (bf16[3,256,384]{2,1,0:T(8,128)(2,1)S(1)}, bf16[3,256,384]{2,1,0:T(8,128)(2,1)S(1)}, u32[]{:S(2)}, u32[]{:S(2)}) collective-permute-start(bf16[3,256,384]{2,1,0:T(8,128)(2,1)S(1)} %get-tuple-element.28.refs_0_), channel_id=1, source_target_pairs={{0,2},{2,4},{4,6},{6,0},{1,3},{3,5},{5,7},{7,1},{8,10},{10,12},{12... | collective-permute-start | bytes 1769480 | tf_op jit(solution)/shard_map/ppermute | solution.py:249
  28.1 15.9 %collective-permute-start.2 = (bf16[3,256,384]{2,1,0:T(8,128)(2,1)S(1)}, bf16[3,256,384]{2,1,0:T(8,128)(2,1)S(1)}, u32[]{:S(2)}, u32[]{:S(2)}) collective-permute-start(bf16[3,256,384]{2,1,0:T(8,128)(2,1)S(1)} %get-tuple-element.29.refs_1_), channel_id=1, source_target_pairs={{0,6},{2,0},{4,2},{6,4},{1,7},{3,1},{5,3},{7,5},{8,14},{10,8},{12,... | collective-permute-start | bytes 1769480 | tf_op jit(solution)/shard_map/ppermute | solution.py:250
  31.5 24.8 %collective-permute-start.1 = (bf16[3,256,384]{2,1,0:T(8,128)(2,1)S(1)}, bf16[3,256,384]{2,1,0:T(8,128)(2,1)S(1)}, u32[]{:S(2)}, u32[]{:S(2)}) collective-permute-start(bf16[3,256,384]{2,1,0:T(8,128)(2,1)S(1)} %get-tuple-element.28.refs_0_), channel_id=1, source_target_pairs={{0,6},{2,0},{4,2},{6,4},{1,7},{3,1},{5,3},{7,5},{8,14},{10,8},{12,... | collective-permute-start | bytes 1769480 | tf_op jit(solution)/shard_map/ppermute | solution.py:252
  34.9 21.5 %collective-permute-start.6 = (bf16[3,256,384]{2,1,0:T(8,128)(2,1)S(1)}, bf16[3,256,384]{2,1,0:T(8,128)(2,1)S(1)}, u32[]{:S(2)}, u32[]{:S(2)}) collective-permute-start(bf16[3,256,384]{2,1,0:T(8,128)(2,1)S(1)} %get-tuple-element.29.refs_1_), channel_id=1, source_target_pairs={{0,2},{2,4},{4,6},{6,0},{1,3},{3,5},{5,7},{7,1},{8,10},{10,12},{12... | collective-permute-start | bytes 1769480 | tf_op jit(solution)/shard_map/ppermute | solution.py:251
  42.1 25.3 %collective-permute-start.4 = (bf16[3,256,384]{2,1,0:T(8,128)(2,1)S(1)}, bf16[3,256,384]{2,1,0:T(8,128)(2,1)S(1)}, u32[]{:S(2)}, u32[]{:S(2)}) collective-permute-start(bf16[3,256,384]{2,1,0:T(8,128)(2,1)S(1)} %collective-permute-done.3.refs_6_), channel_id=1, source_target_pairs={{0,2},{2,4},{4,6},{6,0},{1,3},{3,5},{5,7},{7,1},{8,10},{10,12},{12... | collective-permute-start | bytes 1769480 | tf_op jit(solution)/shard_map/ppermute | solution.py:253
  44.1 24.9 %collective-permute-start.5 = (bf16[3,256,384]{2,1,0:T(8,128)(2,1)S(1)}, bf16[3,256,384]{2,1,0:T(8,128)(2,1)S(1)}, u32[]{:S(2)}, u32[]{:S(2)}) collective-permute-start(bf16[3,256,384]{2,1,0:T(8,128)(2,1)S(1)} %collective-permute-done.2.refs_3_), channel_id=1, source_target_pairs={{0,6},{2,0},{4,2},{6,4},{1,7},{3,1},{5,3},{7,5},{8,14},{10,8},{12,... | collective-permute-start | bytes 1769480 | tf_op jit(solution)/shard_map/ppermute | solution.py:254
  71.3 20.3 %collective-permute-start.7 = (bf16[3,2048,384]{2,1,0:T(8,128)(2,1)}, bf16[3,2048,384]{2,1,0:T(8,128)(2,1)}, u32[]{:S(2)}, u32[]{:S(2)}) collective-permute-start(bf16[3,2048,384]{2,1,0:T(8,128)(2,1)} %assemble.1.own_hbm), channel_id=1, source_target_pairs={{0,1},{1,0},{2,3},{3,2},{4,5},{5,4},{6,7},{7,6},{8,9},{9,8},{10,11... | collective-permute-start | bytes 14155784 | tf_op jit(solution)/shard_map/ppermute | solution.py:285
  84.0 11.5 %collective-permute-start = (bf16[5120,128]{1,0:T(8,128)(2,1)S(1)}, bf16[5120,128]{1,0:T(8,128)(2,1)S(1)}, u32[]{:S(2)}, u32[]{:S(2)}) collective-permute-start(bf16[5120,128]{1,0:T(8,128)(2,1)S(1)} %bitcast.4), channel_id=1, source_target_pairs={{0,1},{1,0},{2,3},{3,2},{4,5},{5,4},{6,7},{7,6},{8,9},{9,8},{10,11... | collective-permute-start | bytes 3932168 | tf_op jit(solution)/shard_map/ppermute | solution.py:286
  102.9 34.5 %copy-start = (bf16[2048,64]{0,1:T(8,128)(2,1)S(1)}, bf16[2048,64]{0,1:T(8,128)(2,1)}, u32[]{:S(2)}) copy-start(bf16[2048,64]{0,1:T(8,128)(2,1)} %param.12) | copy-start | bytes 786436
  102.9 43.3 %all-to-all-start.1 = ((bf16[64,21,2,128]{3,2,1,0:T(2,128)(2,1)}), bf16[64,21,2,128]{3,2,1,0:T(2,128)(2,1)S(1)}, u32[]{:S(2)}, u32[]{:S(2)}) async-start(bf16[64,21,2,128]{3,2,1,0:T(2,128)(2,1)} %get-tuple-element.32), calls=%async_computation.1 | async-start | bytes 1376256 | tf_op jit(solution)/shard_map/all_to_all | solution.py:174
  112.0 13.1 %collective-permute-start.10 = (bf16[256,768]{1,0:T(8,128)(2,1)S(1)}, bf16[256,768]{1,0:T(8,128)(2,1)S(1)}, u32[]{:S(2)}, u32[]{:S(2)}) collective-permute-start(bf16[256,768]{1,0:T(8,128)(2,1)S(1)} %get-tuple-element.44), channel_id=1, source_target_pairs={{0,6},{2,0},{4,2},{6,4},{1,7},{3,1},{5,3},{7,5},{8,14},{10,8},{12,... | collective-permute-start | bytes 1179656 | tf_op jit(solution)/shard_map/ppermute | solution.py:427
  116.6 13.2 %collective-permute-start.9 = (bf16[256,768]{1,0:T(8,128)(2,1)S(1)}, bf16[256,768]{1,0:T(8,128)(2,1)S(1)}, u32[]{:S(2)}, u32[]{:S(2)}) collective-permute-start(bf16[256,768]{1,0:T(8,128)(2,1)S(1)} %get-tuple-element.42), channel_id=1, source_target_pairs={{0,2},{2,4},{4,6},{6,0},{1,3},{3,5},{5,7},{7,1},{8,10},{10,12},{12... | collective-permute-start | bytes 1179656 | tf_op jit(solution)/shard_map/ppermute | solution.py:426
  118.6 34.2 %collective-permute-start.12 = (bf16[256,768]{1,0:T(8,128)(2,1)}, bf16[256,768]{1,0:T(8,128)(2,1)S(1)}, u32[]{:S(2)}, u32[]{:S(2)}) collective-permute-start(bf16[256,768]{1,0:T(8,128)(2,1)} %get-tuple-element.46), channel_id=1, source_target_pairs={{0,6},{2,0},{4,2},{6,4},{1,7},{3,1},{5,3},{7,5},{8,14},{10,8},{12,... | collective-permute-start | bytes 1179656 | tf_op jit(solution)/shard_map/ppermute | solution.py:429
  123.1 29.6 %collective-permute-start.13 = (bf16[256,768]{1,0:T(8,128)(2,1)}, bf16[256,768]{1,0:T(8,128)(2,1)S(1)}, u32[]{:S(2)}, u32[]{:S(2)}) collective-permute-start(bf16[256,768]{1,0:T(8,128)(2,1)} %get-tuple-element.47), channel_id=1, source_target_pairs={{0,2},{2,4},{4,6},{6,0},{1,3},{3,5},{5,7},{7,1},{8,10},{10,12},{12... | collective-permute-start | bytes 1179656 | tf_op jit(solution)/shard_map/ppermute | solution.py:428
  130.8 21.9 %collective-permute-start.11 = (bf16[256,768]{1,0:T(8,128)(2,1)}, bf16[256,768]{1,0:T(8,128)(2,1)S(1)}, u32[]{:S(2)}, u32[]{:S(2)}) collective-permute-start(bf16[256,768]{1,0:T(8,128)(2,1)} %get-tuple-element.45), channel_id=1, source_target_pairs={{0,2},{2,4},{4,6},{6,0},{1,3},{3,5},{5,7},{7,1},{8,10},{10,12},{12... | collective-permute-start | bytes 1179656 | tf_op jit(solution)/shard_map/ppermute | solution.py:444
  132.8 20.0 %collective-permute-start.14 = (bf16[256,768]{1,0:T(8,128)(2,1)}, bf16[256,768]{1,0:T(8,128)(2,1)S(1)}, u32[]{:S(2)}, u32[]{:S(2)}) collective-permute-start(bf16[256,768]{1,0:T(8,128)(2,1)} %get-tuple-element.48), channel_id=1, source_target_pairs={{0,6},{2,0},{4,2},{6,4},{1,7},{3,1},{5,3},{7,5},{8,14},{10,8},{12,... | collective-permute-start | bytes 1179656 | tf_op jit(solution)/shard_map/ppermute | solution.py:445
  147.8 6.0 %collective-permute-start.8 = (bf16[128,1024]{1,0:T(8,128)(2,1)S(1)}, bf16[128,1024]{1,0:T(8,128)(2,1)S(1)}, u32[]{:S(2)}, u32[]{:S(2)}) collective-permute-start(bf16[128,1024]{1,0:T(8,128)(2,1)S(1)} %combine.1.own_ref), channel_id=1, source_target_pairs={{0,1},{1,0},{2,3},{3,2},{4,5},{5,4},{6,7},{7,6},{8,9},{9,8},{10,11... | collective-permute-start | bytes 786440 | tf_op jit(solution)/shard_map/ppermute | solution.py:511
